TPU v7x, 1024 devices: a whole 4x8x16 slice. The times are simulated.
1024 devices in a mesh: dp: 64 (over y, x, core), tensor: 16 (over z).
Axes of the slice: x: 4, y: 8, z: 16, core: 2. Of those that a mesh axis runs over, the one named last changes fastest.
Arguments:
- layer_input: bfloat16 [32768, 8192], P('dp', 'tensor'), may hold values from -180 to 180
- gain: bfloat16 [8192], P('tensor'), may hold values from 0.25 to 1.75
- w_kv: bfloat16 [2048, 8192], P(None, 'tensor'), may hold values from -0.125 to 0.125
- d_kv: bfloat16 [32768, 2048], P('dp', 'tensor'), may hold values from -32 to 32
- destination: int32 [32768], P('dp'), may hold values from -1 to 63, as said below
Outputs:
- grad_x: bfloat16 [32768, 8192], P('dp', 'tensor')
- grad_weight: float32 [2048, 8192], P('dp', 'tensor')
Inputs may be any that keep to these rules, and one draw needn't show every extreme that they name: The rows of one device with destination >= 0 are its first rows, 128 of them or more, and some device has no padding. At most 8 rows of one device name the same destination, and some destination is named by exactly 8 rows of every device.
All inputs are finite; a program needn't handle non-finite values.
Results may differ from a plain program's by a relative error of at most 0.0031.
Values may be sent and summed in bfloat16 or wider, within the bound.
No kernel may reach another device: no remote copies, remote signals or barrier semaphores. Data moves between devices by JAX's collectives and lax.ppermute only.
A program may use at most 32 MiB of HBM per device.

v0:
```python
import jax
import jax.numpy as jnp
from jax import lax
from jax.sharding import PartitionSpec as P

D = 8192


EPS = 1e-06


def gather_columns(own_cot):
    return lax.all_gather(own_cot, "tensor", axis=1, tiled=True)


def layer_backward(inputs, cotangent, gain, w_kv):
    values = inputs.astype(jnp.float32)
    gain_wide = gain.astype(jnp.float32)
    dnormed = jnp.dot(cotangent, w_kv, preferred_element_type=jnp.float32)
    squares, products = lax.psum(
        (jnp.sum(values * values, axis=1), jnp.sum(values * gain_wide * dnormed, axis=1)), "tensor"
    )
    inverse = lax.rsqrt(squares / D + EPS)
    mean_dot = products / D
    grad_rows = (
        inverse[:, None] * gain_wide * dnormed - values * (inverse**3 * mean_dot)[:, None]
    ).astype(jnp.bfloat16)
    normed = (values * inverse[:, None] * gain_wide).astype(jnp.bfloat16)
    grad_weight = lax.psum_scatter(
        lax.dot_general(
            cotangent, normed, (((0,), (0,)), ((), ())), preferred_element_type=jnp.float32
        ),
        "dp",
        scatter_dimension=0,
        tiled=True,
    )
    return (grad_rows, grad_weight)


def shards(layer_input, gain, w_kv, d_kv, destination):
    dp_count = lax.axis_size("dp")
    row_count = destination.shape[0]
    peer_rows = row_count // dp_count
    peer_ids = jnp.arange(dp_count, dtype=jnp.int32)
    onehot = (destination[:, None] == peer_ids[None, :]).astype(jnp.int32)
    before = jnp.cumsum(onehot, axis=0) - onehot
    slot_rank = jnp.sum(before * onehot, axis=1)
    is_live = destination >= 0
    position = jnp.where(is_live, destination * peer_rows + slot_rank, row_count)
    fetch_row = jnp.minimum(position, row_count - 1)
    outgoing = jnp.zeros_like(layer_input).at[position].set(layer_input, mode="drop")
    incoming = lax.all_to_all(
        outgoing.reshape(dp_count, peer_rows, layer_input.shape[1]),
        "dp",
        split_axis=0,
        concat_axis=0,
        tiled=True,
    ).reshape(row_count, layer_input.shape[1])
    grad_slots, grad_weight = layer_backward(incoming, gather_columns(d_kv), gain, w_kv)
    returned = lax.all_to_all(
        grad_slots.reshape(dp_count, peer_rows, layer_input.shape[1]),
        "dp",
        split_axis=0,
        concat_axis=0,
        tiled=True,
    ).reshape(row_count, layer_input.shape[1])
    grad_x = jnp.where(is_live[:, None], returned[fetch_row], jnp.zeros((), returned.dtype))
    return (grad_x, grad_weight)


def solution(mesh):
    return jax.shard_map(
        shards,
        mesh=mesh,
        in_specs=(P("dp", "tensor"), P("tensor"), P(None, "tensor"), P("dp", "tensor"), P("dp")),
        out_specs=(P("dp", "tensor"), P("dp", "tensor")),
        check_vma=False,
    )
```

profile of v0, /device:TPU:16, one launch (start us, length us, event | category | flops | bytes accessed | tf_op | source)
XLA Modules:
  0.0 315.3 jit_solution(14128346866186799344)
XLA Ops:
  7.2 0.0 copy-start
  7.2 0.0 copy-start.2
  7.2 0.0 all-gather.2.cloned.1.call-start
  7.2 0.7 all-gather.2.cloned.1.call-update
  7.9 0.7 fusion.19
  8.6 1.2 reduce-window.6
  9.8 0.2 slice_reduce_fusion
  10.1 0.8 fusion.18
  10.9 0.7 compare_select_fusion
  11.6 3.7 %scatter_custom_fusion = bf16[512,512]{1,0:T(8,128)(2,1)} fusion(s32[512]{0:T(512)S(1)} %get-tuple-element.11, bf16[512,512]{1,0:T(8,128)(2,1)} %param.5, bf16[]{:T(256)} %constant.9.clone.1), kind=kCustom, calls=%fused_computation.19 | custom fusion | bytes 524800 | tf_op jit(solution)/shard_map/scatter | solution.py:51
  15.3 17.1 %all-to-all-start = ((bf16[64,8,512]{2,1,0:T(8,128)(2,1)}), bf16[64,8,512]{2,1,0:T(8,128)(2,1)S(1)}, u32[]{:S(2)}, u32[]{:S(2)}) async-start(bf16[64,8,512]{2,1,0:T(8,128)(2,1)} %bitcast.2), calls=%async_computation | async-start | bytes 1048576 | tf_op jit(solution)/shard_map/all_to_all | solution.py:52
  32.4 0.0 reduce-scatter.4.cloned.1.call-start
  32.4 0.0 copy-done.2
  32.5 17.9 %all-to-all-done = bf16[64,8,512]{2,1,0:T(8,128)(2,1)S(1)} async-done(((bf16[64,8,512]{2,1,0:T(8,128)(2,1)}), bf16[64,8,512]{2,1,0:T(8,128)(2,1)S(1)}, u32[]{:S(2)}, u32[]{:S(2)}) %all-to-all-start) | async-done | bytes 524320 | tf_op jit(solution)/shard_map/all_to_all | solution.py:52
  50.3 0.2 fusion.9
  50.5 0.1 reduce_sum.31
  50.6 49.9 %all-gather.2.cloned.1.call-done = bf16[512,2048]{1,0:T(8,128)(2,1)} async-done(((bf16[512,128]{1,0:T(8,128)(2,1)}), bf16[512,2048]{1,0:T(8,128)(2,1)}) %all-gather.2.cloned.1.call-update) | async-done | bytes 2097168 | tf_op jit(solution)/shard_map/all_gather | solution.py:13
  100.5 0.0 copy-done
  100.5 3.9 %fusion.4 = (f32[512]{0:T(512)S(1)}, f32[512,512]{1,0:T(8,128)}) fusion(bf16[64,8,512]{2,1,0:T(8,128)(2,1)S(1)} %all-to-all-done, f32[512]{0:T(512)S(1)} %convert_element_type.28, bf16[512,2048]{1,0:T(8,128)(2,1)} %all-gather.2.cloned.1.call-done, bf16[2048,512]{1,0:T(8,128)(2,1)S(1)} %copy-done), kind=kOutput, calls=%fused_computation.9 | convolution fusion | flops 1074789888 | bytes 5771264 | tf_op jit(solution)/shard_map/dot_general | solution.py:19
  104.4 29.7 %all-reduce = (f32[512]{0:T(512)S(1)}, f32[512]{0:T(512)S(1)}) all-reduce(f32[512]{0:T(512)S(1)} %get-tuple-element.14, f32[512]{0:T(512)S(1)} %reduce_sum.31), channel_id=1, replica_groups=mesh['dp'=64,'tensor'=16] {'tensor'}, use_global_device_ids=true, to_apply=%region_7.8 | all-reduce | flops 1024 | bytes 8192 | tf_op jit(solution)/shard_map/psum | solution.py:20
  134.2 4.9 %convolution_bitcast_fusion = f32[2048,512]{0,1:T(8,128)} fusion(bf16[512,2048]{1,0:T(8,128)(2,1)} %all-gather.2.cloned.1.call-done, bf16[64,8,512]{2,1,0:T(8,128)(2,1)S(1)} %all-to-all-done, f32[512]{0:T(512)S(1)} %convert_element_type.28, f32[512]{0:T(512)S(1)} %get-tuple-element.12), kind=kOutput, calls=%fused_computation.2 | convolution fusion | flops 1074790400 | bytes 6819840 | tf_op jit(solution)/shard_map/dot_general | solution.py:30
  139.1 5.3 %copy.12 = f32[2048,512]{1,0:T(8,128)} copy(f32[2048,512]{0,1:T(8,128)} %convolution_bitcast_fusion) | data formatting | bytes 8388608
  144.5 0.0 reduce-scatter.4.cloned.1.call-update
  144.5 0.0 copy-start.1
  144.5 2.3 fusion.11
  146.8 10.2 %all-to-all-start.1 = ((bf16[64,8,512]{2,1,0:T(8,128)(2,1)}), bf16[64,8,512]{2,1,0:T(8,128)(2,1)S(1)}, u32[]{:S(2)}, u32[]{:S(2)}) async-start(bf16[64,8,512]{2,1,0:T(8,128)(2,1)} %fusion.11), calls=%async_computation.1 | async-start | bytes 1048576 | tf_op jit(solution)/shard_map/all_to_all | solution.py:60
  157.0 0.0 copy-done.1
  157.0 17.8 %all-to-all-done.1 = bf16[64,8,512]{2,1,0:T(8,128)(2,1)S(1)} async-done(((bf16[64,8,512]{2,1,0:T(8,128)(2,1)}), bf16[64,8,512]{2,1,0:T(8,128)(2,1)S(1)}, u32[]{:S(2)}, u32[]{:S(2)}) %all-to-all-start.1) | async-done | bytes 524320 | tf_op jit(solution)/shard_map/all_to_all | solution.py:60
  174.8 2.0 gather_fusion
  176.8 0.9 broadcast_select_fusion
  177.7 130.7 %reduce-scatter.4.cloned.1.call-done = f32[32,512]{1,0:T(8,128)} async-done(((f32[2048,512]{1,0:T(8,128)}), f32[32,512]{1,0:T(8,128)}) %reduce-scatter.4.cloned.1.call-update) | async-done | bytes 65552
  (6 shorter events, 0.1 us)
Async XLA Ops:
  7.2 93.4 %copy-start = (bf16[2048,512]{1,0:T(8,128)(2,1)S(1)}, bf16[2048,512]{1,0:T(8,128)(2,1)}, u32[]{:S(2)}) copy-start(bf16[2048,512]{1,0:T(8,128)(2,1)} %param.7) | copy-start | bytes 6291460
  7.2 25.3 %copy-start.2 = (bf16[512]{0:T(512)(128)(2,1)S(1)}, bf16[512]{0:T(512)(128)(2,1)}, u32[]{:S(2)}) copy-start(bf16[512]{0:T(512)(128)(2,1)} %param.6) | copy-start | bytes 3076
  7.2 93.3 %all-gather.2.cloned.1.call-start = ((), (), s32[]{:S(2)}) async-start(), calls=%async_computation.3 | async-start | bytes 2228224 | tf_op jit(solution)/shard_map/all_gather | solution.py:13
  15.3 35.1 %all-to-all-start = ((bf16[64,8,512]{2,1,0:T(8,128)(2,1)}), bf16[64,8,512]{2,1,0:T(8,128)(2,1)S(1)}, u32[]{:S(2)}, u32[]{:S(2)}) async-start(bf16[64,8,512]{2,1,0:T(8,128)(2,1)} %bitcast.2), calls=%async_computation | async-start | bytes 1048576 | tf_op jit(solution)/shard_map/all_to_all | solution.py:52
  32.4 276.0 %reduce-scatter.4.cloned.1.call-start = ((), (), s32[]{:S(2)}) async-start(), calls=%async_computation.4 | async-start | bytes 4259840
  144.5 12.5 %copy-start.1 = (s32[512]{0:T(512)S(1)}, s32[512]{0:T(512)}, u32[]{:S(2)}) copy-start(s32[512]{0:T(512)} %param.9) | copy-start | bytes 6148
  146.8 28.0 %all-to-all-start.1 = ((bf16[64,8,512]{2,1,0:T(8,128)(2,1)}), bf16[64,8,512]{2,1,0:T(8,128)(2,1)S(1)}, u32[]{:S(2)}, u32[]{:S(2)}) async-start(bf16[64,8,512]{2,1,0:T(8,128)(2,1)} %fusion.11), calls=%async_computation.1 | async-start | bytes 1048576 | tf_op jit(solution)/shard_map/all_to_all | solution.py:60
Sparse Core Ops, SparseCore 0:
  10.6 89.9 all-gather.1
  144.6 163.7 reduce-scatter.3
where the time goes:
time: 316 us; the launch traced here: 315 us
  waiting for transfers between devices  217 us (69%)
  blocking collectives  29.7 us (9%)
  starting transfers between devices  27.4 us (9%)
  between operations  14.1 us (4%)
  local copies, waits for them, and re-layouts  11.3 us (4%)
  matrix products  8.81 us (3%)
  other arithmetic  6.85 us (2%)
    unnamed x3, waiting for transfers between devices  131 us
    all_gather x1, waiting for transfers between devices, gather_columns(): return lax.all_gather(own_cot, 'tensor', axis=1, tiled=True)  49.9 us
    psum x1, blocking collectives, layer_backward(): lax.psum((jnp.sum(values * values, axis=1), jnp.sum(values * gain_wide *...  29.7 us
    all_to_all x1, waiting for transfers between devices, shards(): lax.all_to_all(outgoing.reshape(dp_count, peer_rows, layer_input.shape[1]...  17.9 us
    all_to_all x1, waiting for transfers between devices, shards(): lax.all_to_all(grad_slots.reshape(dp_count, peer_rows, layer_input.shape[...  17.8 us
    all_to_all x1, starting transfers between devices, shards(): lax.all_to_all(outgoing.reshape(dp_count, peer_rows, layer_input.shape[1]...  17.1 us
    all_to_all x1, starting transfers between devices, shards(): lax.all_to_all(grad_slots.reshape(dp_count, peer_rows, layer_input.shape[...  10.2 us
  transfers between devices with their start and end apart: 4, of which 4 were waited for; matrix products, arithmetic and copies ran while one was open for 4% of the time, Pallas kernels for 0%

commit v1 on v0

v1 whole, which is shorter than its diff:
```python
import jax
import jax.numpy as jnp
from jax import lax
from jax.experimental import pallas as pl
from jax.experimental.pallas import tpu as pltpu
from jax.sharding import Mesh, PartitionSpec as P

D = 8192
EPS = 1e-06
ROWS = 512
FEAT = 512
COLS = 128
TP = 16
CHIPS = 32
PAD = 16
BLOCK = COLS + PAD


def place_kernel(received, onehot, stats, out):
    picked = lax.dot_general(
        received[...], onehot[...], (((0,), (0,)), ((), ())), preferred_element_type=jnp.float32
    )
    out[:COLS, :] = picked.astype(jnp.bfloat16)
    out[COLS:, :] = stats[...]


def place(received, onehot, stats):
    return pl.pallas_call(
        place_kernel,
        out_shape=jax.ShapeDtypeStruct((BLOCK, ROWS), jnp.bfloat16),
        name="place",
    )(received, onehot, stats)


def core_kernel(position, *refs):
    blocks = refs[:TP]
    w, x, gain, keep, send, dnormed, inverse, products = refs[TP:]
    me, core = position[0], position[1]
    total = jnp.zeros((1, ROWS), jnp.float32)
    for block in blocks:
        rows = block[COLS:, :].astype(jnp.float32)
        total = total + (rows[0:1] + rows[1:2] + rows[2:3])
    inv = lax.rsqrt(total / D + EPS)
    inverse[...] = inv
    column = jnp.broadcast_to(inv, (COLS, ROWS)).T
    values = x[...].astype(jnp.float32)
    gain_wide = gain[...].astype(jnp.float32)
    normed = (values * jnp.concatenate([column] * (FEAT // COLS), axis=1) * gain_wide).astype(jnp.bfloat16)
    first = core == 0
    grad = jnp.zeros((ROWS, FEAT), jnp.float32)
    for step, block in enumerate(blocks):
        owner = lax.rem(me + step, TP)
        cot = block[:COLS, :]
        rows = w[pl.ds(pl.multiple_of(owner * COLS, COLS), COLS), :]
        grad = grad + lax.dot_general(
            cot, rows, (((0,), (0,)), ((), ())), preferred_element_type=jnp.float32
        )
        term = jnp.dot(cot, normed, preferred_element_type=jnp.float32)
        at = pl.multiple_of(owner * (COLS // 2), COLS // 2)
        for half in range(2):
            low = term[64 * half : 64 * half + 32]
            high = term[64 * half + 32 : 64 * half + 64]
            keep[pl.ds(at + 32 * half, 32), :] = jnp.where(first, low, high)
            send[pl.ds(at + 32 * half, 32), :] = jnp.where(first, high, low).astype(jnp.bfloat16)
    dnormed[...] = grad
    part = values * gain_wide * grad
    lanes = part[:, :COLS]
    for i in range(1, FEAT // COLS):
        lanes = lanes + part[:, COLS * i : COLS * (i + 1)]
    products[...] = jnp.sum(lanes.T, axis=0, keepdims=True)


def core_step(position, blocks, w_kv, x, gain):
    half = 2 * D // 16
    return pl.pallas_call(
        core_kernel,
        in_specs=[pl.BlockSpec(memory_space=pltpu.SMEM)] + [pl.BlockSpec(memory_space=pltpu.VMEM)] * (TP + 3),
        out_specs=[pl.BlockSpec(memory_space=pltpu.VMEM)] * 5,
        out_shape=[
            jax.ShapeDtypeStruct((half, FEAT), jnp.float32),
            jax.ShapeDtypeStruct((half, FEAT), jnp.bfloat16),
            jax.ShapeDtypeStruct((ROWS, FEAT), jnp.float32),
            jax.ShapeDtypeStruct((1, ROWS), jnp.float32),
            jax.ShapeDtypeStruct((1, ROWS), jnp.float32),
        ],
        compiler_params=pltpu.CompilerParams(vmem_limit_bytes=40 * 1024 * 1024),
        name="core_step",
    )(position, *blocks, w_kv, x, gain)


def shards(layer_input, gain, w_kv, d_kv, destination):
    me = lax.axis_index("tensor")
    core = lax.axis_index("core")
    right = [(i, (i + 1) % TP) for i in range(TP)]
    left = [(i, (i - 1) % TP) for i in range(TP)]

    received = lax.all_to_all(d_kv, ("chip", "core"), split_axis=0, concat_axis=0, tiled=True)

    ids = jnp.arange(ROWS, dtype=jnp.int32)
    same = (destination[:, None] == destination[None, :]) & (ids[:, None] < ids[None, :])
    slot_rank = jnp.sum(same.astype(jnp.int32), axis=0)
    is_live = destination >= 0
    position = jnp.where(is_live, destination * 8 + slot_rank, -1)
    onehot = (ids[:, None] == position[None, :]).astype(jnp.bfloat16)

    values = layer_input.astype(jnp.float32)
    squares = jnp.sum(values * values, axis=1)
    top = lax.reduce_precision(squares, 8, 7)
    rest = squares - top
    middle = lax.reduce_precision(rest, 8, 7)
    stats = jnp.stack([top, middle, rest - middle]).astype(jnp.bfloat16)
    stats = jnp.concatenate([stats, jnp.zeros((PAD - 3, ROWS), jnp.bfloat16)], axis=0)

    own = place(received, onehot, stats)
    blocks = [None] * TP
    blocks[0] = ahead = behind = own
    for step in range(1, TP // 2 + 1):
        behind = lax.ppermute(behind, "tensor", right)
        blocks[TP - step] = behind
        if step < TP // 2:
            ahead = lax.ppermute(ahead, "tensor", left)
            blocks[step] = ahead

    where = jnp.stack([me, core]).astype(jnp.int32)
    keep, send, dnormed, inverse, products = core_step(where, blocks, w_kv, layer_input, gain[None, :])

    taken = lax.ppermute(send, "core", [(0, 1), (1, 0)])
    pair = (keep + taken.astype(jnp.float32)).astype(jnp.bfloat16)
    parts = lax.all_to_all(pair, "chip", split_axis=0, concat_axis=0, tiled=True)
    grad_weight = jnp.sum(parts.reshape(CHIPS, 32, FEAT).astype(jnp.float32), axis=0)

    spread = lax.all_to_all(
        jnp.broadcast_to(products, (TP, ROWS)), "tensor", split_axis=0, concat_axis=0, tiled=True
    )
    mean_dot = jnp.sum(spread, axis=0) / D
    inv = inverse[0]
    gain_wide = gain.astype(jnp.float32)
    grad_x = (inv[:, None] * gain_wide * dnormed - values * (inv**3 * mean_dot)[:, None]).astype(jnp.bfloat16)
    return (grad_x, grad_weight)


def solution(mesh):
    fine = Mesh(mesh.devices.reshape(CHIPS, 2, TP), ("chip", "core", "tensor"))
    dp = ("chip", "core")
    return jax.shard_map(
        shards,
        mesh=fine,
        in_specs=(P(dp, "tensor"), P("tensor"), P(None, "tensor"), P(dp, "tensor"), P(dp)),
        out_specs=(P(dp, "tensor"), P(dp, "tensor")),
        check_vma=False,
    )
```

time: 316 us -> 178 us (0.56)
  waiting for transfers between devices: 217 us -> 51.9 us
  starting transfers between devices: 27.4 us -> 88.6 us
  blocking collectives: 29.7 us -> 0 us
  between operations: 14.1 us -> 0.94 us
  matrix products: 8.81 us -> 0 us
  local copies, waits for them, and re-layouts: 11.3 us -> 18.8 us
  Pallas kernels: 0 us -> 7.1 us
    unnamed x3 -> x0, waiting for transfers between devices: 131 us -> none
    ppermute x0 -> x16, starting transfers between devices: none -> 59.5 us  [the longest x7 42.3 us: shards(): ahead = lax.ppermute(ahead, 'tensor', left)]
    all_gather x1 -> x0, waiting for transfers between devices: 49.9 us -> none  [gather_columns(): return lax.all_gather(own_cot, 'tensor', axis=1, tiled=True)]
    psum x1 -> x0, blocking collectives: 29.7 us -> none  [layer_backward(): lax.psum((jnp.sum(values * values, axis=1), jnp.sum(values * gain_wide *...]
    unnamed x7 -> x50, local copies, waits for them, and re-layouts: 5.36 us -> 18.2 us
    ppermute x0 -> x16, waiting for transfers between devices: none -> 10.5 us  [the longest x8 10.5 us: shards(): behind = lax.ppermute(behind, 'tensor', right)]
    dot_general x2 -> x0, matrix products: 8.81 us -> none  [the longest x1 4.91 us: layer_backward(): lax.dot_general(cotangent, normed, (((0,), (0,)), ((), ())), preferred_el...]
    pallas_call x0 -> x2, Pallas kernels: none -> 7.1 us  [the longest x1 5.13 us: core_step(): pl.pallas_call(core_kernel, in_specs=[pl.BlockSpec(memory_space=pltpu.SME...]
  transfers between devices with their start and end apart: 4 -> 19, of which waited for: 4 -> 8; matrix products, arithmetic and copies ran while one was open for 4% -> 5% of each run, Pallas kernels for 0% -> 0%
where the time goes in v1:
time: 178 us; the launch traced here: 176 us
  starting transfers between devices  88.6 us (50%)
  waiting for transfers between devices  51.9 us (29%)
  local copies, waits for them, and re-layouts  18.8 us (11%)
  other arithmetic  8.98 us (5%)
  Pallas kernels  7.1 us (4%)
    ppermute x7, starting transfers between devices, shards(): ahead = lax.ppermute(ahead, 'tensor', left)  42.3 us
    all_to_all x1, waiting for transfers between devices, shards(): lax.all_to_all(pair, 'chip', split_axis=0, concat_axis=0, tiled=True)  26.3 us
    unnamed x50, local copies, waits for them, and re-layouts  18.2 us
    all_to_all x1, starting transfers between devices, shards(): lax.all_to_all(d_kv, ('chip', 'core'), split_axis=0, concat_axis=0, tiled...  17.3 us
    ppermute x8, starting transfers between devices, shards(): behind = lax.ppermute(behind, 'tensor', right)  15.3 us
    ppermute x8, waiting for transfers between devices, shards(): behind = lax.ppermute(behind, 'tensor', right)  10.5 us
    all_to_all x1, waiting for transfers between devices, shards(): lax.all_to_all(jnp.broadcast_to(products, (TP, ROWS)), 'tensor', split_ax...  9.92 us
    all_to_all x1, starting transfers between devices, shards(): lax.all_to_all(pair, 'chip', split_axis=0, concat_axis=0, tiled=True)  6.18 us
  transfers between devices with their start and end apart: 19, of which 8 were waited for; matrix products, arithmetic and copies ran while one was open for 5% of the time, Pallas kernels for 0%

profile of v1, /device:TPU:16, one launch (start us, length us, event | category | flops | bytes accessed | tf_op | source)
XLA Modules:
  0.0 176.4 jit_solution(9549434022735322993)
XLA Ops:
  0.6 17.3 %all-to-all-start = ((bf16[64,8,128]{2,1,0:T(8,128)(2,1)}), bf16[64,8,128]{2,1,0:T(8,128)(2,1)S(1)}, u32[]{:S(2)}, u32[]{:S(2)}) async-start(bf16[64,8,128]{2,1,0:T(8,128)(2,1)} %bitcast.13), calls=%async_computation | async-start | bytes 262144 | tf_op jit(solution)/shard_map/all_to_all | solution.py:97
  17.9 1.2 fusion
  19.1 0.9 convert_reduce_fusion.1
  20.1 0.7 add_select_fusion
  20.8 0.6 fusion.9.stats
  21.4 0.9 fusion.3.onehot
  22.3 5.2 %all-to-all-done = bf16[64,8,128]{2,1,0:T(8,128)(2,1)S(1)} async-done(((bf16[64,8,128]{2,1,0:T(8,128)(2,1)}), bf16[64,8,128]{2,1,0:T(8,128)(2,1)S(1)}, u32[]{:S(2)}, u32[]{:S(2)}) %all-to-all-start) | async-done | bytes 131104 | tf_op jit(solution)/shard_map/all_to_all | solution.py:97
  27.5 0.6 copy-done.23
  28.1 2.0 %place.1.refs_0_ = bf16[144,512]{1,0:T(8,128)(2,1)} custom-call(bf16[512,128]{1,0:T(8,128)(2,1)} %bitcast.12, bf16[512,512]{1,0:T(8,128)(2,1)} %fusion.3.onehot, bf16[16,512]{1,0:T(8,128)(2,1)} %fusion.9.stats), custom_call_target="tpu_custom_call" | custom-call | tf_op jit(solution)/shard_map/place/pallas_call | solution.py:28
  30.1 1.9 %collective-permute-start.7 = (bf16[144,512]{1,0:T(8,128)(2,1)}, bf16[144,512]{1,0:T(8,128)(2,1)S(1)}, u32[]{:S(2)}, u32[]{:S(2)}) collective-permute-start(bf16[144,512]{1,0:T(8,128)(2,1)} %place.1.refs_0_), channel_id=1, source_target_pairs={{0,1},{1,2},{2,3},{3,4},{4,5},{5,6},{6,7},{7,8},{8,9},{9,10},{10,1... | collective-permute-start | bytes 442376 | tf_op jit(solution)/shard_map/ppermute | solution.py:118
  32.0 11.5 %collective-permute-start = (bf16[144,512]{1,0:T(8,128)(2,1)}, bf16[144,512]{1,0:T(8,128)(2,1)S(1)}, u32[]{:S(2)}, u32[]{:S(2)}) collective-permute-start(bf16[144,512]{1,0:T(8,128)(2,1)} %place.1.refs_0_), channel_id=1, source_target_pairs={{0,15},{1,0},{2,1},{3,2},{4,3},{5,4},{6,5},{7,6},{8,7},{9,8},{10,9... | collective-permute-start | bytes 442376 | tf_op jit(solution)/shard_map/ppermute | solution.py:121
  43.5 2.0 %collective-permute-done.7.refs_15_ = bf16[144,512]{1,0:T(8,128)(2,1)S(1)} collective-permute-done((bf16[144,512]{1,0:T(8,128)(2,1)}, bf16[144,512]{1,0:T(8,128)(2,1)S(1)}, u32[]{:S(2)}, u32[]{:S(2)}) %collective-permute-start.7) | collective-permute-done | bytes 147488 | tf_op jit(solution)/shard_map/ppermute | solution.py:118
  45.6 1.9 %collective-permute-start.8 = (bf16[144,512]{1,0:T(8,128)(2,1)S(1)}, bf16[144,512]{1,0:T(8,128)(2,1)S(1)}, u32[]{:S(2)}, u32[]{:S(2)}) collective-permute-start(bf16[144,512]{1,0:T(8,128)(2,1)S(1)} %collective-permute-done.7.refs_15_), channel_id=1, source_target_pairs={{0,1},{1,2},{2,3},{3,4},{4,5},{5,6},{6,7},{7,8},{8,9},{9,10},{10,1... | collective-permute-start | bytes 442376 | tf_op jit(solution)/shard_map/ppermute | solution.py:118
  47.5 0.0 collective-permute-done.refs_1_
  47.5 5.1 %collective-permute-start.1 = (bf16[144,512]{1,0:T(8,128)(2,1)S(1)}, bf16[144,512]{1,0:T(8,128)(2,1)S(1)}, u32[]{:S(2)}, u32[]{:S(2)}) collective-permute-start(bf16[144,512]{1,0:T(8,128)(2,1)S(1)} %collective-permute-done.refs_1_), channel_id=1, source_target_pairs={{0,15},{1,0},{2,1},{3,2},{4,3},{5,4},{6,5},{7,6},{8,7},{9,8},{10,9... | collective-permute-start | bytes 442376 | tf_op jit(solution)/shard_map/ppermute | solution.py:121
  52.7 1.2 collective-permute-done.8.refs_14_
  53.8 1.9 %collective-permute-start.9 = (bf16[144,512]{1,0:T(8,128)(2,1)S(1)}, bf16[144,512]{1,0:T(8,128)(2,1)S(1)}, u32[]{:S(2)}, u32[]{:S(2)}) collective-permute-start(bf16[144,512]{1,0:T(8,128)(2,1)S(1)} %collective-permute-done.8.refs_14_), channel_id=1, source_target_pairs={{0,1},{1,2},{2,3},{3,4},{4,5},{5,6},{6,7},{7,8},{8,9},{9,10},{10,1... | collective-permute-start | bytes 442376 | tf_op jit(solution)/shard_map/ppermute | solution.py:118
  55.8 5.1 %collective-permute-start.2 = (bf16[144,512]{1,0:T(8,128)(2,1)S(1)}, bf16[144,512]{1,0:T(8,128)(2,1)S(1)}, u32[]{:S(2)}, u32[]{:S(2)}) collective-permute-start(bf16[144,512]{1,0:T(8,128)(2,1)S(1)} %collective-permute-done.1.refs_2_), channel_id=1, source_target_pairs={{0,15},{1,0},{2,1},{3,2},{4,3},{5,4},{6,5},{7,6},{8,7},{9,8},{10,9... | collective-permute-start | bytes 442376 | tf_op jit(solution)/shard_map/ppermute | solution.py:121
  60.9 1.2 collective-permute-done.9.refs_13_
  62.1 1.9 %collective-permute-start.10 = (bf16[144,512]{1,0:T(8,128)(2,1)S(1)}, bf16[144,512]{1,0:T(8,128)(2,1)S(1)}, u32[]{:S(2)}, u32[]{:S(2)}) collective-permute-start(bf16[144,512]{1,0:T(8,128)(2,1)S(1)} %collective-permute-done.9.refs_13_), channel_id=1, source_target_pairs={{0,1},{1,2},{2,3},{3,4},{4,5},{5,6},{6,7},{7,8},{8,9},{9,10},{10,1... | collective-permute-start | bytes 442376 | tf_op jit(solution)/shard_map/ppermute | solution.py:118
  64.0 5.1 %collective-permute-start.3 = (bf16[144,512]{1,0:T(8,128)(2,1)S(1)}, bf16[144,512]{1,0:T(8,128)(2,1)S(1)}, u32[]{:S(2)}, u32[]{:S(2)}) collective-permute-start(bf16[144,512]{1,0:T(8,128)(2,1)S(1)} %collective-permute-done.2.refs_3_), channel_id=1, source_target_pairs={{0,15},{1,0},{2,1},{3,2},{4,3},{5,4},{6,5},{7,6},{8,7},{9,8},{10,9... | collective-permute-start | bytes 442376 | tf_op jit(solution)/shard_map/ppermute | solution.py:121
  69.1 1.2 collective-permute-done.10.refs_12_
  70.3 1.9 %collective-permute-start.11 = (bf16[144,512]{1,0:T(8,128)(2,1)S(1)}, bf16[144,512]{1,0:T(8,128)(2,1)S(1)}, u32[]{:S(2)}, u32[]{:S(2)}) collective-permute-start(bf16[144,512]{1,0:T(8,128)(2,1)S(1)} %collective-permute-done.10.refs_12_), channel_id=1, source_target_pairs={{0,1},{1,2},{2,3},{3,4},{4,5},{5,6},{6,7},{7,8},{8,9},{9,10},{10,1... | collective-permute-start | bytes 442376 | tf_op jit(solution)/shard_map/ppermute | solution.py:118
  72.2 0.6 copy-done.5
  72.9 0.0 collective-permute-done.3.refs_4_
  72.9 5.1 %collective-permute-start.4 = (bf16[144,512]{1,0:T(8,128)(2,1)S(1)}, bf16[144,512]{1,0:T(8,128)(2,1)S(1)}, u32[]{:S(2)}, u32[]{:S(2)}) collective-permute-start(bf16[144,512]{1,0:T(8,128)(2,1)S(1)} %collective-permute-done.3.refs_4_), channel_id=1, source_target_pairs={{0,15},{1,0},{2,1},{3,2},{4,3},{5,4},{6,5},{7,6},{8,7},{9,8},{10,9... | collective-permute-start | bytes 442376 | tf_op jit(solution)/shard_map/ppermute | solution.py:121
  78.0 0.0 copy-start.7
  78.0 0.7 copy-done.7
  78.7 1.9 %collective-permute-start.12 = (bf16[144,512]{1,0:T(8,128)(2,1)S(1)}, bf16[144,512]{1,0:T(8,128)(2,1)S(1)}, u32[]{:S(2)}, u32[]{:S(2)}) collective-permute-start(bf16[144,512]{1,0:T(8,128)(2,1)S(1)} %collective-permute-done.11.refs_11_), channel_id=1, source_target_pairs={{0,1},{1,2},{2,3},{3,4},{4,5},{5,6},{6,7},{7,8},{8,9},{9,10},{10,1... | collective-permute-start | bytes 442376 | tf_op jit(solution)/shard_map/ppermute | solution.py:118
  80.6 0.7 copy-done.9
  81.3 5.1 %collective-permute-start.5 = (bf16[144,512]{1,0:T(8,128)(2,1)S(1)}, bf16[144,512]{1,0:T(8,128)(2,1)S(1)}, u32[]{:S(2)}, u32[]{:S(2)}) collective-permute-start(bf16[144,512]{1,0:T(8,128)(2,1)S(1)} %collective-permute-done.4.refs_5_), channel_id=1, source_target_pairs={{0,15},{1,0},{2,1},{3,2},{4,3},{5,4},{6,5},{7,6},{8,7},{9,8},{10,9... | collective-permute-start | bytes 442376 | tf_op jit(solution)/shard_map/ppermute | solution.py:121
  86.4 0.6 copy-done.11
  87.0 1.9 %collective-permute-start.13 = (bf16[144,512]{1,0:T(8,128)(2,1)S(1)}, bf16[144,512]{1,0:T(8,128)(2,1)S(1)}, u32[]{:S(2)}, u32[]{:S(2)}) collective-permute-start(bf16[144,512]{1,0:T(8,128)(2,1)S(1)} %collective-permute-done.12.refs_10_), channel_id=1, source_target_pairs={{0,1},{1,2},{2,3},{3,4},{4,5},{5,6},{6,7},{7,8},{8,9},{9,10},{10,1... | collective-permute-start | bytes 442376 | tf_op jit(solution)/shard_map/ppermute | solution.py:118
  89.0 0.6 copy-done.13
  89.6 5.1 %collective-permute-start.6 = (bf16[144,512]{1,0:T(8,128)(2,1)S(1)}, bf16[144,512]{1,0:T(8,128)(2,1)S(1)}, u32[]{:S(2)}, u32[]{:S(2)}) collective-permute-start(bf16[144,512]{1,0:T(8,128)(2,1)S(1)} %collective-permute-done.5.refs_6_), channel_id=1, source_target_pairs={{0,15},{1,0},{2,1},{3,2},{4,3},{5,4},{6,5},{7,6},{8,7},{9,8},{10,9... | collective-permute-start | bytes 442376 | tf_op jit(solution)/shard_map/ppermute | solution.py:121
  94.8 0.7 copy-done.15
  95.4 1.9 %collective-permute-start.14 = (bf16[144,512]{1,0:T(8,128)(2,1)S(1)}, bf16[144,512]{1,0:T(8,128)(2,1)S(1)}, u32[]{:S(2)}, u32[]{:S(2)}) collective-permute-start(bf16[144,512]{1,0:T(8,128)(2,1)S(1)} %collective-permute-done.13.refs_9_), channel_id=1, source_target_pairs={{0,1},{1,2},{2,3},{3,4},{4,5},{5,6},{6,7},{7,8},{8,9},{9,10},{10,1... | collective-permute-start | bytes 442376 | tf_op jit(solution)/shard_map/ppermute | solution.py:118
  97.4 0.6 copy-done.17
  98.0 0.1 pad_add_fusion.position
  98.1 0.7 copy-done.19
  98.7 4.9 %collective-permute-done.14.refs_8_ = bf16[144,512]{1,0:T(8,128)(2,1)S(1)} collective-permute-done((bf16[144,512]{1,0:T(8,128)(2,1)S(1)}, bf16[144,512]{1,0:T(8,128)(2,1)S(1)}, u32[]{:S(2)}, u32[]{:S(2)}) %collective-permute-start.14) | collective-permute-done | bytes 147488 | tf_op jit(solution)/shard_map/ppermute | solution.py:118
  103.7 0.6 copy-done.21
  104.3 1.6 copy-done.1
  105.9 0.9 copy-done.4
  106.8 0.9 copy-done.6
  107.7 0.9 copy-done.8
  108.6 0.9 copy-done.10
  109.5 0.9 copy-done.12
  110.5 0.9 copy-done.14
  111.4 0.9 copy-done.16
  112.3 0.9 copy-done.18
  113.2 0.9 copy-done.20
  114.1 0.9 copy-done.22
  115.0 5.1 %core_step.1 = (f32[1024,512]{1,0:T(8,128)S(1)}, bf16[1024,512]{1,0:T(8,128)(2,1)}, f32[512,512]{1,0:T(8,128)S(1)}, f32[1,512]{1,0:T(1,128)S(1)}, f32[1,512]{1,0:T(1,128)S(1)}) custom-call(s32[2]{0:T(128)S(1)} %pad_add_fusion.position, bf16[144,512]{1,0:T(8,128)(2,1)S(1)} %copy-done.4, bf16[144,512]{1,0:T(8,128)(2,1)S(1)} %collective-permute-done.refs_1_, ...), custom_call_target="tpu_custom_call" | custom-call | tf_op jit(solution)/shard_map/core_step/pallas_call | solution.py:75
  120.1 1.0 copy-done.2
  121.1 1.9 %collective-permute-start.15 = (bf16[1024,512]{1,0:T(8,128)(2,1)}, bf16[1024,512]{1,0:T(8,128)(2,1)}, u32[]{:S(2)}, u32[]{:S(2)}) collective-permute-start(bf16[1024,512]{1,0:T(8,128)(2,1)} %get-tuple-element.11), channel_id=1, source_target_pairs={{0,16},{16,0},{1,17},{17,1},{2,18},{18,2},{3,19},{19,3},{4,20},{20... | collective-permute-start | bytes 3145736 | tf_op jit(solution)/shard_map/ppermute | solution.py:127
  123.0 0.6 broadcast_in_dim.10
  123.7 5.7 %all-to-all-start.1 = ((f32[16,1,512]{2,1,0:T(1,128)}), f32[16,1,512]{2,1,0:T(1,128)S(1)}, u32[]{:S(2)}, u32[]{:S(2)}) async-start(f32[16,1,512]{2,1,0:T(1,128)} %broadcast_in_dim.10), calls=%async_computation.1 | async-start | bytes 65536 | tf_op jit(solution)/shard_map/all_to_all | solution.py:132
  129.4 2.6 %add_convert_fusion = bf16[1024,512]{1,0:T(8,128)(2,1)} fusion(f32[1024,512]{1,0:T(8,128)S(1)} %get-tuple-element.10, bf16[1024,512]{1,0:T(8,128)(2,1)} %collective-permute-done.15), kind=kLoop, calls=%fused_computation.1 | loop fusion | flops 1572864 | bytes 4194304 | tf_op jit(solution)/shard_map/convert_element_type | solution.py:128
  132.0 9.9 %all-to-all-done.1 = f32[16,1,512]{2,1,0:T(1,128)S(1)} async-done(((f32[16,1,512]{2,1,0:T(1,128)}), f32[16,1,512]{2,1,0:T(1,128)S(1)}, u32[]{:S(2)}, u32[]{:S(2)}) %all-to-all-start.1) | async-done | bytes 32800 | tf_op jit(solution)/shard_map/all_to_all | solution.py:132
  141.9 6.2 %all-to-all-start.2 = ((bf16[32,32,512]{2,1,0:T(8,128)(2,1)}), bf16[32,32,512]{2,1,0:T(8,128)(2,1)S(1)}, u32[]{:S(2)}, u32[]{:S(2)}) async-start(bf16[32,32,512]{2,1,0:T(8,128)(2,1)} %bitcast.11), calls=%async_computation.2 | async-start | bytes 2097152 | tf_op jit(solution)/shard_map/all_to_all | solution.py:129
  148.2 1.1 fusion.2
  149.3 26.3 %all-to-all-done.2 = bf16[32,32,512]{2,1,0:T(8,128)(2,1)S(1)} async-done(((bf16[32,32,512]{2,1,0:T(8,128)(2,1)}), bf16[32,32,512]{2,1,0:T(8,128)(2,1)S(1)}, u32[]{:S(2)}, u32[]{:S(2)}) %all-to-all-start.2) | async-done | bytes 1048608 | tf_op jit(solution)/shard_map/all_to_all | solution.py:129
  175.6 0.8 convert_reduce_fusion
  (41 shorter events, 0.1 us)
Async XLA Ops:
  0.6 103.7 %copy-start = (bf16[512,512]{1,0:T(8,128)(2,1)S(1)}, bf16[512,512]{1,0:T(8,128)(2,1)}, u32[]{:S(2)}) copy-start(bf16[512,512]{1,0:T(8,128)(2,1)} %refs_17_.1) | copy-start | bytes 1572868
  0.6 97.4 %copy-start.24 = (bf16[512]{0:T(512)(128)(2,1)S(1)}, bf16[512]{0:T(512)(128)(2,1)}, u32[]{:S(2)}) copy-start(bf16[512]{0:T(512)(128)(2,1)} %param.6) | copy-start | bytes 3076
  0.6 26.8 %all-to-all-start = ((bf16[64,8,128]{2,1,0:T(8,128)(2,1)}), bf16[64,8,128]{2,1,0:T(8,128)(2,1)S(1)}, u32[]{:S(2)}, u32[]{:S(2)}) async-start(bf16[64,8,128]{2,1,0:T(8,128)(2,1)} %bitcast.13), calls=%async_computation | async-start | bytes 262144 | tf_op jit(solution)/shard_map/all_to_all | solution.py:97
  27.5 0.6 copy-start.23
  30.1 15.5 %collective-permute-start.7 = (bf16[144,512]{1,0:T(8,128)(2,1)}, bf16[144,512]{1,0:T(8,128)(2,1)S(1)}, u32[]{:S(2)}, u32[]{:S(2)}) collective-permute-start(bf16[144,512]{1,0:T(8,128)(2,1)} %place.1.refs_0_), channel_id=1, source_target_pairs={{0,1},{1,2},{2,3},{3,4},{4,5},{5,6},{6,7},{7,8},{8,9},{9,10},{10,1... | collective-permute-start | bytes 442376 | tf_op jit(solution)/shard_map/ppermute | solution.py:118
  32.0 15.5 %collective-permute-start = (bf16[144,512]{1,0:T(8,128)(2,1)}, bf16[144,512]{1,0:T(8,128)(2,1)S(1)}, u32[]{:S(2)}, u32[]{:S(2)}) collective-permute-start(bf16[144,512]{1,0:T(8,128)(2,1)} %place.1.refs_0_), channel_id=1, source_target_pairs={{0,15},{1,0},{2,1},{3,2},{4,3},{5,4},{6,5},{7,6},{8,7},{9,8},{10,9... | collective-permute-start | bytes 442376 | tf_op jit(solution)/shard_map/ppermute | solution.py:121
  45.6 8.2 %collective-permute-start.8 = (bf16[144,512]{1,0:T(8,128)(2,1)S(1)}, bf16[144,512]{1,0:T(8,128)(2,1)S(1)}, u32[]{:S(2)}, u32[]{:S(2)}) collective-permute-start(bf16[144,512]{1,0:T(8,128)(2,1)S(1)} %collective-permute-done.7.refs_15_), channel_id=1, source_target_pairs={{0,1},{1,2},{2,3},{3,4},{4,5},{5,6},{6,7},{7,8},{8,9},{9,10},{10,1... | collective-permute-start | bytes 442376 | tf_op jit(solution)/shard_map/ppermute | solution.py:118
  47.5 8.2 %collective-permute-start.1 = (bf16[144,512]{1,0:T(8,128)(2,1)S(1)}, bf16[144,512]{1,0:T(8,128)(2,1)S(1)}, u32[]{:S(2)}, u32[]{:S(2)}) collective-permute-start(bf16[144,512]{1,0:T(8,128)(2,1)S(1)} %collective-permute-done.refs_1_), channel_id=1, source_target_pairs={{0,15},{1,0},{2,1},{3,2},{4,3},{5,4},{6,5},{7,6},{8,7},{9,8},{10,9... | collective-permute-start | bytes 442376 | tf_op jit(solution)/shard_map/ppermute | solution.py:121
  53.8 8.2 %collective-permute-start.9 = (bf16[144,512]{1,0:T(8,128)(2,1)S(1)}, bf16[144,512]{1,0:T(8,128)(2,1)S(1)}, u32[]{:S(2)}, u32[]{:S(2)}) collective-permute-start(bf16[144,512]{1,0:T(8,128)(2,1)S(1)} %collective-permute-done.8.refs_14_), channel_id=1, source_target_pairs={{0,1},{1,2},{2,3},{3,4},{4,5},{5,6},{6,7},{7,8},{8,9},{9,10},{10,1... | collective-permute-start | bytes 442376 | tf_op jit(solution)/shard_map/ppermute | solution.py:118
  55.8 8.2 %collective-permute-start.2 = (bf16[144,512]{1,0:T(8,128)(2,1)S(1)}, bf16[144,512]{1,0:T(8,128)(2,1)S(1)}, u32[]{:S(2)}, u32[]{:S(2)}) collective-permute-start(bf16[144,512]{1,0:T(8,128)(2,1)S(1)} %collective-permute-done.1.refs_2_), channel_id=1, source_target_pairs={{0,15},{1,0},{2,1},{3,2},{4,3},{5,4},{6,5},{7,6},{8,7},{9,8},{10,9... | collective-permute-start | bytes 442376 | tf_op jit(solution)/shard_map/ppermute | solution.py:121
  62.1 8.2 %collective-permute-start.10 = (bf16[144,512]{1,0:T(8,128)(2,1)S(1)}, bf16[144,512]{1,0:T(8,128)(2,1)S(1)}, u32[]{:S(2)}, u32[]{:S(2)}) collective-permute-start(bf16[144,512]{1,0:T(8,128)(2,1)S(1)} %collective-permute-done.9.refs_13_), channel_id=1, source_target_pairs={{0,1},{1,2},{2,3},{3,4},{4,5},{5,6},{6,7},{7,8},{8,9},{9,10},{10,1... | collective-permute-start | bytes 442376 | tf_op jit(solution)/shard_map/ppermute | solution.py:118
  64.0 8.9 %collective-permute-start.3 = (bf16[144,512]{1,0:T(8,128)(2,1)S(1)}, bf16[144,512]{1,0:T(8,128)(2,1)S(1)}, u32[]{:S(2)}, u32[]{:S(2)}) collective-permute-start(bf16[144,512]{1,0:T(8,128)(2,1)S(1)} %collective-permute-done.2.refs_3_), channel_id=1, source_target_pairs={{0,15},{1,0},{2,1},{3,2},{4,3},{5,4},{6,5},{7,6},{8,7},{9,8},{10,9... | collective-permute-start | bytes 442376 | tf_op jit(solution)/shard_map/ppermute | solution.py:121
  70.3 8.4 %collective-permute-start.11 = (bf16[144,512]{1,0:T(8,128)(2,1)S(1)}, bf16[144,512]{1,0:T(8,128)(2,1)S(1)}, u32[]{:S(2)}, u32[]{:S(2)}) collective-permute-start(bf16[144,512]{1,0:T(8,128)(2,1)S(1)} %collective-permute-done.10.refs_12_), channel_id=1, source_target_pairs={{0,1},{1,2},{2,3},{3,4},{4,5},{5,6},{6,7},{7,8},{8,9},{9,10},{10,1... | collective-permute-start | bytes 442376 | tf_op jit(solution)/shard_map/ppermute | solution.py:118
  72.2 0.6 copy-start.5
  72.9 8.4 %collective-permute-start.4 = (bf16[144,512]{1,0:T(8,128)(2,1)S(1)}, bf16[144,512]{1,0:T(8,128)(2,1)S(1)}, u32[]{:S(2)}, u32[]{:S(2)}) collective-permute-start(bf16[144,512]{1,0:T(8,128)(2,1)S(1)} %collective-permute-done.3.refs_4_), channel_id=1, source_target_pairs={{0,15},{1,0},{2,1},{3,2},{4,3},{5,4},{6,5},{7,6},{8,7},{9,8},{10,9... | collective-permute-start | bytes 442376 | tf_op jit(solution)/shard_map/ppermute | solution.py:121
  78.0 0.7 copy-start.7
  78.7 8.4 %collective-permute-start.12 = (bf16[144,512]{1,0:T(8,128)(2,1)S(1)}, bf16[144,512]{1,0:T(8,128)(2,1)S(1)}, u32[]{:S(2)}, u32[]{:S(2)}) collective-permute-start(bf16[144,512]{1,0:T(8,128)(2,1)S(1)} %collective-permute-done.11.refs_11_), channel_id=1, source_target_pairs={{0,1},{1,2},{2,3},{3,4},{4,5},{5,6},{6,7},{7,8},{8,9},{9,10},{10,1... | collective-permute-start | bytes 442376 | tf_op jit(solution)/shard_map/ppermute | solution.py:118
  80.6 0.7 copy-start.9
  81.3 8.4 %collective-permute-start.5 = (bf16[144,512]{1,0:T(8,128)(2,1)S(1)}, bf16[144,512]{1,0:T(8,128)(2,1)S(1)}, u32[]{:S(2)}, u32[]{:S(2)}) collective-permute-start(bf16[144,512]{1,0:T(8,128)(2,1)S(1)} %collective-permute-done.4.refs_5_), channel_id=1, source_target_pairs={{0,15},{1,0},{2,1},{3,2},{4,3},{5,4},{6,5},{7,6},{8,7},{9,8},{10,9... | collective-permute-start | bytes 442376 | tf_op jit(solution)/shard_map/ppermute | solution.py:121
  86.4 0.7 copy-start.11
  87.0 8.4 %collective-permute-start.13 = (bf16[144,512]{1,0:T(8,128)(2,1)S(1)}, bf16[144,512]{1,0:T(8,128)(2,1)S(1)}, u32[]{:S(2)}, u32[]{:S(2)}) collective-permute-start(bf16[144,512]{1,0:T(8,128)(2,1)S(1)} %collective-permute-done.12.refs_10_), channel_id=1, source_target_pairs={{0,1},{1,2},{2,3},{3,4},{4,5},{5,6},{6,7},{7,8},{8,9},{9,10},{10,1... | collective-permute-start | bytes 442376 | tf_op jit(solution)/shard_map/ppermute | solution.py:118
  89.0 0.7 copy-start.13
  89.6 8.5 %collective-permute-start.6 = (bf16[144,512]{1,0:T(8,128)(2,1)S(1)}, bf16[144,512]{1,0:T(8,128)(2,1)S(1)}, u32[]{:S(2)}, u32[]{:S(2)}) collective-permute-start(bf16[144,512]{1,0:T(8,128)(2,1)S(1)} %collective-permute-done.5.refs_6_), channel_id=1, source_target_pairs={{0,15},{1,0},{2,1},{3,2},{4,3},{5,4},{6,5},{7,6},{8,7},{9,8},{10,9... | collective-permute-start | bytes 442376 | tf_op jit(solution)/shard_map/ppermute | solution.py:121
  94.8 0.7 copy-start.15
  95.4 8.2 %collective-permute-start.14 = (bf16[144,512]{1,0:T(8,128)(2,1)S(1)}, bf16[144,512]{1,0:T(8,128)(2,1)S(1)}, u32[]{:S(2)}, u32[]{:S(2)}) collective-permute-start(bf16[144,512]{1,0:T(8,128)(2,1)S(1)} %collective-permute-done.13.refs_9_), channel_id=1, source_target_pairs={{0,1},{1,2},{2,3},{3,4},{4,5},{5,6},{6,7},{7,8},{8,9},{9,10},{10,1... | collective-permute-start | bytes 442376 | tf_op jit(solution)/shard_map/ppermute | solution.py:118
  97.3 0.7 copy-start.17
  98.1 0.7 copy-start.19
  103.7 0.6 copy-start.21
  104.3 1.6 copy-start.1
  105.9 0.9 copy-start.4
  106.8 0.9 copy-start.6
  107.7 0.9 copy-start.8
  108.6 0.9 copy-start.10
  109.5 0.9 copy-start.12
  110.5 0.9 copy-start.14
  111.4 0.9 copy-start.16
  112.3 0.9 copy-start.18
  113.2 0.9 copy-start.20
  114.1 0.9 copy-start.22
  120.1 1.0 copy-start.2
  121.1 8.3 %collective-permute-start.15 = (bf16[1024,512]{1,0:T(8,128)(2,1)}, bf16[1024,512]{1,0:T(8,128)(2,1)}, u32[]{:S(2)}, u32[]{:S(2)}) collective-permute-start(bf16[1024,512]{1,0:T(8,128)(2,1)} %get-tuple-element.11), channel_id=1, source_target_pairs={{0,16},{16,0},{1,17},{17,1},{2,18},{18,2},{3,19},{19,3},{4,20},{20... | collective-permute-start | bytes 3145736 | tf_op jit(solution)/shard_map/ppermute | solution.py:127
  123.7 18.3 %all-to-all-start.1 = ((f32[16,1,512]{2,1,0:T(1,128)}), f32[16,1,512]{2,1,0:T(1,128)S(1)}, u32[]{:S(2)}, u32[]{:S(2)}) async-start(f32[16,1,512]{2,1,0:T(1,128)} %broadcast_in_dim.10), calls=%async_computation.1 | async-start | bytes 65536 | tf_op jit(solution)/shard_map/all_to_all | solution.py:132
  132.0 16.2 %copy-start.3 = (f32[512,512]{1,0:T(8,128)S(1)}, f32[512,512]{1,0:T(8,128)}, u32[]{:S(2)}) copy-start(f32[512,512]{1,0:T(8,128)} %copy-done.2) | copy-start | bytes 3145732
  141.9 33.6 %all-to-all-start.2 = ((bf16[32,32,512]{2,1,0:T(8,128)(2,1)}), bf16[32,32,512]{2,1,0:T(8,128)(2,1)S(1)}, u32[]{:S(2)}, u32[]{:S(2)}) async-start(bf16[32,32,512]{2,1,0:T(8,128)(2,1)} %bitcast.11), calls=%async_computation.2 | async-start | bytes 2097152 | tf_op jit(solution)/shard_map/all_to_all | solution.py:129

commit v2 on v0

v2 whole, which is shorter than its diff:
```python
import jax
import jax.numpy as jnp
from jax import lax
from jax.experimental import pallas as pl
from jax.experimental.pallas import tpu as pltpu
from jax.sharding import Mesh, PartitionSpec as P


D = 8192
EPS = 1e-06
ROWS = 512
FEAT = 512
COLS = 128
FAR = 4
NEAR = 4
TP = FAR * NEAR
CHIPS = 32
DP = 2 * CHIPS
HALF = FAR * COLS // 2
Z = ("zh", "zl")
TRANSPOSED = (((0,), (0,)), ((), ()))


def call(body, grid, inputs, outputs, shapes, flops, moved):
    return pl.pallas_call(
        body,
        grid_spec=pltpu.PrefetchScalarGridSpec(
            num_scalar_prefetch=1, grid=(grid,), in_specs=inputs, out_specs=outputs
        ),
        out_shape=shapes,
        cost_estimate=pl.CostEstimate(flops=flops, bytes_accessed=moved, transcendentals=0),
    )


def block(shape, index):
    return pl.BlockSpec(shape, index)


def fixed(shape):
    return pl.BlockSpec(shape, lambda i, where: (0,) * len(shape))


def rows_at(shape):
    return pl.BlockSpec(shape, lambda i, where: (i,) + (0,) * (len(shape) - 1))


def w_rows(shift, first=0):
    return pl.BlockSpec((COLS, FEAT), lambda i, where: ((first + i) * NEAR + lax.rem(where[0] + shift, NEAR), 0))


def place_kernel(where, received, onehot, out):
    picked = lax.dot_general(received[...], onehot[...], TRANSPOSED, preferred_element_type=jnp.float32)
    out[...] = picked.astype(jnp.bfloat16)


def place(where, received, onehot):
    return call(
        place_kernel,
        FAR,
        [rows_at((ROWS, COLS)), fixed((ROWS, ROWS))],
        rows_at((COLS, ROWS)),
        jax.ShapeDtypeStruct((FAR * COLS, ROWS), jnp.bfloat16),
        2 * FAR * ROWS * ROWS * COLS,
        3 * ROWS * ROWS * 2,
    )(where, received, onehot)


def grad_own_kernel(where, own, w, out):
    @pl.when(pl.program_id(0) == 0)
    def _():
        out[...] = jnp.zeros_like(out)

    out[...] += lax.dot_general(own[...], w[...], TRANSPOSED, preferred_element_type=jnp.float32)


def grad_own(where, own, w_kv):
    return call(
        grad_own_kernel,
        FAR,
        [rows_at((COLS, ROWS)), w_rows(0)],
        fixed((ROWS, FEAT)),
        jax.ShapeDtypeStruct((ROWS, FEAT), jnp.float32),
        2 * FAR * ROWS * FEAT * COLS,
        4 * ROWS * ROWS * 2,
    )(where, own, w_kv)


def grad_near_kernel(where, behind, ahead, w_behind, w_ahead, before, out):
    @pl.when(pl.program_id(0) == 0)
    def _():
        out[...] = before[...]

    term = lax.dot_general(behind[...], w_behind[...], TRANSPOSED, preferred_element_type=jnp.float32)
    term = term + lax.dot_general(ahead[...], w_ahead[...], TRANSPOSED, preferred_element_type=jnp.float32)
    out[...] += term


def grad_near(where, behind, ahead, w_kv, before):
    return call(
        grad_near_kernel,
        FAR,
        [rows_at((COLS, ROWS)), rows_at((COLS, ROWS)), w_rows(NEAR - 1), w_rows(1), fixed((ROWS, FEAT))],
        fixed((ROWS, FEAT)),
        jax.ShapeDtypeStruct((ROWS, FEAT), jnp.float32),
        4 * FAR * ROWS * FEAT * COLS,
        8 * ROWS * ROWS * 2,
    )(where, behind, ahead, w_kv, w_kv, before)


def grad_last_kernel(where, far_a, far_b, w_a, w_b, before, x, gain, out, products):
    @pl.when(pl.program_id(0) == 0)
    def _():
        out[...] = before[...]

    term = lax.dot_general(far_a[...], w_a[...], TRANSPOSED, preferred_element_type=jnp.float32)
    term = term + lax.dot_general(far_b[...], w_b[...], TRANSPOSED, preferred_element_type=jnp.float32)
    out[...] += term

    @pl.when(pl.program_id(0) == 1)
    def _():
        part = x[...].astype(jnp.float32) * gain[...].astype(jnp.float32) * out[...]
        lanes = part[:, :COLS]
        for i in range(1, FEAT // COLS):
            lanes = lanes + part[:, COLS * i : COLS * (i + 1)]
        products[...] = jnp.sum(lanes.T, axis=0, keepdims=True)


def grad_last(where, far_a, far_b, w_kv, before, x, gain):
    return call(
        grad_last_kernel,
        2,
        [
            rows_at((COLS, ROWS)),
            rows_at((COLS, ROWS)),
            w_rows(2),
            w_rows(2, 2),
            fixed((ROWS, FEAT)),
            fixed((ROWS, FEAT)),
            fixed((1, FEAT)),
        ],
        [fixed((ROWS, FEAT)), fixed((1, ROWS))],
        [jax.ShapeDtypeStruct((ROWS, FEAT), jnp.float32), jax.ShapeDtypeStruct((1, ROWS), jnp.float32)],
        2 * FAR * ROWS * FEAT * COLS,
        8 * ROWS * ROWS * 2,
    )(where, far_a, far_b, w_kv, w_kv, before, x, gain)


def split_rows(where, term):
    first = where[1] == 0
    low = jnp.concatenate([term[0:32], term[64:96]], axis=0)
    high = jnp.concatenate([term[32:64], term[96:128]], axis=0)
    return jnp.where(first, low, high), jnp.where(first, high, low).astype(jnp.bfloat16)


def weight_near_kernel(where, own, behind, ahead, normed, keep, send):
    for group, ref in enumerate((own, behind, ahead)):
        term = jnp.dot(ref[...], normed[...], preferred_element_type=jnp.float32)
        kept, sent = split_rows(where, term)
        keep[0, group] = kept
        send[0, group] = sent


def weight_near(where, own, behind, ahead, normed):
    spec = rows_at((1, 3, COLS // 2, FEAT))
    return call(
        weight_near_kernel,
        FAR,
        [rows_at((COLS, ROWS))] * 3 + [fixed((ROWS, FEAT))],
        [spec, spec],
        [
            jax.ShapeDtypeStruct((FAR, 3, COLS // 2, FEAT), jnp.float32),
            jax.ShapeDtypeStruct((FAR, 3, COLS // 2, FEAT), jnp.bfloat16),
        ],
        6 * FAR * ROWS * FEAT * COLS,
        12 * ROWS * ROWS * 2,
    )(where, own, behind, ahead, normed)


def weight_far_kernel(where, far_a, far_b, normed, keep, send):
    for group, ref in enumerate((far_a, far_b)):
        term = jnp.dot(ref[...], normed[...], preferred_element_type=jnp.float32)
        kept, sent = split_rows(where, term)
        keep[group, 0] = kept
        send[group, 0] = sent


def weight_far(where, far_a, far_b, normed):
    spec = block((2, 1, COLS // 2, FEAT), lambda i, where: (0, i, 0, 0))
    return call(
        weight_far_kernel,
        2,
        [rows_at((COLS, ROWS))] * 2 + [fixed((ROWS, FEAT))],
        [spec, spec],
        [
            jax.ShapeDtypeStruct((2, 2, COLS // 2, FEAT), jnp.float32),
            jax.ShapeDtypeStruct((2, 2, COLS // 2, FEAT), jnp.bfloat16),
        ],
        2 * FAR * ROWS * FEAT * COLS,
        5 * ROWS * ROWS * 2,
    )(where, far_a, far_b, normed)


def combine_kernel(where, keep_near, taken_near, keep_far, taken_far, out):
    for group, shift in enumerate((0, NEAR - 1, 1)):
        total = keep_near[0, group] + taken_near[0, group].astype(jnp.float32)
        out[0, lax.rem(where[0] + shift, NEAR)] = total.astype(jnp.bfloat16)
    total = keep_far[0] + taken_far[0].astype(jnp.float32)
    out[0, lax.rem(where[0] + 2, NEAR)] = total.astype(jnp.bfloat16)


def combine(where, keep_near, taken_near, keep_far, taken_far):
    near = rows_at((1, 3, COLS // 2, FEAT))
    far = rows_at((1, COLS // 2, FEAT))
    return call(
        combine_kernel,
        FAR,
        [near, near, far, far],
        rows_at((1, NEAR, COLS // 2, FEAT)),
        jax.ShapeDtypeStruct((FAR, NEAR, COLS // 2, FEAT), jnp.bfloat16),
        TP * COLS * FEAT,
        8 * ROWS * ROWS * 2,
    )(where, keep_near, taken_near, keep_far, taken_far)


def tensor_sum(vector):
    spread = jnp.broadcast_to(vector.reshape(1, ROWS), (TP, ROWS))
    return jnp.sum(lax.all_to_all(spread, Z, split_axis=0, concat_axis=0, tiled=True), axis=0)


def hop(array, step):
    return lax.ppermute(array, Z, [(i, (i + step) % TP) for i in range(TP)])


def swap(array):
    return lax.ppermute(array, "core", [(0, 1), (1, 0)])


def step(layer_input, gain, w_kv, d_kv, destination):
    where = jnp.stack([lax.axis_index("zl"), lax.axis_index("core")]).astype(jnp.int32)

    spread = jnp.broadcast_to(d_kv.reshape(1, DP, 8, COLS), (FAR, DP, 8, COLS)).reshape(FAR * DP, 8, COLS)
    received = lax.all_to_all(spread, ("zh", "chip", "core"), split_axis=0, concat_axis=0, tiled=True)

    ids = jnp.arange(ROWS, dtype=jnp.int32)
    same = (destination[:, None] == destination[None, :]) & (ids[:, None] < ids[None, :])
    slot_rank = jnp.sum(same.astype(jnp.int32), axis=0)
    position = jnp.where(destination >= 0, destination * 8 + slot_rank, -1)
    onehot = (ids[:, None] == position[None, :]).astype(jnp.bfloat16)

    values = layer_input.astype(jnp.float32)
    gain_wide = gain.astype(jnp.float32)
    squares = jnp.sum(values * values, axis=1)
    onehot, squares, where = lax.optimization_barrier((onehot, squares, where))

    own = place(where, received.reshape(FAR * ROWS, COLS), onehot)
    own, squares = lax.optimization_barrier((own, squares))
    behind = hop(own, 1)
    ahead = hop(own, -1)
    inverse = lax.rsqrt(tensor_sum(squares) / D + EPS)
    normed = (values * inverse[:, None] * gain_wide).astype(jnp.bfloat16)
    far_a = hop(behind[:HALF], 1)
    far_b = hop(ahead[HALF:], -1)

    grad = grad_own(where, own, w_kv)
    grad = grad_near(where, behind, ahead, w_kv, grad)
    keep_near, send_near = weight_near(where, own, behind, ahead, normed)
    taken_near = swap(send_near)
    dnormed, products = grad_last(where, far_a, far_b, w_kv, grad, layer_input, gain[None, :])
    mean_dot = tensor_sum(products) / D

    keep_far, send_far = weight_far(where, far_a, far_b, normed)
    taken_far = swap(send_far)
    shape = (FAR, COLS // 2, FEAT)
    pair = combine(where, keep_near, taken_near, keep_far.reshape(shape), taken_far.reshape(shape))
    pair, mean_dot, inverse, dnormed = lax.optimization_barrier((pair, mean_dot, inverse, dnormed))
    parts = lax.all_to_all(pair.reshape(CHIPS, 32, FEAT), "chip", split_axis=0, concat_axis=0, tiled=True)
    grad_weight = jnp.sum(parts.astype(jnp.float32), axis=0)
    grad_x = (inverse[:, None] * gain_wide * dnormed - values * (inverse**3 * mean_dot)[:, None]).astype(jnp.bfloat16)
    return (grad_x, grad_weight)


def solution(mesh):
    fine = Mesh(mesh.devices.reshape(CHIPS, 2, FAR, NEAR), ("chip", "core", "zh", "zl"))
    dp = ("chip", "core")
    return jax.shard_map(
        step,
        mesh=fine,
        in_specs=(P(dp, Z), P(Z), P(None, Z), P(dp, Z), P(dp)),
        out_specs=(P(dp, Z), P(dp, Z)),
        check_vma=False,
    )
```

time: 316 us -> 198 us (0.63)
  the two profiles are of different devices: /device:TPU:16 before, /device:TPU:2 now
where the time goes in v2:
time: 198 us; the launch traced here: 197 us
  waiting for transfers between devices  78.7 us (40%)
  starting transfers between devices  67.8 us (34%)
  Pallas kernels  32.8 us (17%)
  local copies, waits for them, and re-layouts  10.3 us (5%)
  other arithmetic  6.65 us (3%)
    all_to_all x1, waiting for transfers between devices, step(): lax.all_to_all(spread, ('zh', 'chip', 'core'), split_axis=0, concat_axis=...  33.5 us
    all_to_all x1, starting transfers between devices, step(): lax.all_to_all(spread, ('zh', 'chip', 'core'), split_axis=0, concat_axis=...  29.8 us
    all_to_all x1, waiting for transfers between devices, step(): lax.all_to_all(pair.reshape(CHIPS, 32, FEAT), 'chip', split_axis=0, conca...  26.1 us
    all_to_all x2, starting transfers between devices, tensor_sum(): lax.all_to_all(spread, Z, split_axis=0, concat_axis=0, tiled=True)  14.6 us
    ppermute x4, starting transfers between devices, hop(): return lax.ppermute(array, Z, [(i, (i + step) % TP) for i in range(TP)])  14.1 us
    all_to_all x2, waiting for transfers between devices, tensor_sum(): lax.all_to_all(spread, Z, split_axis=0, concat_axis=0, tiled=True)  13.1 us
    ppermute x4, waiting for transfers between devices, hop(): return lax.ppermute(array, Z, [(i, (i + step) % TP) for i in range(TP)])  5.9 us
    pallas_call x1, Pallas kernels, grad_near(): call(grad_near_kernel, FAR, [rows_at((COLS, ROWS)), rows_at((COLS, ROWS))...  5.83 us
  transfers between devices with their start and end apart: 10, of which 6 were waited for; matrix products, arithmetic and copies ran while one was open for 5% of the time, Pallas kernels for 9%

profile of v2, /device:TPU:2, one launch (start us, length us, event | category | flops | bytes accessed | tf_op | source)
XLA Modules:
  0.0 197.1 jit_solution(11198391643323089154)
XLA Ops:
  0.6 0.0 copy-start.10
  0.6 0.0 copy-start.11
  0.7 0.0 copy-start
  0.7 1.8 broadcast_in_dim.16
  2.5 29.8 %all-to-all-start = ((bf16[256,8,128]{2,1,0:T(8,128)(2,1)}), bf16[256,8,128]{2,1,0:T(8,128)(2,1)S(1)}, u32[]{:S(2)}, u32[]{:S(2)}) async-start(bf16[256,8,128]{2,1,0:T(8,128)(2,1)} %bitcast.3), calls=%async_computation | async-start | bytes 1048576 | tf_op jit(solution)/shard_map/all_to_all | solution.py:242
  32.3 0.6 pad_add_fusion.where
  32.9 0.9 convert_reduce_fusion.1
  33.9 1.2 fusion
  35.1 0.0 copy-done.10
  35.1 0.9 fusion.5.onehot
  36.0 33.5 %all-to-all-done = bf16[256,8,128]{2,1,0:T(8,128)(2,1)S(1)} async-done(((bf16[256,8,128]{2,1,0:T(8,128)(2,1)}), bf16[256,8,128]{2,1,0:T(8,128)(2,1)S(1)}, u32[]{:S(2)}, u32[]{:S(2)}) %all-to-all-start) | async-done | bytes 524320 | tf_op jit(solution)/shard_map/all_to_all | solution.py:242
  69.6 0.0 copy-start.2
  69.6 0.8 copy-done.2
  70.4 4.5 %shard_map.68.own = bf16[512,512]{1,0:T(8,128)(2,1)} custom-call(s32[2]{0:T(128)} %pad_add_fusion.where, bf16[2048,128]{1,0:T(8,128)(2,1)} %bitcast.10, bf16[512,512]{1,0:T(8,128)(2,1)} %fusion.5.onehot), custom_call_target="tpu_custom_call" | custom-call | flops 268435456 | bytes 1572864 | tf_op jit(solution)/shard_map/pallas_call | solution.py:57
  74.9 0.6 broadcast_in_dim.17
  75.5 3.5 %all-to-all-start.1 = ((f32[16,1,512]{2,1,0:T(1,128)}), f32[16,1,512]{2,1,0:T(1,128)S(1)}, u32[]{:S(2)}, u32[]{:S(2)}) async-start(f32[16,1,512]{2,1,0:T(1,128)} %broadcast_in_dim.17), calls=%async_computation.1 | async-start | bytes 65536 | tf_op jit(solution)/shard_map/all_to_all | solution.py:227
  79.0 3.7 %collective-permute-start = (bf16[512,512]{1,0:T(8,128)(2,1)}, bf16[512,512]{1,0:T(8,128)(2,1)S(1)}, u32[]{:S(2)}, u32[]{:S(2)}) collective-permute-start(bf16[512,512]{1,0:T(8,128)(2,1)} %shard_map.68.own), channel_id=1, source_target_pairs={{0,1},{1,2},{2,3},{3,4},{4,5},{5,6},{6,7},{7,8},{8,9},{9,10},{10,1... | collective-permute-start | bytes 1572872 | tf_op jit(solution)/shard_map/ppermute | solution.py:231
  82.8 3.3 %collective-permute-start.1 = (bf16[512,512]{1,0:T(8,128)(2,1)}, bf16[512,512]{1,0:T(8,128)(2,1)S(1)}, u32[]{:S(2)}, u32[]{:S(2)}) collective-permute-start(bf16[512,512]{1,0:T(8,128)(2,1)} %shard_map.68.own), channel_id=1, source_target_pairs={{0,15},{1,0},{2,1},{3,2},{4,3},{5,4},{6,5},{7,6},{8,7},{9,8},{10,9... | collective-permute-start | bytes 1572872 | tf_op jit(solution)/shard_map/ppermute | solution.py:231
  86.1 0.0 copy-done.11
  86.1 5.8 %all-to-all-done.1 = f32[16,1,512]{2,1,0:T(1,128)S(1)} async-done(((f32[16,1,512]{2,1,0:T(1,128)}), f32[16,1,512]{2,1,0:T(1,128)S(1)}, u32[]{:S(2)}, u32[]{:S(2)}) %all-to-all-start.1) | async-done | bytes 32800 | tf_op jit(solution)/shard_map/all_to_all | solution.py:227
  91.9 0.0 copy-done
  91.9 1.0 fusion.2.normed
  93.0 4.4 %collective-permute-done.behind = bf16[512,512]{1,0:T(8,128)(2,1)S(1)} collective-permute-done((bf16[512,512]{1,0:T(8,128)(2,1)}, bf16[512,512]{1,0:T(8,128)(2,1)S(1)}, u32[]{:S(2)}, u32[]{:S(2)}) %collective-permute-start) | collective-permute-done | bytes 524320 | tf_op jit(solution)/shard_map/ppermute | solution.py:231
  97.3 0.0 copy-start.3
  97.3 1.5 collective-permute-done.1.ahead
  98.9 0.0 copy-done.3
  98.9 0.0 copy-start.4
  98.9 0.8 copy-done.4
  99.7 5.5 %shard_map.69 = (f32[4,3,64,512]{3,2,1,0:T(8,128)}, bf16[4,3,64,512]{3,2,1,0:T(8,128)(2,1)}) custom-call(s32[2]{0:T(128)} %pad_add_fusion.where, bf16[512,512]{1,0:T(8,128)(2,1)} %shard_map.68.own, bf16[512,512]{1,0:T(8,128)(2,1)} %copy-done.3, bf16[512,512]{1,0:T(8,128)(2,1)} %copy-done.4, bf16[512,512]{1,0:T(8,128)(2,1)} %fusion.2.normed), custom_call_target="tpu_custom_call" | custom-call | flops 805306368 | bytes 6291456 | tf_op jit(solution)/shard_map/pallas_call | solution.py:165
  105.2 1.9 collective-permute-start.2
  107.1 1.0 slice.8
  108.1 3.4 %collective-permute-start.3 = (bf16[256,512]{1,0:T(8,128)(2,1)S(1)}, bf16[256,512]{1,0:T(8,128)(2,1)S(1)}, u32[]{:S(2)}, u32[]{:S(2)}) collective-permute-start(bf16[256,512]{1,0:T(8,128)(2,1)S(1)} %slice.8), channel_id=1, source_target_pairs={{0,1},{1,2},{2,3},{3,4},{4,5},{5,6},{6,7},{7,8},{8,9},{9,10},{10,1... | collective-permute-start | bytes 786440 | tf_op jit(solution)/shard_map/ppermute | solution.py:231
  111.5 1.0 slice.9
  112.5 3.7 %collective-permute-start.4 = (bf16[256,512]{1,0:T(8,128)(2,1)S(1)}, bf16[256,512]{1,0:T(8,128)(2,1)S(1)}, u32[]{:S(2)}, u32[]{:S(2)}) collective-permute-start(bf16[256,512]{1,0:T(8,128)(2,1)S(1)} %slice.9), channel_id=1, source_target_pairs={{0,15},{1,0},{2,1},{3,2},{4,3},{5,4},{6,5},{7,6},{8,7},{9,8},{10,9... | collective-permute-start | bytes 786440 | tf_op jit(solution)/shard_map/ppermute | solution.py:231
  116.1 0.6 broadcast_in_dim.18.gain
  116.7 4.7 %shard_map.72.before = f32[512,512]{1,0:T(8,128)} custom-call(s32[2]{0:T(128)} %pad_add_fusion.where, bf16[512,512]{1,0:T(8,128)(2,1)} %shard_map.68.own, bf16[2048,512]{1,0:T(8,128)(2,1)} %w_b.1), custom_call_target="tpu_custom_call" | custom-call | flops 268435456 | bytes 2097152 | tf_op jit(solution)/shard_map/pallas_call | solution.py:77
  121.4 5.8 %shard_map.73.before = f32[512,512]{1,0:T(8,128)} custom-call(s32[2]{0:T(128)} %pad_add_fusion.where, bf16[512,512]{1,0:T(8,128)(2,1)} %copy-done.3, bf16[512,512]{1,0:T(8,128)(2,1)} %copy-done.4, bf16[2048,512]{1,0:T(8,128)(2,1)} %w_b.1, bf16[2048,512]{1,0:T(8,128)(2,1)} %w_b.1, f32[512,512]{1,0:T(8,128)} %shard_map.72.before), custom_call_target="tpu_custom_call" | custom-call | flops 536870912 | bytes 4194304 | tf_op jit(solution)/shard_map/pallas_call | solution.py:99
  127.2 0.0 collective-permute-done.3.far_a
  127.2 0.0 copy-start.6
  127.2 0.0 collective-permute-done.4.far_b
  127.2 0.7 copy-done.6
  127.9 0.0 copy-start.7
  127.9 0.7 copy-done.7
  128.7 4.6 %shard_map.74 = (f32[512,512]{1,0:T(8,128)}, f32[1,512]{1,0:T(1,128)}) custom-call(s32[2]{0:T(128)} %pad_add_fusion.where, bf16[256,512]{1,0:T(8,128)(2,1)} %copy-done.6, bf16[256,512]{1,0:T(8,128)(2,1)} %copy-done.7, bf16[2048,512]{1,0:T(8,128)(2,1)} %w_b.1, bf16[2048,512]{1,0:T(8,128)(2,1)} %w_b.1, f32[512,512]{1,0:T(8,128)} %shard_map.73.before, ...), custom_call_target="tpu_custom_call" | custom-call | flops 268435456 | bytes 4194304 | tf_op jit(solution)/shard_map/pallas_call | solution.py:129
  133.2 1.3 broadcast_in_dim.19
  134.5 11.1 %all-to-all-start.2 = ((f32[16,1,512]{2,1,0:T(1,128)}), f32[16,1,512]{2,1,0:T(1,128)S(1)}, u32[]{:S(2)}, u32[]{:S(2)}) async-start(f32[16,1,512]{2,1,0:T(1,128)} %broadcast_in_dim.19), calls=%async_computation.2 | async-start | bytes 65536 | tf_op jit(solution)/shard_map/all_to_all | solution.py:227
  145.7 3.3 %shard_map.70 = (f32[2,2,64,512]{3,2,1,0:T(8,128)}, bf16[2,2,64,512]{3,2,1,0:T(8,128)(2,1)}) custom-call(s32[2]{0:T(128)} %pad_add_fusion.where, bf16[256,512]{1,0:T(8,128)(2,1)} %copy-done.6, bf16[256,512]{1,0:T(8,128)(2,1)} %copy-done.7, bf16[512,512]{1,0:T(8,128)(2,1)} %fusion.2.normed), custom_call_target="tpu_custom_call" | custom-call | flops 268435456 | bytes 2621440 | tf_op jit(solution)/shard_map/pallas_call | solution.py:189
  148.9 1.9 collective-permute-start.5
  150.8 7.4 %all-to-all-done.2 = f32[16,1,512]{2,1,0:T(1,128)S(1)} async-done(((f32[16,1,512]{2,1,0:T(1,128)}), f32[16,1,512]{2,1,0:T(1,128)S(1)}, u32[]{:S(2)}, u32[]{:S(2)}) %all-to-all-start.2) | async-done | bytes 32800 | tf_op jit(solution)/shard_map/all_to_all | solution.py:227
  158.3 0.0 collective-permute-done.5
  158.3 0.0 copy-start.9
  158.3 0.0 collective-permute-done.2.taken_near
  158.3 0.0 copy-start.8
  158.3 0.7 copy-done.9
  159.0 0.3 copy-done.8
  159.2 4.4 %shard_map.71 = bf16[4,4,64,512]{3,2,1,0:T(8,128)(2,1)} custom-call(s32[2]{0:T(128)} %pad_add_fusion.where, f32[4,3,64,512]{3,2,1,0:T(8,128)} %get-tuple-element.22.keep_near, bf16[4,3,64,512]{3,2,1,0:T(8,128)(2,1)} %copy-done.8, f32[4,64,512]{2,1,0:T(8,128)} %bitcast.11, bf16[4,64,512]{2,1,0:T(8,128)(2,1)} %bitcast.12), custom_call_target="tpu_custom_call" | custom-call | flops 1048576 | bytes 4194304 | tf_op jit(solution)/shard_map/pallas_call | solution.py:214
  163.7 0.0 copy-start.1
  163.7 0.0 copy-start.5
  163.7 5.4 %all-to-all-start.3 = ((bf16[32,32,512]{2,1,0:T(8,128)(2,1)}), bf16[32,32,512]{2,1,0:T(8,128)(2,1)S(1)}, u32[]{:S(2)}, u32[]{:S(2)}) async-start(bf16[32,32,512]{2,1,0:T(8,128)(2,1)} %bitcast.9), calls=%async_computation.3 | async-start | bytes 2097152 | tf_op jit(solution)/shard_map/all_to_all | solution.py:276
  169.1 0.0 copy-done.1
  169.1 0.0 copy-done.5
  169.1 1.1 fusion.4
  170.2 26.1 %all-to-all-done.3 = bf16[32,32,512]{2,1,0:T(8,128)(2,1)S(1)} async-done(((bf16[32,32,512]{2,1,0:T(8,128)(2,1)}), bf16[32,32,512]{2,1,0:T(8,128)(2,1)S(1)}, u32[]{:S(2)}, u32[]{:S(2)}) %all-to-all-start.3) | async-done | bytes 1048608 | tf_op jit(solution)/shard_map/all_to_all | solution.py:276
  196.3 0.8 convert_reduce_fusion
  (7 shorter events, 0.1 us)
Async XLA Ops:
  0.6 34.5 %copy-start.10 = (s32[512]{0:T(512)S(1)}, s32[512]{0:T(512)}, u32[]{:S(2)}) copy-start(s32[512]{0:T(512)} %param.9) | copy-start | bytes 6148
  0.6 85.5 %copy-start.11 = (bf16[512]{0:T(512)(128)(2,1)S(1)}, bf16[512]{0:T(512)(128)(2,1)}, u32[]{:S(2)}) copy-start(bf16[512]{0:T(512)(128)(2,1)} %param.6) | copy-start | bytes 3076
  0.7 91.3 %copy-start = (bf16[512,512]{1,0:T(8,128)(2,1)S(1)}, bf16[512,512]{1,0:T(8,128)(2,1)}, u32[]{:S(2)}) copy-start(bf16[512,512]{1,0:T(8,128)(2,1)} %x.1) | copy-start | bytes 1572868
  2.5 67.1 %all-to-all-start = ((bf16[256,8,128]{2,1,0:T(8,128)(2,1)}), bf16[256,8,128]{2,1,0:T(8,128)(2,1)S(1)}, u32[]{:S(2)}, u32[]{:S(2)}) async-start(bf16[256,8,128]{2,1,0:T(8,128)(2,1)} %bitcast.3), calls=%async_computation | async-start | bytes 1048576 | tf_op jit(solution)/shard_map/all_to_all | solution.py:242
  69.6 0.8 copy-start.2
  75.5 16.4 %all-to-all-start.1 = ((f32[16,1,512]{2,1,0:T(1,128)}), f32[16,1,512]{2,1,0:T(1,128)S(1)}, u32[]{:S(2)}, u32[]{:S(2)}) async-start(f32[16,1,512]{2,1,0:T(1,128)} %broadcast_in_dim.17), calls=%async_computation.1 | async-start | bytes 65536 | tf_op jit(solution)/shard_map/all_to_all | solution.py:227
  79.0 18.3 %collective-permute-start = (bf16[512,512]{1,0:T(8,128)(2,1)}, bf16[512,512]{1,0:T(8,128)(2,1)S(1)}, u32[]{:S(2)}, u32[]{:S(2)}) collective-permute-start(bf16[512,512]{1,0:T(8,128)(2,1)} %shard_map.68.own), channel_id=1, source_target_pairs={{0,1},{1,2},{2,3},{3,4},{4,5},{5,6},{6,7},{7,8},{8,9},{9,10},{10,1... | collective-permute-start | bytes 1572872 | tf_op jit(solution)/shard_map/ppermute | solution.py:231
  82.8 16.1 %collective-permute-start.1 = (bf16[512,512]{1,0:T(8,128)(2,1)}, bf16[512,512]{1,0:T(8,128)(2,1)S(1)}, u32[]{:S(2)}, u32[]{:S(2)}) collective-permute-start(bf16[512,512]{1,0:T(8,128)(2,1)} %shard_map.68.own), channel_id=1, source_target_pairs={{0,15},{1,0},{2,1},{3,2},{4,3},{5,4},{6,5},{7,6},{8,7},{9,8},{10,9... | collective-permute-start | bytes 1572872 | tf_op jit(solution)/shard_map/ppermute | solution.py:231
  97.3 1.5 copy-start.3
  98.9 0.8 copy-start.4
  105.2 53.1 %collective-permute-start.2 = (bf16[4,3,64,512]{3,2,1,0:T(8,128)(2,1)}, bf16[4,3,64,512]{3,2,1,0:T(8,128)(2,1)S(1)}, u32[]{:S(2)}, u32[]{:S(2)}) collective-permute-start(bf16[4,3,64,512]{3,2,1,0:T(8,128)(2,1)} %get-tuple-element.23), channel_id=1, source_target_pairs={{0,16},{16,0},{1,17},{17,1},{2,18},{18,2},{3,19},{19,3},{4,20},{20... | collective-permute-start | bytes 2359304 | tf_op jit(solution)/shard_map/ppermute | solution.py:235
  108.1 19.1 %collective-permute-start.3 = (bf16[256,512]{1,0:T(8,128)(2,1)S(1)}, bf16[256,512]{1,0:T(8,128)(2,1)S(1)}, u32[]{:S(2)}, u32[]{:S(2)}) collective-permute-start(bf16[256,512]{1,0:T(8,128)(2,1)S(1)} %slice.8), channel_id=1, source_target_pairs={{0,1},{1,2},{2,3},{3,4},{4,5},{5,6},{6,7},{7,8},{8,9},{9,10},{10,1... | collective-permute-start | bytes 786440 | tf_op jit(solution)/shard_map/ppermute | solution.py:231
  112.5 14.8 %collective-permute-start.4 = (bf16[256,512]{1,0:T(8,128)(2,1)S(1)}, bf16[256,512]{1,0:T(8,128)(2,1)S(1)}, u32[]{:S(2)}, u32[]{:S(2)}) collective-permute-start(bf16[256,512]{1,0:T(8,128)(2,1)S(1)} %slice.9), channel_id=1, source_target_pairs={{0,15},{1,0},{2,1},{3,2},{4,3},{5,4},{6,5},{7,6},{8,7},{9,8},{10,9... | collective-permute-start | bytes 786440 | tf_op jit(solution)/shard_map/ppermute | solution.py:231
  127.2 0.7 copy-start.6
  127.9 0.7 copy-start.7
  134.5 23.7 %all-to-all-start.2 = ((f32[16,1,512]{2,1,0:T(1,128)}), f32[16,1,512]{2,1,0:T(1,128)S(1)}, u32[]{:S(2)}, u32[]{:S(2)}) async-start(f32[16,1,512]{2,1,0:T(1,128)} %broadcast_in_dim.19), calls=%async_computation.2 | async-start | bytes 65536 | tf_op jit(solution)/shard_map/all_to_all | solution.py:227
  148.9 9.3 %collective-permute-start.5 = (bf16[2,2,64,512]{3,2,1,0:T(8,128)(2,1)}, bf16[2,2,64,512]{3,2,1,0:T(8,128)(2,1)S(1)}, u32[]{:S(2)}, u32[]{:S(2)}) collective-permute-start(bf16[2,2,64,512]{3,2,1,0:T(8,128)(2,1)} %get-tuple-element.25), channel_id=1, source_target_pairs={{0,16},{16,0},{1,17},{17,1},{2,18},{18,2},{3,19},{19,3},{4,20},{20... | collective-permute-start | bytes 786440 | tf_op jit(solution)/shard_map/ppermute | solution.py:235
  158.3 0.7 copy-start.9
  158.3 1.0 copy-start.8
  163.7 5.4 %copy-start.1 = (bf16[512,512]{1,0:T(8,128)(2,1)S(1)}, bf16[512,512]{1,0:T(8,128)(2,1)}, u32[]{:S(2)}) copy-start(bf16[512,512]{1,0:T(8,128)(2,1)} %x.1) | copy-start | bytes 1572868
  163.7 5.4 %copy-start.5 = (f32[512,512]{1,0:T(8,128)S(1)}, f32[512,512]{1,0:T(8,128)}, u32[]{:S(2)}) copy-start(f32[512,512]{1,0:T(8,128)} %get-tuple-element.29) | copy-start | bytes 3145732
  163.7 32.6 %all-to-all-start.3 = ((bf16[32,32,512]{2,1,0:T(8,128)(2,1)}), bf16[32,32,512]{2,1,0:T(8,128)(2,1)S(1)}, u32[]{:S(2)}, u32[]{:S(2)}) async-start(bf16[32,32,512]{2,1,0:T(8,128)(2,1)} %bitcast.9), calls=%async_computation.3 | async-start | bytes 2097152 | tf_op jit(solution)/shard_map/all_to_all | solution.py:276

commit v3 on v0

v3 whole, which is shorter than its diff:
```python
import jax
import jax.numpy as jnp
from jax import lax
from jax.experimental import pallas as pl
from jax.experimental.pallas import tpu as pltpu
from jax.sharding import Mesh, PartitionSpec as P


D = 8192
EPS = 1e-06
ROWS = 512
FEAT = 512
COLS = 128
FAR = 4
NEAR = 4
TP = FAR * NEAR
CHIPS = 32
HALF = FAR * COLS // 2
Z = ("zh", "zl")
TRANSPOSED = (((0,), (0,)), ((), ()))


def call(body, inputs, shapes, flops, moved, outputs=None, scratch=(), aliases=None):
    vmem = pl.BlockSpec(memory_space=pltpu.VMEM)
    specs = [pl.BlockSpec(memory_space=pltpu.SMEM)] + [vmem if s is None else s for s in inputs]
    return pl.pallas_call(
        body,
        in_specs=specs,
        out_specs=outputs if outputs is not None else jax.tree.map(lambda _: vmem, shapes),
        out_shape=shapes,
        scratch_shapes=scratch,
        input_output_aliases=aliases or {},
        cost_estimate=pl.CostEstimate(flops=flops, bytes_accessed=moved, transcendentals=0),
    )


def place_kernel(where, received, onehot, out):
    picked = lax.dot_general(received[...], onehot[...], TRANSPOSED, preferred_element_type=jnp.float32)
    out[...] = picked.astype(jnp.bfloat16)


def place(where, received, onehot):
    shape = jax.ShapeDtypeStruct((COLS, ROWS), jnp.bfloat16)
    return call(place_kernel, [None] * 2, shape, 2 * ROWS * ROWS * COLS, ROWS * ROWS * 3)(where, received, onehot)


def gradient(where, total, blocks, w):
    for ref, at, shift, far in blocks:
        owner = far * NEAR + lax.rem(where[0] + shift, NEAR)
        rows = w[pl.ds(pl.multiple_of(owner * COLS, COLS), COLS), :]
        term = lax.dot_general(ref[at : at + COLS, :], rows, TRANSPOSED, preferred_element_type=jnp.float32)
        total = term if total is None else total + term
    return total


def grad_own_kernel(where, own, w, out):
    out[...] = gradient(where, None, [(own, COLS * far, 0, far) for far in range(FAR)], w)


def grad_own(where, own, w_kv):
    shape = jax.ShapeDtypeStruct((ROWS, FEAT), jnp.float32)
    flops = 2 * FAR * ROWS * FEAT * COLS
    return call(grad_own_kernel, [None] * 2, shape, flops, 14 * ROWS * FEAT)(where, own, w_kv)


def grad_rest_kernel(where, behind, ahead, far_a, far_b, w, before, x, gain, out, products):
    blocks = [(behind, COLS * far, NEAR - 1, far) for far in range(FAR)]
    blocks += [(ahead, COLS * far, 1, far) for far in range(FAR)]
    blocks += [(far_a, COLS * far, 2, far) for far in range(2)]
    blocks += [(far_b, COLS * far, 2, 2 + far) for far in range(2)]
    total = gradient(where, before[...], blocks, w)
    out[...] = total
    part = x[...].astype(jnp.float32) * gain[...].astype(jnp.float32) * total
    lanes = part[:, :COLS]
    for i in range(1, FEAT // COLS):
        lanes = lanes + part[:, COLS * i : COLS * (i + 1)]
    products[...] = jnp.sum(lanes.T, axis=0, keepdims=True)


def grad_rest(where, behind, ahead, far_a, far_b, w_kv, before, x, gain):
    shapes = [jax.ShapeDtypeStruct((ROWS, FEAT), jnp.float32), jax.ShapeDtypeStruct((1, ROWS), jnp.float32)]
    flops = 6 * FAR * ROWS * FEAT * COLS
    return call(grad_rest_kernel, [None] * 8, shapes, flops, 24 * ROWS * FEAT)(
        where, behind, ahead, far_a, far_b, w_kv, before, x, gain
    )


def split_rows(where, term):
    first = where[1] == 0
    low = jnp.concatenate([term[0:32], term[64:96]], axis=0)
    high = jnp.concatenate([term[32:64], term[96:128]], axis=0)
    return jnp.where(first, low, high), jnp.where(first, high, low).astype(jnp.bfloat16)


def weight_near_kernel(where, own, behind, ahead, normed, keep, send):
    for group, ref in enumerate((own, behind, ahead)):
        for far in range(FAR):
            term = jnp.dot(ref[COLS * far : COLS * (far + 1), :], normed[...], preferred_element_type=jnp.float32)
            kept, sent = split_rows(where, term)
            keep[far, group] = kept
            send[far, group] = sent


def weight_near(where, own, behind, ahead, normed):
    shapes = [jax.ShapeDtypeStruct((FAR, 3, COLS // 2, FEAT), kind) for kind in (jnp.float32, jnp.bfloat16)]
    flops = 6 * FAR * ROWS * FEAT * COLS
    return call(weight_near_kernel, [None] * 4, shapes, flops, 18 * ROWS * FEAT)(where, own, behind, ahead, normed)


def weight_far_kernel(where, far_a, far_b, normed, keep, send):
    for far in range(FAR):
        ref, at = (far_a, far_b)[far // 2], COLS * (far % 2)
        term = jnp.dot(ref[at : at + COLS, :], normed[...], preferred_element_type=jnp.float32)
        kept, sent = split_rows(where, term)
        keep[far] = kept
        send[far] = sent


def weight_far(where, far_a, far_b, normed):
    shapes = [jax.ShapeDtypeStruct((FAR, COLS // 2, FEAT), kind) for kind in (jnp.float32, jnp.bfloat16)]
    flops = 2 * FAR * ROWS * FEAT * COLS
    return call(weight_far_kernel, [None] * 3, shapes, flops, 8 * ROWS * FEAT)(where, far_a, far_b, normed)


def combine_near_kernel(where, keep, taken, out, total, sems):
    copies = []
    for far in range(FAR):
        for group, shift in enumerate((0, NEAR - 1, 1)):
            total[far, group] = (keep[far, group] + taken[far, group].astype(jnp.float32)).astype(jnp.bfloat16)
            to = out.at[far, lax.rem(where[0] + shift, NEAR)]
            copies.append(pltpu.make_async_copy(total.at[far, group], to, sems.at[far, group]))
            copies[-1].start()
    for copy in copies:
        copy.wait()


def combine_near(where, keep, taken):
    return call(
        combine_near_kernel,
        [None] * 2,
        jax.ShapeDtypeStruct((FAR, NEAR, COLS // 2, FEAT), jnp.bfloat16),
        3 * FAR * COLS * FEAT,
        12 * ROWS * FEAT,
        outputs=pl.BlockSpec(memory_space=pltpu.HBM),
        scratch=[pltpu.VMEM((FAR, 3, COLS // 2, FEAT), jnp.bfloat16), pltpu.SemaphoreType.DMA((FAR, 3))],
    )(where, keep, taken)


def combine_far_kernel(where, keep, taken, placed, out, total, sems):
    copies = []
    for far in range(FAR):
        total[far] = (keep[far] + taken[far].astype(jnp.float32)).astype(jnp.bfloat16)
        to = out.at[far, lax.rem(where[0] + 2, NEAR)]
        copies.append(pltpu.make_async_copy(total.at[far], to, sems.at[far]))
        copies[-1].start()
    for copy in copies:
        copy.wait()


def combine_far(where, keep, taken, placed):
    hbm = pl.BlockSpec(memory_space=pltpu.HBM)
    return call(
        combine_far_kernel,
        [None, None, hbm],
        jax.ShapeDtypeStruct(placed.shape, placed.dtype),
        FAR * COLS * FEAT,
        5 * ROWS * FEAT,
        outputs=hbm,
        scratch=[pltpu.VMEM((FAR, COLS // 2, FEAT), jnp.bfloat16), pltpu.SemaphoreType.DMA((FAR,))],
        aliases={3: 0},
    )(where, keep, taken, placed)


def tensor_sum(vector):
    spread = jnp.broadcast_to(vector.reshape(1, ROWS), (TP, ROWS))
    return jnp.sum(lax.all_to_all(spread, Z, split_axis=0, concat_axis=0, tiled=True), axis=0)


def hop(array, step):
    return lax.ppermute(array, Z, [(i, (i + step) % TP) for i in range(TP)])


def swap(array):
    return lax.ppermute(array, "core", [(0, 1), (1, 0)])


def ladder(vector):
    for distance in (8, 4, 2, 1):
        vector = vector + hop(vector, distance)
    return vector


def step(layer_input, gain, w_kv, d_kv, destination):
    where = jnp.stack([lax.axis_index("zl"), lax.axis_index("core")]).astype(jnp.int32)
    received = lax.all_to_all(d_kv, ("chip", "core"), split_axis=0, concat_axis=0, tiled=True)

    ids = jnp.arange(ROWS, dtype=jnp.int32)
    same = (destination[:, None] == destination[None, :]) & (ids[:, None] < ids[None, :])
    slot_rank = jnp.sum(same.astype(jnp.int32), axis=0)
    position = jnp.where(destination >= 0, destination * 8 + slot_rank, -1)
    onehot = (ids[:, None] == position[None, :]).astype(jnp.bfloat16)

    values = layer_input.astype(jnp.float32)
    gain_wide = gain.astype(jnp.float32)
    squares = jnp.sum(values * values, axis=1)
    onehot, squares, where = lax.optimization_barrier((onehot, squares, where))

    block = place(where, received, onehot)
    copies = jnp.broadcast_to(block[None], (FAR, COLS, ROWS))
    own = lax.all_to_all(copies, "zh", split_axis=0, concat_axis=0, tiled=True).reshape(FAR * COLS, ROWS)
    own, squares = lax.optimization_barrier((own, squares))
    behind = hop(own, 1)
    ahead = hop(own, -1)
    inverse = lax.rsqrt(tensor_sum(squares) / D + EPS)
    normed = (values * inverse[:, None] * gain_wide).astype(jnp.bfloat16)
    far_a = hop(behind[:HALF], 1)
    far_b = hop(ahead[HALF:], -1)

    grad = grad_own(where, own, w_kv)
    keep_near, send_near = weight_near(where, own, behind, ahead, normed)
    taken_near = swap(send_near)
    placed = combine_near(where, keep_near, taken_near)
    keep_far, send_far = weight_far(where, far_a, far_b, normed)
    taken_far = swap(send_far)
    pair = combine_far(where, keep_far, taken_far, placed)
    pair, x, inverse = lax.optimization_barrier((pair, layer_input, inverse))
    parts = lax.all_to_all(pair.reshape(CHIPS, 32, FEAT), "chip", split_axis=0, concat_axis=0, tiled=True)
    grad_weight = jnp.sum(parts.astype(jnp.float32), axis=0)

    dnormed, products = grad_rest(where, behind, ahead, far_a, far_b, w_kv, grad, x, gain[None, :])
    mean_dot = ladder(products[0]) / D
    along = x.astype(jnp.float32) * (inverse**3 * mean_dot)[:, None]
    grad_x = (inverse[:, None] * gain_wide * dnormed - along).astype(jnp.bfloat16)
    return (grad_x, grad_weight)


def solution(mesh):
    fine = Mesh(mesh.devices.reshape(CHIPS, 2, FAR, NEAR), ("chip", "core", "zh", "zl"))
    dp = ("chip", "core")
    return jax.shard_map(
        step,
        mesh=fine,
        in_specs=(P(dp, Z), P(Z), P(None, Z), P(dp, Z), P(dp)),
        out_specs=(P(dp, Z), P(dp, Z)),
        check_vma=False,
    )
```

time: 316 us -> 191 us (0.60)
  the two profiles are of different devices: /device:TPU:16 before, /device:TPU:2 now
where the time goes in v3:
time: 191 us; the launch traced here: 190 us
  starting transfers between devices  82.4 us (43%)
  blocking collectives  34.5 us (18%)
  waiting for transfers between devices  32.9 us (17%)
  Pallas kernels  21.8 us (11%)
  other arithmetic  9.24 us (5%)
  local copies, waits for them, and re-layouts  7.95 us (4%)
    ppermute x8, starting transfers between devices, hop(): return lax.ppermute(array, Z, [(i, (i + step) % TP) for i in range(TP)])  42.2 us
    all_to_all x1, blocking collectives, step(): lax.all_to_all(copies, 'zh', split_axis=0, concat_axis=0, tiled=True)  34.5 us
    ppermute x8, waiting for transfers between devices, hop(): return lax.ppermute(array, Z, [(i, (i + step) % TP) for i in range(TP)])  21.5 us
    all_to_all x1, starting transfers between devices, step(): lax.all_to_all(d_kv, ('chip', 'core'), split_axis=0, concat_axis=0, tiled...  17.4 us
    all_to_all x1, starting transfers between devices, tensor_sum(): lax.all_to_all(spread, Z, split_axis=0, concat_axis=0, tiled=True)  13.9 us
    all_to_all x1, waiting for transfers between devices, tensor_sum(): lax.all_to_all(spread, Z, split_axis=0, concat_axis=0, tiled=True)  5.86 us
    all_to_all x1, waiting for transfers between devices, step(): lax.all_to_all(d_kv, ('chip', 'core'), split_axis=0, concat_axis=0, tiled...  5.52 us
    pallas_call x1, Pallas kernels, grad_rest(): call(grad_rest_kernel, [None] * 8, shapes, flops, 24 * ROWS * FEAT)  5.32 us
  transfers between devices with their start and end apart: 13, of which 10 were waited for; matrix products, arithmetic and copies ran while one was open for 6% of the time, Pallas kernels for 7%

profile of v3, /device:TPU:2, one launch (start us, length us, event | category | flops | bytes accessed | tf_op | source)
XLA Modules:
  0.0 189.6 jit_solution(15289868942671276378)
XLA Ops:
  0.6 0.0 copy-start
  0.6 0.0 copy-start.10
  0.7 17.4 %all-to-all-start = ((bf16[64,8,128]{2,1,0:T(8,128)(2,1)}), bf16[64,8,128]{2,1,0:T(8,128)(2,1)S(1)}, u32[]{:S(2)}, u32[]{:S(2)}) async-start(bf16[64,8,128]{2,1,0:T(8,128)(2,1)} %bitcast.13), calls=%async_computation | async-start | bytes 262144 | tf_op jit(solution)/shard_map/all_to_all | solution.py:195
  18.0 0.9 convert_reduce_fusion.1
  18.9 0.7 add_select_fusion
  19.6 1.2 fusion
  20.9 0.7 pad_add_fusion.where
  21.5 0.9 fusion.3.onehot
  22.5 5.5 %all-to-all-done = bf16[64,8,128]{2,1,0:T(8,128)(2,1)S(1)} async-done(((bf16[64,8,128]{2,1,0:T(8,128)(2,1)}), bf16[64,8,128]{2,1,0:T(8,128)(2,1)S(1)}, u32[]{:S(2)}, u32[]{:S(2)}) %all-to-all-start) | async-done | bytes 131104 | tf_op jit(solution)/shard_map/all_to_all | solution.py:195
  28.0 0.0 copy-start.8
  28.0 0.7 copy-done.8
  28.6 2.0 %shard_map.68 = bf16[128,512]{1,0:T(8,128)(2,1)} custom-call(s32[2]{0:T(128)} %pad_add_fusion.where, bf16[512,128]{1,0:T(8,128)(2,1)} %bitcast.12, bf16[512,512]{1,0:T(8,128)(2,1)} %fusion.3.onehot), custom_call_target="tpu_custom_call" | custom-call | flops 67108864 | bytes 786432 | tf_op jit(solution)/shard_map/pallas_call | solution.py:44
  30.7 0.9 broadcast_in_dim.11
  31.6 34.5 %all_to_all.27 = bf16[4,128,512]{2,1,0:T(8,128)(2,1)S(1)} all-to-all(bf16[4,128,512]{2,1,0:T(8,128)(2,1)S(1)} %broadcast_in_dim.11), channel_id=1, replica_groups=mesh['chip'=32,'core'=2,'zh'=4,'zl'=4] {'zh'}, dimensions={0} | all-to-all | bytes 1048576 | tf_op jit(solution)/shard_map/all_to_all | solution.py:210
  66.1 0.7 broadcast_in_dim.12
  66.8 13.9 %all-to-all-start.2 = ((f32[16,1,512]{2,1,0:T(1,128)}), f32[16,1,512]{2,1,0:T(1,128)S(1)}, u32[]{:S(2)}, u32[]{:S(2)}) async-start(f32[16,1,512]{2,1,0:T(1,128)} %broadcast_in_dim.12), calls=%async_computation.2 | async-start | bytes 65536 | tf_op jit(solution)/shard_map/all_to_all | solution.py:176
  80.6 3.8 %collective-permute-start = (bf16[512,512]{1,0:T(8,128)(2,1)S(1)}, bf16[512,512]{1,0:T(8,128)(2,1)S(1)}, u32[]{:S(2)}, u32[]{:S(2)}) collective-permute-start(bf16[512,512]{1,0:T(8,128)(2,1)S(1)} %bitcast.8), channel_id=1, source_target_pairs={{0,1},{1,2},{2,3},{3,4},{4,5},{5,6},{6,7},{7,8},{8,9},{9,10},{10,1... | collective-permute-start | bytes 1572872 | tf_op jit(solution)/shard_map/ppermute | solution.py:180
  84.5 3.2 %collective-permute-start.2 = (bf16[512,512]{1,0:T(8,128)(2,1)S(1)}, bf16[512,512]{1,0:T(8,128)(2,1)S(1)}, u32[]{:S(2)}, u32[]{:S(2)}) collective-permute-start(bf16[512,512]{1,0:T(8,128)(2,1)S(1)} %bitcast.9), channel_id=1, source_target_pairs={{0,15},{1,0},{2,1},{3,2},{4,3},{5,4},{6,5},{7,6},{8,7},{9,8},{10,9... | collective-permute-start | bytes 1572872 | tf_op jit(solution)/shard_map/ppermute | solution.py:180
  87.7 0.0 copy-done.10
  87.7 5.9 %all-to-all-done.2 = f32[16,1,512]{2,1,0:T(1,128)S(1)} async-done(((f32[16,1,512]{2,1,0:T(1,128)}), f32[16,1,512]{2,1,0:T(1,128)S(1)}, u32[]{:S(2)}, u32[]{:S(2)}) %all-to-all-start.2) | async-done | bytes 32800 | tf_op jit(solution)/shard_map/all_to_all | solution.py:176
  93.6 0.0 copy-done
  93.6 1.0 fusion.2.normed
  94.6 3.1 %collective-permute-done.behind = bf16[512,512]{1,0:T(8,128)(2,1)S(1)} collective-permute-done((bf16[512,512]{1,0:T(8,128)(2,1)S(1)}, bf16[512,512]{1,0:T(8,128)(2,1)S(1)}, u32[]{:S(2)}, u32[]{:S(2)}) %collective-permute-start) | collective-permute-done | bytes 524320 | tf_op jit(solution)/shard_map/ppermute | solution.py:180
  97.7 1.3 collective-permute-done.2.ahead
  99.1 0.0 copy-done.2
  99.1 0.0 copy-done.3
  99.1 0.8 copy-done.4
  99.9 3.9 %shard_map.70 = (f32[4,3,64,512]{3,2,1,0:T(8,128)}, bf16[4,3,64,512]{3,2,1,0:T(8,128)(2,1)}) custom-call(s32[2]{0:T(128)} %pad_add_fusion.where, bf16[512,512]{1,0:T(8,128)(2,1)} %bitcast.10, bf16[512,512]{1,0:T(8,128)(2,1)} %copy-done.3, bf16[512,512]{1,0:T(8,128)(2,1)} %copy-done.4, bf16[512,512]{1,0:T(8,128)(2,1)} %fusion.2.normed), custom_call_target="tpu_custom_call" | custom-call | flops 805306368 | bytes 4718592 | tf_op jit(solution)/shard_map/pallas_call | solution.py:107
  103.8 1.9 %collective-permute-start.5 = (bf16[4,3,64,512]{3,2,1,0:T(8,128)(2,1)}, bf16[4,3,64,512]{3,2,1,0:T(8,128)(2,1)S(1)}, u32[]{:S(2)}, u32[]{:S(2)}) collective-permute-start(bf16[4,3,64,512]{3,2,1,0:T(8,128)(2,1)} %get-tuple-element.24), channel_id=1, source_target_pairs={{0,16},{16,0},{1,17},{17,1},{2,18},{18,2},{3,19},{19,3},{4,20},{20... | collective-permute-start | bytes 2359304 | tf_op jit(solution)/shard_map/ppermute | solution.py:184
  105.7 1.0 slice.8
  106.7 3.4 %collective-permute-start.1 = (bf16[256,512]{1,0:T(8,128)(2,1)S(1)}, bf16[256,512]{1,0:T(8,128)(2,1)S(1)}, u32[]{:S(2)}, u32[]{:S(2)}) collective-permute-start(bf16[256,512]{1,0:T(8,128)(2,1)S(1)} %slice.8), channel_id=1, source_target_pairs={{0,1},{1,2},{2,3},{3,4},{4,5},{5,6},{6,7},{7,8},{8,9},{9,10},{10,1... | collective-permute-start | bytes 786440 | tf_op jit(solution)/shard_map/ppermute | solution.py:180
  110.1 1.0 slice.9
  111.1 3.6 %collective-permute-start.3 = (bf16[256,512]{1,0:T(8,128)(2,1)S(1)}, bf16[256,512]{1,0:T(8,128)(2,1)S(1)}, u32[]{:S(2)}, u32[]{:S(2)}) collective-permute-start(bf16[256,512]{1,0:T(8,128)(2,1)S(1)} %slice.9), channel_id=1, source_target_pairs={{0,15},{1,0},{2,1},{3,2},{4,3},{5,4},{6,5},{7,6},{8,7},{9,8},{10,9... | collective-permute-start | bytes 786440 | tf_op jit(solution)/shard_map/ppermute | solution.py:180
  114.7 3.8 %collective-permute-done.1.far_a = bf16[256,512]{1,0:T(8,128)(2,1)S(1)} collective-permute-done((bf16[256,512]{1,0:T(8,128)(2,1)S(1)}, bf16[256,512]{1,0:T(8,128)(2,1)S(1)}, u32[]{:S(2)}, u32[]{:S(2)}) %collective-permute-start.1) | collective-permute-done | bytes 262176 | tf_op jit(solution)/shard_map/ppermute | solution.py:180
  118.5 3.4 %collective-permute-done.3.far_b = bf16[256,512]{1,0:T(8,128)(2,1)S(1)} collective-permute-done((bf16[256,512]{1,0:T(8,128)(2,1)S(1)}, bf16[256,512]{1,0:T(8,128)(2,1)S(1)}, u32[]{:S(2)}, u32[]{:S(2)}) %collective-permute-start.3) | collective-permute-done | bytes 262176 | tf_op jit(solution)/shard_map/ppermute | solution.py:180
  122.0 0.0 copy-done.5
  122.0 0.7 copy-done.6
  122.7 2.6 %shard_map.69 = (f32[4,64,512]{2,1,0:T(8,128)}, bf16[4,64,512]{2,1,0:T(8,128)(2,1)}) custom-call(s32[2]{0:T(128)} %pad_add_fusion.where, bf16[256,512]{1,0:T(8,128)(2,1)} %copy-done.5, bf16[256,512]{1,0:T(8,128)(2,1)} %copy-done.6, bf16[512,512]{1,0:T(8,128)(2,1)} %fusion.2.normed), custom_call_target="tpu_custom_call" | custom-call | flops 268435456 | bytes 2097152 | tf_op jit(solution)/shard_map/pallas_call | solution.py:122
  125.2 1.9 %collective-permute-start.4 = (bf16[4,64,512]{2,1,0:T(8,128)(2,1)}, bf16[4,64,512]{2,1,0:T(8,128)(2,1)S(1)}, u32[]{:S(2)}, u32[]{:S(2)}) collective-permute-start(bf16[4,64,512]{2,1,0:T(8,128)(2,1)} %get-tuple-element.22), channel_id=1, source_target_pairs={{0,16},{16,0},{1,17},{17,1},{2,18},{18,2},{3,19},{19,3},{4,20},{20... | collective-permute-start | bytes 786440 | tf_op jit(solution)/shard_map/ppermute | solution.py:184
  127.1 0.0 collective-permute-done.5.taken
  127.2 0.0 copy-start.7
  127.2 0.9 copy-done.7
  128.1 2.6 %shard_map.71.placed = bf16[4,4,64,512]{3,2,1,0:T(8,128)(2,1)} custom-call(s32[2]{0:T(128)} %pad_add_fusion.where, f32[4,3,64,512]{3,2,1,0:T(8,128)} %get-tuple-element.23.keep, bf16[4,3,64,512]{3,2,1,0:T(8,128)(2,1)} %copy-done.7), custom_call_target="tpu_custom_call" | custom-call | flops 786432 | bytes 3145728 | tf_op jit(solution)/shard_map/pallas_call | solution.py:138
  130.7 0.0 collective-permute-done.4.taken
  130.7 0.0 copy-start.9
  130.7 0.7 copy-done.9
  131.4 1.9 shard_map.72
  133.3 5.2 %all-to-all-start.3 = ((bf16[32,32,512]{2,1,0:T(8,128)(2,1)}), bf16[32,32,512]{2,1,0:T(8,128)(2,1)S(1)}, u32[]{:S(2)}, u32[]{:S(2)}) async-start(bf16[32,32,512]{2,1,0:T(8,128)(2,1)} %bitcast.7), calls=%async_computation.3 | async-start | bytes 2097152 | tf_op jit(solution)/shard_map/all_to_all | solution.py:227
  138.5 0.6 broadcast_in_dim.13.gain
  139.1 3.5 %shard_map.73.before = f32[512,512]{1,0:T(8,128)} custom-call(s32[2]{0:T(128)} %pad_add_fusion.where, bf16[512,512]{1,0:T(8,128)(2,1)} %bitcast.11, bf16[2048,512]{1,0:T(8,128)(2,1)} %w.3), custom_call_target="tpu_custom_call" | custom-call | flops 268435456 | bytes 3670016 | tf_op jit(solution)/shard_map/pallas_call | solution.py:63
  142.5 5.3 %shard_map.74 = (f32[512,512]{1,0:T(8,128)}, f32[1,512]{1,0:T(1,128)}) custom-call(s32[2]{0:T(128)} %pad_add_fusion.where, bf16[512,512]{1,0:T(8,128)(2,1)} %copy-done.3, bf16[512,512]{1,0:T(8,128)(2,1)} %copy-done.4, bf16[256,512]{1,0:T(8,128)(2,1)} %copy-done.5, bf16[256,512]{1,0:T(8,128)(2,1)} %copy-done.6, bf16[2048,512]{1,0:T(8,128)(2,1)} %w.3, ...), custom_call_target="tpu_custom_call" | custom-call | flops 805306368 | bytes 6291456 | tf_op jit(solution)/shard_map/pallas_call | solution.py:83
  147.8 10.5 %collective-permute-start.6 = (f32[512]{0:T(512)}, f32[512]{0:T(512)S(1)}, u32[]{:S(2)}, u32[]{:S(2)}) collective-permute-start(f32[512]{0:T(512)} %bitcast.14), channel_id=1, source_target_pairs={{0,8},{1,9},{2,10},{3,11},{4,12},{5,13},{6,14},{7,15},{8,0},{9,1},... | collective-permute-start | bytes 6152 | tf_op jit(solution)/shard_map/ppermute | solution.py:180
  158.3 3.9 %collective-permute-done.6 = f32[512]{0:T(512)S(1)} collective-permute-done((f32[512]{0:T(512)}, f32[512]{0:T(512)S(1)}, u32[]{:S(2)}, u32[]{:S(2)}) %collective-permute-start.6) | collective-permute-done | bytes 2080 | tf_op jit(solution)/shard_map/ppermute | solution.py:180
  162.2 0.7 add.28
  162.9 7.0 %collective-permute-start.7 = (f32[512]{0:T(512)S(1)}, f32[512]{0:T(512)S(1)}, u32[]{:S(2)}, u32[]{:S(2)}) collective-permute-start(f32[512]{0:T(512)S(1)} %add.28), channel_id=1, source_target_pairs={{0,4},{1,5},{2,6},{3,7},{4,8},{5,9},{6,10},{7,11},{8,12},{9,13},{1... | collective-permute-start | bytes 6152 | tf_op jit(solution)/shard_map/ppermute | solution.py:180
  169.9 2.4 %collective-permute-done.7 = f32[512]{0:T(512)S(1)} collective-permute-done((f32[512]{0:T(512)S(1)}, f32[512]{0:T(512)S(1)}, u32[]{:S(2)}, u32[]{:S(2)}) %collective-permute-start.7) | collective-permute-done | bytes 2080 | tf_op jit(solution)/shard_map/ppermute | solution.py:180
  172.3 5.9 %collective-permute-start.8 = (f32[512]{0:T(512)S(1)}, f32[512]{0:T(512)S(1)}, u32[]{:S(2)}, u32[]{:S(2)}) collective-permute-start(f32[512]{0:T(512)S(1)} %add.29), channel_id=1, source_target_pairs={{0,2},{1,3},{2,4},{3,5},{4,6},{5,7},{6,8},{7,9},{8,10},{9,11},{10,... | collective-permute-start | bytes 6152 | tf_op jit(solution)/shard_map/ppermute | solution.py:180
  178.2 1.7 collective-permute-done.8
  179.9 4.8 %collective-permute-start.9 = (f32[512]{0:T(512)S(1)}, f32[512]{0:T(512)S(1)}, u32[]{:S(2)}, u32[]{:S(2)}) collective-permute-start(f32[512]{0:T(512)S(1)} %add.30), channel_id=1, source_target_pairs={{0,1},{1,2},{2,3},{3,4},{4,5},{5,6},{6,7},{7,8},{8,9},{9,10},{10,1... | collective-permute-start | bytes 6152 | tf_op jit(solution)/shard_map/ppermute | solution.py:180
  184.6 1.9 %collective-permute-done.9 = f32[512]{0:T(512)S(1)} collective-permute-done((f32[512]{0:T(512)S(1)}, f32[512]{0:T(512)S(1)}, u32[]{:S(2)}, u32[]{:S(2)}) %collective-permute-start.9) | collective-permute-done | bytes 2080 | tf_op jit(solution)/shard_map/ppermute | solution.py:180
  186.6 0.0 copy-done.1
  186.6 2.3 %subtract_convert_fusion = bf16[512,512]{1,0:T(8,128)(2,1)} fusion(bf16[512,512]{1,0:T(8,128)(2,1)S(1)} %copy-done.1, f32[512,512]{1,0:T(8,128)} %get-tuple-element.27, f32[512]{0:T(512)S(1)} %fusion.5, f32[512]{0:T(512)S(1)} %add_rsqrt_fusion, f32[512]{0:T(512)S(1)} %convert_element_type.27), kind=kLoop, calls=%fused_computation.6 | loop fusion | flops 1572864 | bytes 2103296 | tf_op jit(solution)/shard_map/convert_element_type | solution.py:233
  188.8 0.0 all-to-all-done.3
  188.8 0.8 convert_reduce_fusion
  (12 shorter events, 0.1 us)
Async XLA Ops:
  0.6 93.0 %copy-start = (bf16[512,512]{1,0:T(8,128)(2,1)S(1)}, bf16[512,512]{1,0:T(8,128)(2,1)}, u32[]{:S(2)}) copy-start(bf16[512,512]{1,0:T(8,128)(2,1)} %x) | copy-start | bytes 1572868
  0.6 87.1 %copy-start.10 = (bf16[512]{0:T(512)(128)(2,1)S(1)}, bf16[512]{0:T(512)(128)(2,1)}, u32[]{:S(2)}) copy-start(bf16[512]{0:T(512)(128)(2,1)} %param.6) | copy-start | bytes 3076
  0.7 27.3 %all-to-all-start = ((bf16[64,8,128]{2,1,0:T(8,128)(2,1)}), bf16[64,8,128]{2,1,0:T(8,128)(2,1)S(1)}, u32[]{:S(2)}, u32[]{:S(2)}) async-start(bf16[64,8,128]{2,1,0:T(8,128)(2,1)} %bitcast.13), calls=%async_computation | async-start | bytes 262144 | tf_op jit(solution)/shard_map/all_to_all | solution.py:195
  28.0 0.7 copy-start.8
  66.1 33.0 %copy-start.2 = (bf16[4,128,512]{2,1,0:T(8,128)(2,1)}, bf16[4,128,512]{2,1,0:T(8,128)(2,1)S(1)}, u32[]{:S(2)}) copy-start(bf16[4,128,512]{2,1,0:T(8,128)(2,1)S(1)} %all_to_all.27) | copy-start | bytes 1572868
  66.8 26.8 %all-to-all-start.2 = ((f32[16,1,512]{2,1,0:T(1,128)}), f32[16,1,512]{2,1,0:T(1,128)S(1)}, u32[]{:S(2)}, u32[]{:S(2)}) async-start(f32[16,1,512]{2,1,0:T(1,128)} %broadcast_in_dim.12), calls=%async_computation.2 | async-start | bytes 65536 | tf_op jit(solution)/shard_map/all_to_all | solution.py:176
  80.6 17.1 %collective-permute-start = (bf16[512,512]{1,0:T(8,128)(2,1)S(1)}, bf16[512,512]{1,0:T(8,128)(2,1)S(1)}, u32[]{:S(2)}, u32[]{:S(2)}) collective-permute-start(bf16[512,512]{1,0:T(8,128)(2,1)S(1)} %bitcast.8), channel_id=1, source_target_pairs={{0,1},{1,2},{2,3},{3,4},{4,5},{5,6},{6,7},{7,8},{8,9},{9,10},{10,1... | collective-permute-start | bytes 1572872 | tf_op jit(solution)/shard_map/ppermute | solution.py:180
  84.5 14.6 %collective-permute-start.2 = (bf16[512,512]{1,0:T(8,128)(2,1)S(1)}, bf16[512,512]{1,0:T(8,128)(2,1)S(1)}, u32[]{:S(2)}, u32[]{:S(2)}) collective-permute-start(bf16[512,512]{1,0:T(8,128)(2,1)S(1)} %bitcast.9), channel_id=1, source_target_pairs={{0,15},{1,0},{2,1},{3,2},{4,3},{5,4},{6,5},{7,6},{8,7},{9,8},{10,9... | collective-permute-start | bytes 1572872 | tf_op jit(solution)/shard_map/ppermute | solution.py:180
  97.7 1.3 copy-start.3
  99.1 0.8 copy-start.4
  103.8 23.3 %collective-permute-start.5 = (bf16[4,3,64,512]{3,2,1,0:T(8,128)(2,1)}, bf16[4,3,64,512]{3,2,1,0:T(8,128)(2,1)S(1)}, u32[]{:S(2)}, u32[]{:S(2)}) collective-permute-start(bf16[4,3,64,512]{3,2,1,0:T(8,128)(2,1)} %get-tuple-element.24), channel_id=1, source_target_pairs={{0,16},{16,0},{1,17},{17,1},{2,18},{18,2},{3,19},{19,3},{4,20},{20... | collective-permute-start | bytes 2359304 | tf_op jit(solution)/shard_map/ppermute | solution.py:184
  106.7 11.8 %collective-permute-start.1 = (bf16[256,512]{1,0:T(8,128)(2,1)S(1)}, bf16[256,512]{1,0:T(8,128)(2,1)S(1)}, u32[]{:S(2)}, u32[]{:S(2)}) collective-permute-start(bf16[256,512]{1,0:T(8,128)(2,1)S(1)} %slice.8), channel_id=1, source_target_pairs={{0,1},{1,2},{2,3},{3,4},{4,5},{5,6},{6,7},{7,8},{8,9},{9,10},{10,1... | collective-permute-start | bytes 786440 | tf_op jit(solution)/shard_map/ppermute | solution.py:180
  111.1 10.8 %collective-permute-start.3 = (bf16[256,512]{1,0:T(8,128)(2,1)S(1)}, bf16[256,512]{1,0:T(8,128)(2,1)S(1)}, u32[]{:S(2)}, u32[]{:S(2)}) collective-permute-start(bf16[256,512]{1,0:T(8,128)(2,1)S(1)} %slice.9), channel_id=1, source_target_pairs={{0,15},{1,0},{2,1},{3,2},{4,3},{5,4},{6,5},{7,6},{8,7},{9,8},{10,9... | collective-permute-start | bytes 786440 | tf_op jit(solution)/shard_map/ppermute | solution.py:180
  118.5 3.4 %copy-start.5 = (bf16[256,512]{1,0:T(8,128)(2,1)}, bf16[256,512]{1,0:T(8,128)(2,1)S(1)}, u32[]{:S(2)}) copy-start(bf16[256,512]{1,0:T(8,128)(2,1)S(1)} %collective-permute-done.1.far_a) | copy-start | bytes 786436
  122.0 0.7 copy-start.6
  125.2 5.5 %collective-permute-start.4 = (bf16[4,64,512]{2,1,0:T(8,128)(2,1)}, bf16[4,64,512]{2,1,0:T(8,128)(2,1)S(1)}, u32[]{:S(2)}, u32[]{:S(2)}) collective-permute-start(bf16[4,64,512]{2,1,0:T(8,128)(2,1)} %get-tuple-element.22), channel_id=1, source_target_pairs={{0,16},{16,0},{1,17},{17,1},{2,18},{18,2},{3,19},{19,3},{4,20},{20... | collective-permute-start | bytes 786440 | tf_op jit(solution)/shard_map/ppermute | solution.py:184
  127.2 0.9 copy-start.7
  130.7 0.7 copy-start.9
  133.3 55.5 %all-to-all-start.3 = ((bf16[32,32,512]{2,1,0:T(8,128)(2,1)}), bf16[32,32,512]{2,1,0:T(8,128)(2,1)S(1)}, u32[]{:S(2)}, u32[]{:S(2)}) async-start(bf16[32,32,512]{2,1,0:T(8,128)(2,1)} %bitcast.7), calls=%async_computation.3 | async-start | bytes 2097152 | tf_op jit(solution)/shard_map/all_to_all | solution.py:227
  142.5 44.0 %copy-start.1 = (bf16[512,512]{1,0:T(8,128)(2,1)S(1)}, bf16[512,512]{1,0:T(8,128)(2,1)}, u32[]{:S(2)}) copy-start(bf16[512,512]{1,0:T(8,128)(2,1)} %x) | copy-start | bytes 1572868
  147.8 14.4 %collective-permute-start.6 = (f32[512]{0:T(512)}, f32[512]{0:T(512)S(1)}, u32[]{:S(2)}, u32[]{:S(2)}) collective-permute-start(f32[512]{0:T(512)} %bitcast.14), channel_id=1, source_target_pairs={{0,8},{1,9},{2,10},{3,11},{4,12},{5,13},{6,14},{7,15},{8,0},{9,1},... | collective-permute-start | bytes 6152 | tf_op jit(solution)/shard_map/ppermute | solution.py:180
  162.9 9.4 %collective-permute-start.7 = (f32[512]{0:T(512)S(1)}, f32[512]{0:T(512)S(1)}, u32[]{:S(2)}, u32[]{:S(2)}) collective-permute-start(f32[512]{0:T(512)S(1)} %add.28), channel_id=1, source_target_pairs={{0,4},{1,5},{2,6},{3,7},{4,8},{5,9},{6,10},{7,11},{8,12},{9,13},{1... | collective-permute-start | bytes 6152 | tf_op jit(solution)/shard_map/ppermute | solution.py:180
  172.3 7.6 %collective-permute-start.8 = (f32[512]{0:T(512)S(1)}, f32[512]{0:T(512)S(1)}, u32[]{:S(2)}, u32[]{:S(2)}) collective-permute-start(f32[512]{0:T(512)S(1)} %add.29), channel_id=1, source_target_pairs={{0,2},{1,3},{2,4},{3,5},{4,6},{5,7},{6,8},{7,9},{8,10},{9,11},{10,... | collective-permute-start | bytes 6152 | tf_op jit(solution)/shard_map/ppermute | solution.py:180
  179.9 6.7 %collective-permute-start.9 = (f32[512]{0:T(512)S(1)}, f32[512]{0:T(512)S(1)}, u32[]{:S(2)}, u32[]{:S(2)}) collective-permute-start(f32[512]{0:T(512)S(1)} %add.30), channel_id=1, source_target_pairs={{0,1},{1,2},{2,3},{3,4},{4,5},{5,6},{6,7},{7,8},{8,9},{9,10},{10,1... | collective-permute-start | bytes 6152 | tf_op jit(solution)/shard_map/ppermute | solution.py:180

commit v4 on v3

--- a/solution.py
+++ b/solution.py
@@ -16,6 +16,7 @@
 TP = FAR * NEAR
 CHIPS = 32
 HALF = FAR * COLS // 2
+GRANT = 24 * 1024 * 1024
 Z = ("zh", "zl")
 TRANSPOSED = (((0,), (0,)), ((), ()))
 
@@ -31,6 +32,7 @@
         scratch_shapes=scratch,
         input_output_aliases=aliases or {},
         cost_estimate=pl.CostEstimate(flops=flops, bytes_accessed=moved, transcendentals=0),
+        compiler_params=pltpu.CompilerParams(vmem_limit_bytes=GRANT),
     )
 
 
@@ -184,10 +186,8 @@
     return lax.ppermute(array, "core", [(0, 1), (1, 0)])
 
 
-def ladder(vector):
-    for distance in (8, 4, 2, 1):
-        vector = vector + hop(vector, distance)
-    return vector
+def gather_sum(vector):
+    return jnp.sum(lax.all_gather(vector, Z, axis=0, tiled=True), axis=0)
 
 
 def step(layer_input, gain, w_kv, d_kv, destination):
@@ -206,8 +206,7 @@
     onehot, squares, where = lax.optimization_barrier((onehot, squares, where))
 
     block = place(where, received, onehot)
-    copies = jnp.broadcast_to(block[None], (FAR, COLS, ROWS))
-    own = lax.all_to_all(copies, "zh", split_axis=0, concat_axis=0, tiled=True).reshape(FAR * COLS, ROWS)
+    own = lax.all_gather(block, "zh", axis=0, tiled=True)
     own, squares = lax.optimization_barrier((own, squares))
     behind = hop(own, 1)
     ahead = hop(own, -1)
@@ -228,7 +227,7 @@
     grad_weight = jnp.sum(parts.astype(jnp.float32), axis=0)
 
     dnormed, products = grad_rest(where, behind, ahead, far_a, far_b, w_kv, grad, x, gain[None, :])
-    mean_dot = ladder(products[0]) / D
+    mean_dot = gather_sum(products) / D
     along = x.astype(jnp.float32) * (inverse**3 * mean_dot)[:, None]
     grad_x = (inverse[:, None] * gain_wide * dnormed - along).astype(jnp.bfloat16)
     return (grad_x, grad_weight)

time: 191 us -> 159 us (0.83)
  starting transfers between devices: 82.4 us -> 52.9 us
  blocking collectives: 34.5 us -> 59.4 us
  Pallas kernels: 21.8 us -> 9.89 us
  waiting for transfers between devices: 32.9 us -> 25.9 us
  local copies, waits for them, and re-layouts: 7.95 us -> 1.71 us
    all_gather x0 -> x2, blocking collectives: none -> 59.4 us  [the longest x1 30 us: step(): own = lax.all_gather(block, 'zh', axis=0, tiled=True)]
    all_to_all x1 -> x0, blocking collectives: 34.5 us -> none  [step(): lax.all_to_all(copies, 'zh', split_axis=0, concat_axis=0, tiled=True)]
    ppermute x8 -> x4, starting transfers between devices: 42.2 us -> 14.1 us  [hop(): return lax.ppermute(array, Z, [(i, (i + step) % TP) for i in range(TP)])]
    ppermute x8 -> x4, waiting for transfers between devices: 21.5 us -> 13.2 us  [hop(): return lax.ppermute(array, Z, [(i, (i + step) % TP) for i in range(TP)])]
    pallas_call x1, Pallas kernels: 5.32 us -> 2.45 us  [grad_rest(): call(grad_rest_kernel, [None] * 8, shapes, flops, 24 * ROWS * FEAT)]
    unnamed x22 -> x20, local copies, waits for them, and re-layouts: 3.8 us -> 1.03 us
    pallas_call x1, Pallas kernels: 3.94 us -> 1.54 us  [weight_near(): call(weight_near_kernel, [None] * 4, shapes, flops, 18 * ROWS * FEAT)]
    pallas_call x1, Pallas kernels: 3.46 us -> 1.27 us  [grad_own(): call(grad_own_kernel, [None] * 2, shape, flops, 14 * ROWS * FEAT)]
  transfers between devices with their start and end apart: 13 -> 9, of which waited for: 10 -> 6; matrix products, arithmetic and copies ran while one was open for 6% -> 4% of each run, Pallas kernels for 7% -> 4%
where the time goes in v4:
time: 159 us; the launch traced here: 158 us
  blocking collectives  59.4 us (37%)
  starting transfers between devices  52.9 us (33%)
  waiting for transfers between devices  25.9 us (16%)
  Pallas kernels  9.89 us (6%)
  other arithmetic  7.63 us (5%)
  local copies, waits for them, and re-layouts  1.71 us (1%)
    all_gather x1, blocking collectives, step(): own = lax.all_gather(block, 'zh', axis=0, tiled=True)  30 us
    all_gather x1, blocking collectives, gather_sum(): return jnp.sum(lax.all_gather(vector, Z, axis=0, tiled=True), axis=0)  29.4 us
    all_to_all x1, starting transfers between devices, step(): lax.all_to_all(d_kv, ('chip', 'core'), split_axis=0, concat_axis=0, tiled...  17.4 us
    ppermute x4, starting transfers between devices, hop(): return lax.ppermute(array, Z, [(i, (i + step) % TP) for i in range(TP)])  14.1 us
    ppermute x4, waiting for transfers between devices, hop(): return lax.ppermute(array, Z, [(i, (i + step) % TP) for i in range(TP)])  13.2 us
    all_to_all x1, starting transfers between devices, tensor_sum(): lax.all_to_all(spread, Z, split_axis=0, concat_axis=0, tiled=True)  11.8 us
    all_to_all x1, waiting for transfers between devices, step(): lax.all_to_all(d_kv, ('chip', 'core'), split_axis=0, concat_axis=0, tiled...  6.9 us
    all_to_all x1, starting transfers between devices, step(): lax.all_to_all(pair.reshape(CHIPS, 32, FEAT), 'chip', split_axis=0, conca...  5.84 us
  transfers between devices with their start and end apart: 9, of which 6 were waited for; matrix products, arithmetic and copies ran while one was open for 4% of the time, Pallas kernels for 4%

profile of v4, /device:TPU:2, one launch (start us, length us, event | category | flops | bytes accessed | tf_op | source)
XLA Modules:
  0.0 158.4 jit_solution(12846107114727772092)
XLA Ops:
  0.6 0.0 copy-start.1
  0.6 0.0 copy-start.9
  0.7 17.4 %all-to-all-start = ((bf16[64,8,128]{2,1,0:T(8,128)(2,1)}), bf16[64,8,128]{2,1,0:T(8,128)(2,1)S(1)}, u32[]{:S(2)}, u32[]{:S(2)}) async-start(bf16[64,8,128]{2,1,0:T(8,128)(2,1)} %bitcast.8), calls=%async_computation | async-start | bytes 262144 | tf_op jit(solution)/shard_map/all_to_all | solution.py:195
  18.0 0.9 convert_reduce_fusion.1
  18.9 0.7 add_select_fusion
  19.6 1.2 fusion
  20.9 0.1 pad_add_fusion.where
  20.9 0.1 fusion.3.onehot
  21.1 6.9 %all-to-all-done = bf16[64,8,128]{2,1,0:T(8,128)(2,1)S(1)} async-done(((bf16[64,8,128]{2,1,0:T(8,128)(2,1)}), bf16[64,8,128]{2,1,0:T(8,128)(2,1)S(1)}, u32[]{:S(2)}, u32[]{:S(2)}) %all-to-all-start) | async-done | bytes 131104 | tf_op jit(solution)/shard_map/all_to_all | solution.py:195
  28.0 0.8 shard_map.68
  28.8 30.0 %all_gather.6.own = bf16[512,512]{1,0:T(8,128)(2,1)S(1)} all-gather(bf16[128,512]{1,0:T(8,128)(2,1)S(1)} %shard_map.68), channel_id=1, replica_groups=mesh['chip'=32,'core'=2,'zh'=4,'zl'=4] {'zh'}, dimensions={0}, use_global_device_ids=true | all-gather | bytes 655360 | tf_op jit(solution)/shard_map/all_gather | solution.py:209
  58.8 0.6 broadcast_in_dim.9
  59.4 11.8 %all-to-all-start.1 = ((f32[16,1,512]{2,1,0:T(1,128)}), f32[16,1,512]{2,1,0:T(1,128)S(1)}, u32[]{:S(2)}, u32[]{:S(2)}) async-start(f32[16,1,512]{2,1,0:T(1,128)} %broadcast_in_dim.9), calls=%async_computation.1 | async-start | bytes 65536 | tf_op jit(solution)/shard_map/all_to_all | solution.py:178
  71.2 3.8 %collective-permute-start = (bf16[512,512]{1,0:T(8,128)(2,1)S(1)}, bf16[512,512]{1,0:T(8,128)(2,1)S(1)}, u32[]{:S(2)}, u32[]{:S(2)}) collective-permute-start(bf16[512,512]{1,0:T(8,128)(2,1)S(1)} %all_gather.6.own), channel_id=1, source_target_pairs={{0,1},{1,2},{2,3},{3,4},{4,5},{5,6},{6,7},{7,8},{8,9},{9,10},{10,1... | collective-permute-start | bytes 1572872 | tf_op jit(solution)/shard_map/ppermute | solution.py:182
  75.1 3.2 %collective-permute-start.2 = (bf16[512,512]{1,0:T(8,128)(2,1)S(1)}, bf16[512,512]{1,0:T(8,128)(2,1)S(1)}, u32[]{:S(2)}, u32[]{:S(2)}) collective-permute-start(bf16[512,512]{1,0:T(8,128)(2,1)S(1)} %all_gather.6.own), channel_id=1, source_target_pairs={{0,15},{1,0},{2,1},{3,2},{4,3},{5,4},{6,5},{7,6},{8,7},{9,8},{10,9... | collective-permute-start | bytes 1572872 | tf_op jit(solution)/shard_map/ppermute | solution.py:182
  78.3 0.0 copy-done.9
  78.3 5.8 %all-to-all-done.1 = f32[16,1,512]{2,1,0:T(1,128)S(1)} async-done(((f32[16,1,512]{2,1,0:T(1,128)}), f32[16,1,512]{2,1,0:T(1,128)S(1)}, u32[]{:S(2)}, u32[]{:S(2)}) %all-to-all-start.1) | async-done | bytes 32800 | tf_op jit(solution)/shard_map/all_to_all | solution.py:178
  84.2 0.0 copy-done.1
  84.2 0.2 fusion.2.normed
  84.4 4.5 %collective-permute-done.behind = bf16[512,512]{1,0:T(8,128)(2,1)S(1)} collective-permute-done((bf16[512,512]{1,0:T(8,128)(2,1)S(1)}, bf16[512,512]{1,0:T(8,128)(2,1)S(1)}, u32[]{:S(2)}, u32[]{:S(2)}) %collective-permute-start) | collective-permute-done | bytes 524320 | tf_op jit(solution)/shard_map/ppermute | solution.py:182
  88.9 0.0 copy-start.2
  88.9 1.5 collective-permute-done.2.ahead
  90.3 0.0 copy-start.4
  90.4 1.5 shard_map.70
  91.9 1.9 %collective-permute-start.5 = (bf16[4,3,64,512]{3,2,1,0:T(8,128)(2,1)S(1)}, bf16[4,3,64,512]{3,2,1,0:T(8,128)(2,1)S(1)}, u32[]{:S(2)}, u32[]{:S(2)}) collective-permute-start(bf16[4,3,64,512]{3,2,1,0:T(8,128)(2,1)S(1)} %get-tuple-element.24), channel_id=1, source_target_pairs={{0,16},{16,0},{1,17},{17,1},{2,18},{18,2},{3,19},{19,3},{4,20},{20... | collective-permute-start | bytes 2359304 | tf_op jit(solution)/shard_map/ppermute | solution.py:186
  93.8 3.4 %collective-permute-start.1 = (bf16[256,512]{1,0:T(8,128)(2,1)S(1)}, bf16[256,512]{1,0:T(8,128)(2,1)S(1)}, u32[]{:S(2)}, u32[]{:S(2)}) collective-permute-start(bf16[256,512]{1,0:T(8,128)(2,1)S(1)} %slice.8), channel_id=1, source_target_pairs={{0,1},{1,2},{2,3},{3,4},{4,5},{5,6},{6,7},{7,8},{8,9},{9,10},{10,1... | collective-permute-start | bytes 786440 | tf_op jit(solution)/shard_map/ppermute | solution.py:182
  97.3 3.6 %collective-permute-start.3 = (bf16[256,512]{1,0:T(8,128)(2,1)S(1)}, bf16[256,512]{1,0:T(8,128)(2,1)S(1)}, u32[]{:S(2)}, u32[]{:S(2)}) collective-permute-start(bf16[256,512]{1,0:T(8,128)(2,1)S(1)} %slice.9), channel_id=1, source_target_pairs={{0,15},{1,0},{2,1},{3,2},{4,3},{5,4},{6,5},{7,6},{8,7},{9,8},{10,9... | collective-permute-start | bytes 786440 | tf_op jit(solution)/shard_map/ppermute | solution.py:182
  100.9 4.7 %collective-permute-done.1.far_a = bf16[256,512]{1,0:T(8,128)(2,1)S(1)} collective-permute-done((bf16[256,512]{1,0:T(8,128)(2,1)S(1)}, bf16[256,512]{1,0:T(8,128)(2,1)S(1)}, u32[]{:S(2)}, u32[]{:S(2)}) %collective-permute-start.1) | collective-permute-done | bytes 262176 | tf_op jit(solution)/shard_map/ppermute | solution.py:182
  105.7 2.5 %collective-permute-done.3.far_b = bf16[256,512]{1,0:T(8,128)(2,1)S(1)} collective-permute-done((bf16[256,512]{1,0:T(8,128)(2,1)S(1)}, bf16[256,512]{1,0:T(8,128)(2,1)S(1)}, u32[]{:S(2)}, u32[]{:S(2)}) %collective-permute-start.3) | collective-permute-done | bytes 262176 | tf_op jit(solution)/shard_map/ppermute | solution.py:182
  108.2 0.0 copy-start.7
  108.2 1.0 shard_map.69
  109.2 0.0 copy-done.2
  109.2 0.0 copy-done.4
  109.2 1.9 %collective-permute-start.4 = (bf16[4,64,512]{2,1,0:T(8,128)(2,1)S(1)}, bf16[4,64,512]{2,1,0:T(8,128)(2,1)S(1)}, u32[]{:S(2)}, u32[]{:S(2)}) collective-permute-start(bf16[4,64,512]{2,1,0:T(8,128)(2,1)S(1)} %get-tuple-element.22), channel_id=1, source_target_pairs={{0,16},{16,0},{1,17},{17,1},{2,18},{18,2},{3,19},{19,3},{4,20},{20... | collective-permute-start | bytes 786440 | tf_op jit(solution)/shard_map/ppermute | solution.py:186
  111.1 0.0 collective-permute-done.5.taken
  111.1 1.5 shard_map.71.placed
  112.7 0.0 copy-done.7
  112.7 0.0 collective-permute-done.4.taken
  112.7 0.0 copy-start
  112.7 1.3 shard_map.72
  114.0 5.8 %all-to-all-start.2 = ((bf16[32,32,512]{2,1,0:T(8,128)(2,1)}), bf16[32,32,512]{2,1,0:T(8,128)(2,1)}, u32[]{:S(2)}, u32[]{:S(2)}) async-start(bf16[32,32,512]{2,1,0:T(8,128)(2,1)} %bitcast.5), calls=%async_computation.2 | async-start | bytes 2097152 | tf_op jit(solution)/shard_map/all_to_all | solution.py:226
  119.9 0.0 copy-start.3
  119.9 0.0 copy-start.5
  119.9 0.0 copy-start.8
  119.9 0.0 copy-done
  119.9 1.3 shard_map.73.before
  121.2 0.0 copy-done.3
  121.2 0.0 copy-done.5
  121.2 0.0 copy-done.8
  121.2 2.5 %shard_map.74 = (f32[512,512]{1,0:T(8,128)S(1)}, f32[1,512]{1,0:T(1,128)S(1)}) custom-call(s32[2]{0:T(128)S(1)} %pad_add_fusion.where, bf16[512,512]{1,0:T(8,128)(2,1)S(1)} %copy-done.3, bf16[512,512]{1,0:T(8,128)(2,1)S(1)} %copy-done.5, bf16[256,512]{1,0:T(8,128)(2,1)S(1)} %collective-permute-done.1.far_a, bf16[256,512]{1,0:T(8,128)(2,1)S(1)} %copy-done.8, ...), custom_call_target="tpu_custom_call" | custom-call | flops 805306368 | bytes 6291456 | tf_op jit(solution)/shard_map/pallas_call | solution.py:85
  123.7 0.0 copy-start.6
  123.7 1.0 copy-done.6
  124.7 29.4 %all-gather = f32[16,1,512]{2,1,0:T(1,128)S(1)} all-gather(f32[1,1,512]{2,1,0:T(1,128)S(1)} %bitcast.7), channel_id=1, replica_groups=mesh['chip'=32,'core'=2,'zh'=4,'zl'=4] {'zh','zl'}, dimensions={0}, use_global_device_ids=true | all-gather | bytes 34816 | tf_op jit(solution)/shard_map/all_gather | solution.py:190
  154.1 2.3 %subtract_convert_fusion = bf16[512,512]{1,0:T(8,128)(2,1)} fusion(bf16[512,512]{1,0:T(8,128)(2,1)S(1)} %copy-done.1, f32[512,512]{1,0:T(8,128)} %copy-done.6, f32[512]{0:T(512)S(1)} %fusion.5, f32[512]{0:T(512)S(1)} %add_rsqrt_fusion, f32[512]{0:T(512)S(1)} %convert_element_type.27), kind=kLoop, calls=%fused_computation.6 | loop fusion | flops 1572864 | bytes 2103296 | tf_op jit(solution)/shard_map/convert_element_type | solution.py:232
  156.4 0.0 all-to-all-done.2
  156.4 2.0 %convert_reduce_fusion = f32[32,512]{1,0:T(8,128)} fusion(bf16[32,32,512]{2,1,0:T(8,128)(2,1)} %all-to-all-done.2), kind=kLoop, calls=%fused_computation | loop fusion | flops 1032192 | bytes 1114112 | tf_op jit(solution)/shard_map/reduce_sum | solution.py:227
  (8 shorter events, 0.1 us)
Async XLA Ops:
  0.6 83.5 %copy-start.1 = (bf16[512,512]{1,0:T(8,128)(2,1)S(1)}, bf16[512,512]{1,0:T(8,128)(2,1)}, u32[]{:S(2)}) copy-start(bf16[512,512]{1,0:T(8,128)(2,1)} %x) | copy-start | bytes 1572868
  0.6 77.7 %copy-start.9 = (bf16[512]{0:T(512)(128)(2,1)S(1)}, bf16[512]{0:T(512)(128)(2,1)}, u32[]{:S(2)}) copy-start(bf16[512]{0:T(512)(128)(2,1)} %param.6) | copy-start | bytes 3076
  0.7 27.3 %all-to-all-start = ((bf16[64,8,128]{2,1,0:T(8,128)(2,1)}), bf16[64,8,128]{2,1,0:T(8,128)(2,1)S(1)}, u32[]{:S(2)}, u32[]{:S(2)}) async-start(bf16[64,8,128]{2,1,0:T(8,128)(2,1)} %bitcast.8), calls=%async_computation | async-start | bytes 262144 | tf_op jit(solution)/shard_map/all_to_all | solution.py:195
  59.4 24.7 %all-to-all-start.1 = ((f32[16,1,512]{2,1,0:T(1,128)}), f32[16,1,512]{2,1,0:T(1,128)S(1)}, u32[]{:S(2)}, u32[]{:S(2)}) async-start(f32[16,1,512]{2,1,0:T(1,128)} %broadcast_in_dim.9), calls=%async_computation.1 | async-start | bytes 65536 | tf_op jit(solution)/shard_map/all_to_all | solution.py:178
  71.2 17.7 %collective-permute-start = (bf16[512,512]{1,0:T(8,128)(2,1)S(1)}, bf16[512,512]{1,0:T(8,128)(2,1)S(1)}, u32[]{:S(2)}, u32[]{:S(2)}) collective-permute-start(bf16[512,512]{1,0:T(8,128)(2,1)S(1)} %all_gather.6.own), channel_id=1, source_target_pairs={{0,1},{1,2},{2,3},{3,4},{4,5},{5,6},{6,7},{7,8},{8,9},{9,10},{10,1... | collective-permute-start | bytes 1572872 | tf_op jit(solution)/shard_map/ppermute | solution.py:182
  75.1 15.3 %collective-permute-start.2 = (bf16[512,512]{1,0:T(8,128)(2,1)S(1)}, bf16[512,512]{1,0:T(8,128)(2,1)S(1)}, u32[]{:S(2)}, u32[]{:S(2)}) collective-permute-start(bf16[512,512]{1,0:T(8,128)(2,1)S(1)} %all_gather.6.own), channel_id=1, source_target_pairs={{0,15},{1,0},{2,1},{3,2},{4,3},{5,4},{6,5},{7,6},{8,7},{9,8},{10,9... | collective-permute-start | bytes 1572872 | tf_op jit(solution)/shard_map/ppermute | solution.py:182
  88.9 20.3 %copy-start.2 = (bf16[512,512]{1,0:T(8,128)(2,1)}, bf16[512,512]{1,0:T(8,128)(2,1)S(1)}, u32[]{:S(2)}) copy-start(bf16[512,512]{1,0:T(8,128)(2,1)S(1)} %collective-permute-done.behind) | copy-start | bytes 1572868
  90.3 18.8 %copy-start.4 = (bf16[512,512]{1,0:T(8,128)(2,1)}, bf16[512,512]{1,0:T(8,128)(2,1)S(1)}, u32[]{:S(2)}) copy-start(bf16[512,512]{1,0:T(8,128)(2,1)S(1)} %collective-permute-done.2.ahead) | copy-start | bytes 1572868
  91.9 19.2 %collective-permute-start.5 = (bf16[4,3,64,512]{3,2,1,0:T(8,128)(2,1)S(1)}, bf16[4,3,64,512]{3,2,1,0:T(8,128)(2,1)S(1)}, u32[]{:S(2)}, u32[]{:S(2)}) collective-permute-start(bf16[4,3,64,512]{3,2,1,0:T(8,128)(2,1)S(1)} %get-tuple-element.24), channel_id=1, source_target_pairs={{0,16},{16,0},{1,17},{17,1},{2,18},{18,2},{3,19},{19,3},{4,20},{20... | collective-permute-start | bytes 2359304 | tf_op jit(solution)/shard_map/ppermute | solution.py:186
  93.8 11.8 %collective-permute-start.1 = (bf16[256,512]{1,0:T(8,128)(2,1)S(1)}, bf16[256,512]{1,0:T(8,128)(2,1)S(1)}, u32[]{:S(2)}, u32[]{:S(2)}) collective-permute-start(bf16[256,512]{1,0:T(8,128)(2,1)S(1)} %slice.8), channel_id=1, source_target_pairs={{0,1},{1,2},{2,3},{3,4},{4,5},{5,6},{6,7},{7,8},{8,9},{9,10},{10,1... | collective-permute-start | bytes 786440 | tf_op jit(solution)/shard_map/ppermute | solution.py:182
  97.3 10.9 %collective-permute-start.3 = (bf16[256,512]{1,0:T(8,128)(2,1)S(1)}, bf16[256,512]{1,0:T(8,128)(2,1)S(1)}, u32[]{:S(2)}, u32[]{:S(2)}) collective-permute-start(bf16[256,512]{1,0:T(8,128)(2,1)S(1)} %slice.9), channel_id=1, source_target_pairs={{0,15},{1,0},{2,1},{3,2},{4,3},{5,4},{6,5},{7,6},{8,7},{9,8},{10,9... | collective-permute-start | bytes 786440 | tf_op jit(solution)/shard_map/ppermute | solution.py:182
  108.2 4.5 %copy-start.7 = (bf16[256,512]{1,0:T(8,128)(2,1)}, bf16[256,512]{1,0:T(8,128)(2,1)S(1)}, u32[]{:S(2)}) copy-start(bf16[256,512]{1,0:T(8,128)(2,1)S(1)} %collective-permute-done.3.far_b) | copy-start | bytes 786436
  109.2 3.5 %collective-permute-start.4 = (bf16[4,64,512]{2,1,0:T(8,128)(2,1)S(1)}, bf16[4,64,512]{2,1,0:T(8,128)(2,1)S(1)}, u32[]{:S(2)}, u32[]{:S(2)}) collective-permute-start(bf16[4,64,512]{2,1,0:T(8,128)(2,1)S(1)} %get-tuple-element.22), channel_id=1, source_target_pairs={{0,16},{16,0},{1,17},{17,1},{2,18},{18,2},{3,19},{19,3},{4,20},{20... | collective-permute-start | bytes 786440 | tf_op jit(solution)/shard_map/ppermute | solution.py:186
  112.7 7.2 %copy-start = (bf16[2048,512]{1,0:T(8,128)(2,1)S(1)}, bf16[2048,512]{1,0:T(8,128)(2,1)}, u32[]{:S(2)}) copy-start(bf16[2048,512]{1,0:T(8,128)(2,1)} %w.3) | copy-start | bytes 6291460
  114.0 42.4 %all-to-all-start.2 = ((bf16[32,32,512]{2,1,0:T(8,128)(2,1)}), bf16[32,32,512]{2,1,0:T(8,128)(2,1)}, u32[]{:S(2)}, u32[]{:S(2)}) async-start(bf16[32,32,512]{2,1,0:T(8,128)(2,1)} %bitcast.5), calls=%async_computation.2 | async-start | bytes 2097152 | tf_op jit(solution)/shard_map/all_to_all | solution.py:226
  119.9 1.3 copy-start.3
  119.9 1.3 copy-start.5
  119.9 1.3 copy-start.8
  123.7 1.0 copy-start.6

commit v5 on v4

--- a/solution.py
+++ b/solution.py
@@ -46,31 +46,50 @@
     return call(place_kernel, [None] * 2, shape, 2 * ROWS * ROWS * COLS, ROWS * ROWS * 3)(where, received, onehot)
 
 
-def gradient(where, total, blocks, w):
-    for ref, at, shift, far in blocks:
+def fetch(where, w, pieces, rows, sems):
+    copies = []
+    for i, (_, _, shift, far) in enumerate(pieces):
         owner = far * NEAR + lax.rem(where[0] + shift, NEAR)
-        rows = w[pl.ds(pl.multiple_of(owner * COLS, COLS), COLS), :]
-        term = lax.dot_general(ref[at : at + COLS, :], rows, TRANSPOSED, preferred_element_type=jnp.float32)
+        source = w.at[pl.ds(pl.multiple_of(owner * COLS, COLS), COLS), :]
+        copies.append(pltpu.make_async_copy(source, rows.at[i], sems.at[i]))
+        copies[-1].start()
+    return copies
+
+
+def gradient(where, w, pieces, rows, sems, total):
+    copies = fetch(where, w, pieces, rows, sems)
+    for i, (ref, at, _, _) in enumerate(pieces):
+        copies[i].wait()
+        term = lax.dot_general(ref[at : at + COLS, :], rows[i], TRANSPOSED, preferred_element_type=jnp.float32)
         total = term if total is None else total + term
     return total
 
 
-def grad_own_kernel(where, own, w, out):
-    out[...] = gradient(where, None, [(own, COLS * far, 0, far) for far in range(FAR)], w)
-
-
-def grad_own(where, own, w_kv):
+def grad_near_kernel(where, own, behind, ahead, w, out, rows, sems):
+    pieces = [
+        (ref, COLS * far, shift, far)
+        for ref, shift in ((own, 0), (behind, NEAR - 1), (ahead, 1))
+        for far in range(FAR)
+    ]
+    out[...] = gradient(where, w, pieces, rows, sems, None)
+
+
+def w_scratch(count):
+    return [pltpu.VMEM((count, COLS, FEAT), jnp.bfloat16), pltpu.SemaphoreType.DMA((count,))]
+
+
+def grad_near(where, own, behind, ahead, w_kv):
     shape = jax.ShapeDtypeStruct((ROWS, FEAT), jnp.float32)
-    flops = 2 * FAR * ROWS * FEAT * COLS
-    return call(grad_own_kernel, [None] * 2, shape, flops, 14 * ROWS * FEAT)(where, own, w_kv)
-
-
-def grad_rest_kernel(where, behind, ahead, far_a, far_b, w, before, x, gain, out, products):
-    blocks = [(behind, COLS * far, NEAR - 1, far) for far in range(FAR)]
-    blocks += [(ahead, COLS * far, 1, far) for far in range(FAR)]
-    blocks += [(far_a, COLS * far, 2, far) for far in range(2)]
-    blocks += [(far_b, COLS * far, 2, 2 + far) for far in range(2)]
-    total = gradient(where, before[...], blocks, w)
+    flops = 6 * FAR * ROWS * FEAT * COLS
+    hbm = pl.BlockSpec(memory_space=pltpu.HBM)
+    return call(
+        grad_near_kernel, [None] * 3 + [hbm], shape, flops, 14 * ROWS * FEAT, scratch=w_scratch(3 * FAR)
+    )(where, own, behind, ahead, w_kv)
+
+
+def grad_far_kernel(where, far_a, far_b, w, before, x, gain, out, products, rows, sems):
+    pieces = [(ref, COLS * (far % 2), 2, far) for far, ref in enumerate((far_a, far_a, far_b, far_b))]
+    total = gradient(where, w, pieces, rows, sems, before[...])
     out[...] = total
     part = x[...].astype(jnp.float32) * gain[...].astype(jnp.float32) * total
     lanes = part[:, :COLS]
@@ -79,12 +98,13 @@
     products[...] = jnp.sum(lanes.T, axis=0, keepdims=True)
 
 
-def grad_rest(where, behind, ahead, far_a, far_b, w_kv, before, x, gain):
+def grad_far(where, far_a, far_b, w_kv, before, x, gain):
     shapes = [jax.ShapeDtypeStruct((ROWS, FEAT), jnp.float32), jax.ShapeDtypeStruct((1, ROWS), jnp.float32)]
-    flops = 6 * FAR * ROWS * FEAT * COLS
-    return call(grad_rest_kernel, [None] * 8, shapes, flops, 24 * ROWS * FEAT)(
-        where, behind, ahead, far_a, far_b, w_kv, before, x, gain
-    )
+    flops = 2 * FAR * ROWS * FEAT * COLS
+    hbm = pl.BlockSpec(memory_space=pltpu.HBM)
+    return call(
+        grad_far_kernel, [None, None, hbm, None, None, None], shapes, flops, 14 * ROWS * FEAT, scratch=w_scratch(FAR)
+    )(where, far_a, far_b, w_kv, before, x, gain)
 
 
 def split_rows(where, term):
@@ -191,6 +211,7 @@
 
 
 def step(layer_input, gain, w_kv, d_kv, destination):
+    w_kv = pltpu.with_memory_space_constraint(w_kv, pltpu.HBM)
     where = jnp.stack([lax.axis_index("zl"), lax.axis_index("core")]).astype(jnp.int32)
     received = lax.all_to_all(d_kv, ("chip", "core"), split_axis=0, concat_axis=0, tiled=True)
 
@@ -215,7 +236,7 @@
     far_a = hop(behind[:HALF], 1)
     far_b = hop(ahead[HALF:], -1)
 
-    grad = grad_own(where, own, w_kv)
+    grad = grad_near(where, own, behind, ahead, w_kv)
     keep_near, send_near = weight_near(where, own, behind, ahead, normed)
     taken_near = swap(send_near)
     placed = combine_near(where, keep_near, taken_near)
@@ -226,7 +247,7 @@
     parts = lax.all_to_all(pair.reshape(CHIPS, 32, FEAT), "chip", split_axis=0, concat_axis=0, tiled=True)
     grad_weight = jnp.sum(parts.astype(jnp.float32), axis=0)
 
-    dnormed, products = grad_rest(where, behind, ahead, far_a, far_b, w_kv, grad, x, gain[None, :])
+    dnormed, products = grad_far(where, far_a, far_b, w_kv, grad, x, gain[None, :])
     mean_dot = gather_sum(products) / D
     along = x.astype(jnp.float32) * (inverse**3 * mean_dot)[:, None]
     grad_x = (inverse[:, None] * gain_wide * dnormed - along).astype(jnp.bfloat16)

time: 159 us -> 160 us (level)
  Pallas kernels: 9.89 us -> 12.8 us
    pallas_call x2, Pallas kernels: 3.73 us -> 6.6 us  [the longest x1 4.1 us: grad_near(): call(grad_near_kernel, [None] * 3 + [hbm], shape, flops, 14 * ROWS * FEAT...]
  transfers between devices with their start and end apart: 9 -> 9, of which waited for: 6 -> 6; matrix products, arithmetic and copies ran while one was open for 4% -> 3% of each run, Pallas kernels for 4% -> 6%
where the time goes in v5:
time: 160 us; the launch traced here: 159 us
  blocking collectives  59.4 us (37%)
  starting transfers between devices  52.9 us (33%)
  waiting for transfers between devices  25.9 us (16%)
  Pallas kernels  12.8 us (8%)
  other arithmetic  6.41 us (4%)
    all_gather x1, blocking collectives, step(): own = lax.all_gather(block, 'zh', axis=0, tiled=True)  30 us
    all_gather x1, blocking collectives, gather_sum(): return jnp.sum(lax.all_gather(vector, Z, axis=0, tiled=True), axis=0)  29.4 us
    all_to_all x1, starting transfers between devices, step(): lax.all_to_all(d_kv, ('chip', 'core'), split_axis=0, concat_axis=0, tiled...  17.4 us
    ppermute x4, starting transfers between devices, hop(): return lax.ppermute(array, Z, [(i, (i + step) % TP) for i in range(TP)])  14.1 us
    ppermute x4, waiting for transfers between devices, hop(): return lax.ppermute(array, Z, [(i, (i + step) % TP) for i in range(TP)])  13.2 us
    all_to_all x1, starting transfers between devices, tensor_sum(): lax.all_to_all(spread, Z, split_axis=0, concat_axis=0, tiled=True)  11.8 us
    all_to_all x1, waiting for transfers between devices, step(): lax.all_to_all(d_kv, ('chip', 'core'), split_axis=0, concat_axis=0, tiled...  6.9 us
    all_to_all x1, starting transfers between devices, step(): lax.all_to_all(pair.reshape(CHIPS, 32, FEAT), 'chip', split_axis=0, conca...  5.84 us
  transfers between devices with their start and end apart: 9, of which 6 were waited for; matrix products, arithmetic and copies ran while one was open for 3% of the time, Pallas kernels for 6%

profile of v5, /device:TPU:2, one launch (start us, length us, event | category | flops | bytes accessed | tf_op | source)
XLA Modules:
  0.0 159.0 jit_solution(2287739863243219302)
XLA Ops:
  0.6 0.0 copy-start
  0.6 0.0 copy-start.1
  0.7 17.4 %all-to-all-start = ((bf16[64,8,128]{2,1,0:T(8,128)(2,1)}), bf16[64,8,128]{2,1,0:T(8,128)(2,1)S(1)}, u32[]{:S(2)}, u32[]{:S(2)}) async-start(bf16[64,8,128]{2,1,0:T(8,128)(2,1)} %bitcast.8), calls=%async_computation | async-start | bytes 262144 | tf_op jit(solution)/shard_map/all_to_all | solution.py:216
  18.0 0.9 convert_reduce_fusion.1
  18.9 0.7 add_select_fusion
  19.6 1.2 fusion
  20.9 0.1 pad_add_fusion.where
  20.9 0.1 fusion.3.onehot
  21.1 6.9 %all-to-all-done = bf16[64,8,128]{2,1,0:T(8,128)(2,1)S(1)} async-done(((bf16[64,8,128]{2,1,0:T(8,128)(2,1)}), bf16[64,8,128]{2,1,0:T(8,128)(2,1)S(1)}, u32[]{:S(2)}, u32[]{:S(2)}) %all-to-all-start) | async-done | bytes 131104 | tf_op jit(solution)/shard_map/all_to_all | solution.py:216
  28.0 0.8 shard_map.68
  28.8 30.0 %all_gather.6.own = bf16[512,512]{1,0:T(8,128)(2,1)S(1)} all-gather(bf16[128,512]{1,0:T(8,128)(2,1)S(1)} %shard_map.68), channel_id=1, replica_groups=mesh['chip'=32,'core'=2,'zh'=4,'zl'=4] {'zh'}, dimensions={0}, use_global_device_ids=true | all-gather | bytes 655360 | tf_op jit(solution)/shard_map/all_gather | solution.py:230
  58.8 0.6 broadcast_in_dim.9
  59.4 11.8 %all-to-all-start.1 = ((f32[16,1,512]{2,1,0:T(1,128)}), f32[16,1,512]{2,1,0:T(1,128)S(1)}, u32[]{:S(2)}, u32[]{:S(2)}) async-start(f32[16,1,512]{2,1,0:T(1,128)} %broadcast_in_dim.9), calls=%async_computation.1 | async-start | bytes 65536 | tf_op jit(solution)/shard_map/all_to_all | solution.py:198
  71.2 3.8 %collective-permute-start = (bf16[512,512]{1,0:T(8,128)(2,1)S(1)}, bf16[512,512]{1,0:T(8,128)(2,1)S(1)}, u32[]{:S(2)}, u32[]{:S(2)}) collective-permute-start(bf16[512,512]{1,0:T(8,128)(2,1)S(1)} %all_gather.6.own), channel_id=1, source_target_pairs={{0,1},{1,2},{2,3},{3,4},{4,5},{5,6},{6,7},{7,8},{8,9},{9,10},{10,1... | collective-permute-start | bytes 1572872 | tf_op jit(solution)/shard_map/ppermute | solution.py:202
  75.1 3.2 %collective-permute-start.2 = (bf16[512,512]{1,0:T(8,128)(2,1)S(1)}, bf16[512,512]{1,0:T(8,128)(2,1)S(1)}, u32[]{:S(2)}, u32[]{:S(2)}) collective-permute-start(bf16[512,512]{1,0:T(8,128)(2,1)S(1)} %all_gather.6.own), channel_id=1, source_target_pairs={{0,15},{1,0},{2,1},{3,2},{4,3},{5,4},{6,5},{7,6},{8,7},{9,8},{10,9... | collective-permute-start | bytes 1572872 | tf_op jit(solution)/shard_map/ppermute | solution.py:202
  78.3 0.0 copy-done.1
  78.3 5.8 %all-to-all-done.1 = f32[16,1,512]{2,1,0:T(1,128)S(1)} async-done(((f32[16,1,512]{2,1,0:T(1,128)}), f32[16,1,512]{2,1,0:T(1,128)S(1)}, u32[]{:S(2)}, u32[]{:S(2)}) %all-to-all-start.1) | async-done | bytes 32800 | tf_op jit(solution)/shard_map/all_to_all | solution.py:198
  84.2 0.0 copy-done
  84.2 0.2 fusion.2.normed
  84.4 4.5 %collective-permute-done.behind = bf16[512,512]{1,0:T(8,128)(2,1)S(1)} collective-permute-done((bf16[512,512]{1,0:T(8,128)(2,1)S(1)}, bf16[512,512]{1,0:T(8,128)(2,1)S(1)}, u32[]{:S(2)}, u32[]{:S(2)}) %collective-permute-start) | collective-permute-done | bytes 524320 | tf_op jit(solution)/shard_map/ppermute | solution.py:202
  88.9 1.5 collective-permute-done.2.ahead
  90.3 1.5 shard_map.70
  91.9 1.9 %collective-permute-start.5 = (bf16[4,3,64,512]{3,2,1,0:T(8,128)(2,1)S(1)}, bf16[4,3,64,512]{3,2,1,0:T(8,128)(2,1)S(1)}, u32[]{:S(2)}, u32[]{:S(2)}) collective-permute-start(bf16[4,3,64,512]{3,2,1,0:T(8,128)(2,1)S(1)} %get-tuple-element.24), channel_id=1, source_target_pairs={{0,16},{16,0},{1,17},{17,1},{2,18},{18,2},{3,19},{19,3},{4,20},{20... | collective-permute-start | bytes 2359304 | tf_op jit(solution)/shard_map/ppermute | solution.py:206
  93.8 3.4 %collective-permute-start.1 = (bf16[256,512]{1,0:T(8,128)(2,1)S(1)}, bf16[256,512]{1,0:T(8,128)(2,1)S(1)}, u32[]{:S(2)}, u32[]{:S(2)}) collective-permute-start(bf16[256,512]{1,0:T(8,128)(2,1)S(1)} %slice.8), channel_id=1, source_target_pairs={{0,1},{1,2},{2,3},{3,4},{4,5},{5,6},{6,7},{7,8},{8,9},{9,10},{10,1... | collective-permute-start | bytes 786440 | tf_op jit(solution)/shard_map/ppermute | solution.py:202
  97.3 3.6 %collective-permute-start.3 = (bf16[256,512]{1,0:T(8,128)(2,1)S(1)}, bf16[256,512]{1,0:T(8,128)(2,1)S(1)}, u32[]{:S(2)}, u32[]{:S(2)}) collective-permute-start(bf16[256,512]{1,0:T(8,128)(2,1)S(1)} %slice.9), channel_id=1, source_target_pairs={{0,15},{1,0},{2,1},{3,2},{4,3},{5,4},{6,5},{7,6},{8,7},{9,8},{10,9... | collective-permute-start | bytes 786440 | tf_op jit(solution)/shard_map/ppermute | solution.py:202
  100.9 4.7 %collective-permute-done.1.far_a = bf16[256,512]{1,0:T(8,128)(2,1)S(1)} collective-permute-done((bf16[256,512]{1,0:T(8,128)(2,1)S(1)}, bf16[256,512]{1,0:T(8,128)(2,1)S(1)}, u32[]{:S(2)}, u32[]{:S(2)}) %collective-permute-start.1) | collective-permute-done | bytes 262176 | tf_op jit(solution)/shard_map/ppermute | solution.py:202
  105.7 2.5 %collective-permute-done.3.far_b = bf16[256,512]{1,0:T(8,128)(2,1)S(1)} collective-permute-done((bf16[256,512]{1,0:T(8,128)(2,1)S(1)}, bf16[256,512]{1,0:T(8,128)(2,1)S(1)}, u32[]{:S(2)}, u32[]{:S(2)}) %collective-permute-start.3) | collective-permute-done | bytes 262176 | tf_op jit(solution)/shard_map/ppermute | solution.py:202
  108.2 1.0 shard_map.69
  109.1 1.9 %collective-permute-start.4 = (bf16[4,64,512]{2,1,0:T(8,128)(2,1)S(1)}, bf16[4,64,512]{2,1,0:T(8,128)(2,1)S(1)}, u32[]{:S(2)}, u32[]{:S(2)}) collective-permute-start(bf16[4,64,512]{2,1,0:T(8,128)(2,1)S(1)} %get-tuple-element.22), channel_id=1, source_target_pairs={{0,16},{16,0},{1,17},{17,1},{2,18},{18,2},{3,19},{19,3},{4,20},{20... | collective-permute-start | bytes 786440 | tf_op jit(solution)/shard_map/ppermute | solution.py:206
  111.1 0.0 collective-permute-done.5.taken
  111.1 1.6 shard_map.71.placed
  112.6 0.0 collective-permute-done.4.taken
  112.7 1.3 shard_map.72
  114.0 5.8 %all-to-all-start.2 = ((bf16[32,32,512]{2,1,0:T(8,128)(2,1)}), bf16[32,32,512]{2,1,0:T(8,128)(2,1)}, u32[]{:S(2)}, u32[]{:S(2)}) async-start(bf16[32,32,512]{2,1,0:T(8,128)(2,1)} %bitcast.5), calls=%async_computation.2 | async-start | bytes 2097152 | tf_op jit(solution)/shard_map/all_to_all | solution.py:247
  119.9 4.1 %shard_map.73.before = f32[512,512]{1,0:T(8,128)S(1)} custom-call(s32[2]{0:T(128)S(1)} %pad_add_fusion.where, bf16[512,512]{1,0:T(8,128)(2,1)S(1)} %all_gather.6.own, bf16[512,512]{1,0:T(8,128)(2,1)S(1)} %collective-permute-done.behind, bf16[512,512]{1,0:T(8,128)(2,1)S(1)} %collective-permute-done.2.ahead, bf16[2048,512]{1,0:T(8,128)(2,1)} %w.3), custom_call_target="tpu_custom_call" | custom-call | flops 805306368 | bytes 3670016 | tf_op jit(solution)/shard_map/pallas_call | solution.py:85
  124.0 2.5 %shard_map.74 = (f32[512,512]{1,0:T(8,128)S(1)}, f32[1,512]{1,0:T(1,128)S(1)}) custom-call(s32[2]{0:T(128)S(1)} %pad_add_fusion.where, bf16[256,512]{1,0:T(8,128)(2,1)S(1)} %collective-permute-done.1.far_a, bf16[256,512]{1,0:T(8,128)(2,1)S(1)} %collective-permute-done.3.far_b, bf16[2048,512]{1,0:T(8,128)(2,1)} %w.3, f32[512,512]{1,0:T(8,128)S(1)} %shard_map.73.before, ...), custom_call_target="tpu_custom_call" | custom-call | flops 268435456 | bytes 3670016 | tf_op jit(solution)/shard_map/pallas_call | solution.py:105
  126.5 29.4 %all-gather = f32[16,1,512]{2,1,0:T(1,128)S(1)} all-gather(f32[1,1,512]{2,1,0:T(1,128)S(1)} %bitcast.7), channel_id=1, replica_groups=mesh['chip'=32,'core'=2,'zh'=4,'zl'=4] {'zh','zl'}, dimensions={0}, use_global_device_ids=true | all-gather | bytes 34816 | tf_op jit(solution)/shard_map/all_gather | solution.py:210
  155.9 1.1 subtract_convert_fusion
  157.0 0.0 all-to-all-done.2
  157.0 2.0 %convert_reduce_fusion = f32[32,512]{1,0:T(8,128)} fusion(bf16[32,32,512]{2,1,0:T(8,128)(2,1)} %all-to-all-done.2), kind=kLoop, calls=%fused_computation | loop fusion | flops 1032192 | bytes 1114112 | tf_op jit(solution)/shard_map/reduce_sum | solution.py:248
  (8 shorter events, 0.1 us)
Async XLA Ops:
  0.6 83.5 %copy-start = (bf16[512,512]{1,0:T(8,128)(2,1)S(1)}, bf16[512,512]{1,0:T(8,128)(2,1)}, u32[]{:S(2)}) copy-start(bf16[512,512]{1,0:T(8,128)(2,1)} %x) | copy-start | bytes 1572868
  0.6 77.7 %copy-start.1 = (bf16[512]{0:T(512)(128)(2,1)S(1)}, bf16[512]{0:T(512)(128)(2,1)}, u32[]{:S(2)}) copy-start(bf16[512]{0:T(512)(128)(2,1)} %param.6) | copy-start | bytes 3076
  0.7 27.3 %all-to-all-start = ((bf16[64,8,128]{2,1,0:T(8,128)(2,1)}), bf16[64,8,128]{2,1,0:T(8,128)(2,1)S(1)}, u32[]{:S(2)}, u32[]{:S(2)}) async-start(bf16[64,8,128]{2,1,0:T(8,128)(2,1)} %bitcast.8), calls=%async_computation | async-start | bytes 262144 | tf_op jit(solution)/shard_map/all_to_all | solution.py:216
  59.4 24.7 %all-to-all-start.1 = ((f32[16,1,512]{2,1,0:T(1,128)}), f32[16,1,512]{2,1,0:T(1,128)S(1)}, u32[]{:S(2)}, u32[]{:S(2)}) async-start(f32[16,1,512]{2,1,0:T(1,128)} %broadcast_in_dim.9), calls=%async_computation.1 | async-start | bytes 65536 | tf_op jit(solution)/shard_map/all_to_all | solution.py:198
  71.2 17.7 %collective-permute-start = (bf16[512,512]{1,0:T(8,128)(2,1)S(1)}, bf16[512,512]{1,0:T(8,128)(2,1)S(1)}, u32[]{:S(2)}, u32[]{:S(2)}) collective-permute-start(bf16[512,512]{1,0:T(8,128)(2,1)S(1)} %all_gather.6.own), channel_id=1, source_target_pairs={{0,1},{1,2},{2,3},{3,4},{4,5},{5,6},{6,7},{7,8},{8,9},{9,10},{10,1... | collective-permute-start | bytes 1572872 | tf_op jit(solution)/shard_map/ppermute | solution.py:202
  75.1 15.3 %collective-permute-start.2 = (bf16[512,512]{1,0:T(8,128)(2,1)S(1)}, bf16[512,512]{1,0:T(8,128)(2,1)S(1)}, u32[]{:S(2)}, u32[]{:S(2)}) collective-permute-start(bf16[512,512]{1,0:T(8,128)(2,1)S(1)} %all_gather.6.own), channel_id=1, source_target_pairs={{0,15},{1,0},{2,1},{3,2},{4,3},{5,4},{6,5},{7,6},{8,7},{9,8},{10,9... | collective-permute-start | bytes 1572872 | tf_op jit(solution)/shard_map/ppermute | solution.py:202
  91.9 19.2 %collective-permute-start.5 = (bf16[4,3,64,512]{3,2,1,0:T(8,128)(2,1)S(1)}, bf16[4,3,64,512]{3,2,1,0:T(8,128)(2,1)S(1)}, u32[]{:S(2)}, u32[]{:S(2)}) collective-permute-start(bf16[4,3,64,512]{3,2,1,0:T(8,128)(2,1)S(1)} %get-tuple-element.24), channel_id=1, source_target_pairs={{0,16},{16,0},{1,17},{17,1},{2,18},{18,2},{3,19},{19,3},{4,20},{20... | collective-permute-start | bytes 2359304 | tf_op jit(solution)/shard_map/ppermute | solution.py:206
  93.8 11.8 %collective-permute-start.1 = (bf16[256,512]{1,0:T(8,128)(2,1)S(1)}, bf16[256,512]{1,0:T(8,128)(2,1)S(1)}, u32[]{:S(2)}, u32[]{:S(2)}) collective-permute-start(bf16[256,512]{1,0:T(8,128)(2,1)S(1)} %slice.8), channel_id=1, source_target_pairs={{0,1},{1,2},{2,3},{3,4},{4,5},{5,6},{6,7},{7,8},{8,9},{9,10},{10,1... | collective-permute-start | bytes 786440 | tf_op jit(solution)/shard_map/ppermute | solution.py:202
  97.3 10.9 %collective-permute-start.3 = (bf16[256,512]{1,0:T(8,128)(2,1)S(1)}, bf16[256,512]{1,0:T(8,128)(2,1)S(1)}, u32[]{:S(2)}, u32[]{:S(2)}) collective-permute-start(bf16[256,512]{1,0:T(8,128)(2,1)S(1)} %slice.9), channel_id=1, source_target_pairs={{0,15},{1,0},{2,1},{3,2},{4,3},{5,4},{6,5},{7,6},{8,7},{9,8},{10,9... | collective-permute-start | bytes 786440 | tf_op jit(solution)/shard_map/ppermute | solution.py:202
  109.1 3.5 %collective-permute-start.4 = (bf16[4,64,512]{2,1,0:T(8,128)(2,1)S(1)}, bf16[4,64,512]{2,1,0:T(8,128)(2,1)S(1)}, u32[]{:S(2)}, u32[]{:S(2)}) collective-permute-start(bf16[4,64,512]{2,1,0:T(8,128)(2,1)S(1)} %get-tuple-element.22), channel_id=1, source_target_pairs={{0,16},{16,0},{1,17},{17,1},{2,18},{18,2},{3,19},{19,3},{4,20},{20... | collective-permute-start | bytes 786440 | tf_op jit(solution)/shard_map/ppermute | solution.py:206
  114.0 43.0 %all-to-all-start.2 = ((bf16[32,32,512]{2,1,0:T(8,128)(2,1)}), bf16[32,32,512]{2,1,0:T(8,128)(2,1)}, u32[]{:S(2)}, u32[]{:S(2)}) async-start(bf16[32,32,512]{2,1,0:T(8,128)(2,1)} %bitcast.5), calls=%async_computation.2 | async-start | bytes 2097152 | tf_op jit(solution)/shard_map/all_to_all | solution.py:247

commit v6 on v5

--- a/solution.py
+++ b/solution.py
@@ -65,31 +65,18 @@
     return total
 
 
-def grad_near_kernel(where, own, behind, ahead, w, out, rows, sems):
+def w_scratch(count):
+    return [pltpu.VMEM((count, COLS, FEAT), jnp.bfloat16), pltpu.SemaphoreType.DMA((count,))]
+
+
+def grad_kernel(where, own, behind, ahead, far_a, far_b, w, x, gain, out, products, rows, sems):
     pieces = [
         (ref, COLS * far, shift, far)
         for ref, shift in ((own, 0), (behind, NEAR - 1), (ahead, 1))
         for far in range(FAR)
     ]
-    out[...] = gradient(where, w, pieces, rows, sems, None)
-
-
-def w_scratch(count):
-    return [pltpu.VMEM((count, COLS, FEAT), jnp.bfloat16), pltpu.SemaphoreType.DMA((count,))]
-
-
-def grad_near(where, own, behind, ahead, w_kv):
-    shape = jax.ShapeDtypeStruct((ROWS, FEAT), jnp.float32)
-    flops = 6 * FAR * ROWS * FEAT * COLS
-    hbm = pl.BlockSpec(memory_space=pltpu.HBM)
-    return call(
-        grad_near_kernel, [None] * 3 + [hbm], shape, flops, 14 * ROWS * FEAT, scratch=w_scratch(3 * FAR)
-    )(where, own, behind, ahead, w_kv)
-
-
-def grad_far_kernel(where, far_a, far_b, w, before, x, gain, out, products, rows, sems):
-    pieces = [(ref, COLS * (far % 2), 2, far) for far, ref in enumerate((far_a, far_a, far_b, far_b))]
-    total = gradient(where, w, pieces, rows, sems, before[...])
+    pieces += [(ref, COLS * (far % 2), 2, far) for far, ref in enumerate((far_a, far_a, far_b, far_b))]
+    total = gradient(where, w, pieces, rows, sems, None)
     out[...] = total
     part = x[...].astype(jnp.float32) * gain[...].astype(jnp.float32) * total
     lanes = part[:, :COLS]
@@ -98,13 +85,13 @@
     products[...] = jnp.sum(lanes.T, axis=0, keepdims=True)
 
 
-def grad_far(where, far_a, far_b, w_kv, before, x, gain):
+def grad_step(where, own, behind, ahead, far_a, far_b, w_kv, x, gain):
     shapes = [jax.ShapeDtypeStruct((ROWS, FEAT), jnp.float32), jax.ShapeDtypeStruct((1, ROWS), jnp.float32)]
-    flops = 2 * FAR * ROWS * FEAT * COLS
+    flops = 2 * TP * ROWS * FEAT * COLS
     hbm = pl.BlockSpec(memory_space=pltpu.HBM)
     return call(
-        grad_far_kernel, [None, None, hbm, None, None, None], shapes, flops, 14 * ROWS * FEAT, scratch=w_scratch(FAR)
-    )(where, far_a, far_b, w_kv, before, x, gain)
+        grad_kernel, [None] * 5 + [hbm, None, None], shapes, flops, 24 * ROWS * FEAT, scratch=w_scratch(TP)
+    )(where, own, behind, ahead, far_a, far_b, w_kv, x, gain)
 
 
 def split_rows(where, term):
@@ -207,7 +194,8 @@
 
 
 def gather_sum(vector):
-    return jnp.sum(lax.all_gather(vector, Z, axis=0, tiled=True), axis=0)
+    near = jnp.sum(lax.all_gather(vector, "zl", axis=0, tiled=True), axis=0, keepdims=True)
+    return jnp.sum(lax.all_gather(near, "zh", axis=0, tiled=True), axis=0)
 
 
 def step(layer_input, gain, w_kv, d_kv, destination):
@@ -236,7 +224,6 @@
     far_a = hop(behind[:HALF], 1)
     far_b = hop(ahead[HALF:], -1)
 
-    grad = grad_near(where, own, behind, ahead, w_kv)
     keep_near, send_near = weight_near(where, own, behind, ahead, normed)
     taken_near = swap(send_near)
     placed = combine_near(where, keep_near, taken_near)
@@ -247,7 +234,7 @@
     parts = lax.all_to_all(pair.reshape(CHIPS, 32, FEAT), "chip", split_axis=0, concat_axis=0, tiled=True)
     grad_weight = jnp.sum(parts.astype(jnp.float32), axis=0)
 
-    dnormed, products = grad_far(where, far_a, far_b, w_kv, grad, x, gain[None, :])
+    dnormed, products = grad_step(where, own, behind, ahead, far_a, far_b, w_kv, x, gain[None, :])
     mean_dot = gather_sum(products) / D
     along = x.astype(jnp.float32) * (inverse**3 * mean_dot)[:, None]
     grad_x = (inverse[:, None] * gain_wide * dnormed - along).astype(jnp.bfloat16)

time: 160 us -> 162 us (1.012)
  blocking collectives: 59.4 us -> 62.6 us
    all_gather x1 -> x2, blocking collectives: 29.4 us -> 32.6 us  [the longest x1 19.1 us: gather_sum(): return jnp.sum(lax.all_gather(near, 'zh', axis=0, tiled=True), axis=0)]
    pallas_call x2 -> x1, Pallas kernels: 6.6 us -> 5.03 us  [grad_step(): call(grad_kernel, [None] * 5 + [hbm, None, None], shapes, flops, 24 * ROW...]
  transfers between devices with their start and end apart: 9 -> 9, of which waited for: 6 -> 6; matrix products, arithmetic and copies ran while one was open for 3% -> 3% of each run, Pallas kernels for 6% -> 5%
where the time goes in v6:
time: 162 us
  blocking collectives  62.6 us (39%)
  starting transfers between devices  52.9 us (33%)
  waiting for transfers between devices  25.9 us (16%)
  Pallas kernels  11.2 us (7%)
  other arithmetic  6.42 us (4%)
  local copies, waits for them, and re-layouts  1.63 us (1%)
    all_gather x1, blocking collectives, step(): own = lax.all_gather(block, 'zh', axis=0, tiled=True)  30 us
    all_gather x1, blocking collectives, gather_sum(): return jnp.sum(lax.all_gather(near, 'zh', axis=0, tiled=True), axis=0)  19.1 us
    all_to_all x1, starting transfers between devices, step(): lax.all_to_all(d_kv, ('chip', 'core'), split_axis=0, concat_axis=0, tiled...  17.4 us
    ppermute x4, starting transfers between devices, hop(): return lax.ppermute(array, Z, [(i, (i + step) % TP) for i in range(TP)])  14.1 us
    all_gather x1, blocking collectives, gather_sum(): lax.all_gather(vector, 'zl', axis=0, tiled=True)  13.5 us
    ppermute x4, waiting for transfers between devices, hop(): return lax.ppermute(array, Z, [(i, (i + step) % TP) for i in range(TP)])  13.2 us
    all_to_all x1, starting transfers between devices, tensor_sum(): lax.all_to_all(spread, Z, split_axis=0, concat_axis=0, tiled=True)  11.8 us
    all_to_all x1, waiting for transfers between devices, step(): lax.all_to_all(d_kv, ('chip', 'core'), split_axis=0, concat_axis=0, tiled...  6.9 us
  transfers between devices with their start and end apart: 9, of which 6 were waited for; matrix products, arithmetic and copies ran while one was open for 3% of the time, Pallas kernels for 5%

profile of v6, /device:TPU:2, one launch (start us, length us, event | category | flops | bytes accessed | tf_op | source)
XLA Modules:
  0.0 161.5 jit_solution(5704601092077238932)
XLA Ops:
  0.6 0.0 copy-start
  0.6 0.0 copy-start.3
  0.7 17.4 %all-to-all-start = ((bf16[64,8,128]{2,1,0:T(8,128)(2,1)}), bf16[64,8,128]{2,1,0:T(8,128)(2,1)S(1)}, u32[]{:S(2)}, u32[]{:S(2)}) async-start(bf16[64,8,128]{2,1,0:T(8,128)(2,1)} %bitcast.9), calls=%async_computation | async-start | bytes 262144 | tf_op jit(solution)/shard_map/all_to_all | solution.py:204
  18.0 0.9 convert_reduce_fusion.1
  18.9 0.7 add_select_fusion
  19.6 1.2 fusion
  20.9 0.1 pad_add_fusion.where
  20.9 0.1 fusion.3.onehot
  21.1 6.9 %all-to-all-done = bf16[64,8,128]{2,1,0:T(8,128)(2,1)S(1)} async-done(((bf16[64,8,128]{2,1,0:T(8,128)(2,1)}), bf16[64,8,128]{2,1,0:T(8,128)(2,1)S(1)}, u32[]{:S(2)}, u32[]{:S(2)}) %all-to-all-start) | async-done | bytes 131104 | tf_op jit(solution)/shard_map/all_to_all | solution.py:204
  28.0 0.8 shard_map.68
  28.8 30.0 %all_gather.9.own = bf16[512,512]{1,0:T(8,128)(2,1)S(1)} all-gather(bf16[128,512]{1,0:T(8,128)(2,1)S(1)} %shard_map.68), channel_id=1, replica_groups=mesh['chip'=32,'core'=2,'zh'=4,'zl'=4] {'zh'}, dimensions={0}, use_global_device_ids=true | all-gather | bytes 655360 | tf_op jit(solution)/shard_map/all_gather | solution.py:218
  58.8 0.6 broadcast_in_dim.11
  59.4 11.8 %all-to-all-start.1 = ((f32[16,1,512]{2,1,0:T(1,128)}), f32[16,1,512]{2,1,0:T(1,128)S(1)}, u32[]{:S(2)}, u32[]{:S(2)}) async-start(f32[16,1,512]{2,1,0:T(1,128)} %broadcast_in_dim.11), calls=%async_computation.1 | async-start | bytes 65536 | tf_op jit(solution)/shard_map/all_to_all | solution.py:185
  71.2 3.8 %collective-permute-start = (bf16[512,512]{1,0:T(8,128)(2,1)S(1)}, bf16[512,512]{1,0:T(8,128)(2,1)S(1)}, u32[]{:S(2)}, u32[]{:S(2)}) collective-permute-start(bf16[512,512]{1,0:T(8,128)(2,1)S(1)} %all_gather.9.own), channel_id=1, source_target_pairs={{0,1},{1,2},{2,3},{3,4},{4,5},{5,6},{6,7},{7,8},{8,9},{9,10},{10,1... | collective-permute-start | bytes 1572872 | tf_op jit(solution)/shard_map/ppermute | solution.py:189
  75.1 3.2 %collective-permute-start.2 = (bf16[512,512]{1,0:T(8,128)(2,1)S(1)}, bf16[512,512]{1,0:T(8,128)(2,1)S(1)}, u32[]{:S(2)}, u32[]{:S(2)}) collective-permute-start(bf16[512,512]{1,0:T(8,128)(2,1)S(1)} %all_gather.9.own), channel_id=1, source_target_pairs={{0,15},{1,0},{2,1},{3,2},{4,3},{5,4},{6,5},{7,6},{8,7},{9,8},{10,9... | collective-permute-start | bytes 1572872 | tf_op jit(solution)/shard_map/ppermute | solution.py:189
  78.3 0.0 copy-done.3
  78.3 5.8 %all-to-all-done.1 = f32[16,1,512]{2,1,0:T(1,128)S(1)} async-done(((f32[16,1,512]{2,1,0:T(1,128)}), f32[16,1,512]{2,1,0:T(1,128)S(1)}, u32[]{:S(2)}, u32[]{:S(2)}) %all-to-all-start.1) | async-done | bytes 32800 | tf_op jit(solution)/shard_map/all_to_all | solution.py:185
  84.2 0.0 copy-done
  84.2 0.2 fusion.2.normed
  84.4 4.5 %collective-permute-done.behind = bf16[512,512]{1,0:T(8,128)(2,1)S(1)} collective-permute-done((bf16[512,512]{1,0:T(8,128)(2,1)S(1)}, bf16[512,512]{1,0:T(8,128)(2,1)S(1)}, u32[]{:S(2)}, u32[]{:S(2)}) %collective-permute-start) | collective-permute-done | bytes 524320 | tf_op jit(solution)/shard_map/ppermute | solution.py:189
  88.9 1.5 collective-permute-done.2.ahead
  90.3 1.5 shard_map.70
  91.9 1.9 %collective-permute-start.5 = (bf16[4,3,64,512]{3,2,1,0:T(8,128)(2,1)S(1)}, bf16[4,3,64,512]{3,2,1,0:T(8,128)(2,1)S(1)}, u32[]{:S(2)}, u32[]{:S(2)}) collective-permute-start(bf16[4,3,64,512]{3,2,1,0:T(8,128)(2,1)S(1)} %get-tuple-element.24), channel_id=1, source_target_pairs={{0,16},{16,0},{1,17},{17,1},{2,18},{18,2},{3,19},{19,3},{4,20},{20... | collective-permute-start | bytes 2359304 | tf_op jit(solution)/shard_map/ppermute | solution.py:193
  93.8 3.4 %collective-permute-start.1 = (bf16[256,512]{1,0:T(8,128)(2,1)S(1)}, bf16[256,512]{1,0:T(8,128)(2,1)S(1)}, u32[]{:S(2)}, u32[]{:S(2)}) collective-permute-start(bf16[256,512]{1,0:T(8,128)(2,1)S(1)} %slice.8), channel_id=1, source_target_pairs={{0,1},{1,2},{2,3},{3,4},{4,5},{5,6},{6,7},{7,8},{8,9},{9,10},{10,1... | collective-permute-start | bytes 786440 | tf_op jit(solution)/shard_map/ppermute | solution.py:189
  97.3 3.6 %collective-permute-start.3 = (bf16[256,512]{1,0:T(8,128)(2,1)S(1)}, bf16[256,512]{1,0:T(8,128)(2,1)S(1)}, u32[]{:S(2)}, u32[]{:S(2)}) collective-permute-start(bf16[256,512]{1,0:T(8,128)(2,1)S(1)} %slice.9), channel_id=1, source_target_pairs={{0,15},{1,0},{2,1},{3,2},{4,3},{5,4},{6,5},{7,6},{8,7},{9,8},{10,9... | collective-permute-start | bytes 786440 | tf_op jit(solution)/shard_map/ppermute | solution.py:189
  100.9 4.7 %collective-permute-done.1.far_a = bf16[256,512]{1,0:T(8,128)(2,1)S(1)} collective-permute-done((bf16[256,512]{1,0:T(8,128)(2,1)S(1)}, bf16[256,512]{1,0:T(8,128)(2,1)S(1)}, u32[]{:S(2)}, u32[]{:S(2)}) %collective-permute-start.1) | collective-permute-done | bytes 262176 | tf_op jit(solution)/shard_map/ppermute | solution.py:189
  105.7 2.5 %collective-permute-done.3.far_b = bf16[256,512]{1,0:T(8,128)(2,1)S(1)} collective-permute-done((bf16[256,512]{1,0:T(8,128)(2,1)S(1)}, bf16[256,512]{1,0:T(8,128)(2,1)S(1)}, u32[]{:S(2)}, u32[]{:S(2)}) %collective-permute-start.3) | collective-permute-done | bytes 262176 | tf_op jit(solution)/shard_map/ppermute | solution.py:189
  108.2 0.0 copy-start.1
  108.2 1.0 shard_map.69
  109.1 1.9 %collective-permute-start.4 = (bf16[4,64,512]{2,1,0:T(8,128)(2,1)S(1)}, bf16[4,64,512]{2,1,0:T(8,128)(2,1)S(1)}, u32[]{:S(2)}, u32[]{:S(2)}) collective-permute-start(bf16[4,64,512]{2,1,0:T(8,128)(2,1)S(1)} %get-tuple-element.22), channel_id=1, source_target_pairs={{0,16},{16,0},{1,17},{17,1},{2,18},{18,2},{3,19},{19,3},{4,20},{20... | collective-permute-start | bytes 786440 | tf_op jit(solution)/shard_map/ppermute | solution.py:193
  111.1 0.0 collective-permute-done.5.taken
  111.1 1.6 shard_map.71.placed
  112.7 0.0 copy-done.1
  112.7 0.0 collective-permute-done.4.taken
  112.7 1.3 shard_map.72
  114.0 5.8 %all-to-all-start.2 = ((bf16[32,32,512]{2,1,0:T(8,128)(2,1)}), bf16[32,32,512]{2,1,0:T(8,128)(2,1)}, u32[]{:S(2)}, u32[]{:S(2)}) async-start(bf16[32,32,512]{2,1,0:T(8,128)(2,1)} %bitcast.6), calls=%async_computation.2 | async-start | bytes 2097152 | tf_op jit(solution)/shard_map/all_to_all | solution.py:234
  119.8 0.0 copy-start.2
  119.8 0.9 copy-done.2
  120.8 5.0 %shard_map.73 = (f32[512,512]{1,0:T(8,128)S(1)}, f32[1,512]{1,0:T(1,128)S(1)}) custom-call(s32[2]{0:T(128)S(1)} %pad_add_fusion.where, bf16[512,512]{1,0:T(8,128)(2,1)S(1)} %all_gather.9.own, bf16[512,512]{1,0:T(8,128)(2,1)S(1)} %collective-permute-done.behind, bf16[512,512]{1,0:T(8,128)(2,1)S(1)} %collective-permute-done.2.ahead, ...), custom_call_target="tpu_custom_call" | custom-call | flops 1073741824 | bytes 6291456 | tf_op jit(solution)/shard_map/pallas_call | solution.py:92
  125.8 13.5 %all-gather.1 = f32[4,1,512]{2,1,0:T(1,128)S(1)} all-gather(f32[1,1,512]{2,1,0:T(1,128)S(1)} %bitcast.8), channel_id=1, replica_groups=mesh['chip'=32,'core'=2,'zh'=4,'zl'=4] {'zl'}, dimensions={0}, use_global_device_ids=true | all-gather | bytes 10240 | tf_op jit(solution)/shard_map/all_gather | solution.py:197
  139.4 19.1 %all-gather.2 = f32[4,1,512]{2,1,0:T(1,128)S(1)} all-gather(f32[1,1,512]{2,1,0:T(1,128)S(1)} %bitcast.10), channel_id=2, replica_groups=mesh['chip'=32,'core'=2,'zh'=4,'zl'=4] {'zh'}, dimensions={0}, use_global_device_ids=true | all-gather | bytes 10240 | tf_op jit(solution)/shard_map/all_gather | solution.py:198
  158.4 1.1 subtract_convert_fusion
  159.5 0.0 all-to-all-done.2
  159.5 2.0 %convert_reduce_fusion = f32[32,512]{1,0:T(8,128)} fusion(bf16[32,32,512]{2,1,0:T(8,128)(2,1)} %all-to-all-done.2), kind=kLoop, calls=%fused_computation | loop fusion | flops 1032192 | bytes 1114112 | tf_op jit(solution)/shard_map/reduce_sum | solution.py:235
  (9 shorter events, 0.2 us)
Async XLA Ops:
  0.6 83.5 %copy-start = (bf16[512,512]{1,0:T(8,128)(2,1)S(1)}, bf16[512,512]{1,0:T(8,128)(2,1)}, u32[]{:S(2)}) copy-start(bf16[512,512]{1,0:T(8,128)(2,1)} %x) | copy-start | bytes 1572868
  0.6 77.7 %copy-start.3 = (bf16[512]{0:T(512)(128)(2,1)S(1)}, bf16[512]{0:T(512)(128)(2,1)}, u32[]{:S(2)}) copy-start(bf16[512]{0:T(512)(128)(2,1)} %param.6) | copy-start | bytes 3076
  0.7 27.3 %all-to-all-start = ((bf16[64,8,128]{2,1,0:T(8,128)(2,1)}), bf16[64,8,128]{2,1,0:T(8,128)(2,1)S(1)}, u32[]{:S(2)}, u32[]{:S(2)}) async-start(bf16[64,8,128]{2,1,0:T(8,128)(2,1)} %bitcast.9), calls=%async_computation | async-start | bytes 262144 | tf_op jit(solution)/shard_map/all_to_all | solution.py:204
  59.4 24.7 %all-to-all-start.1 = ((f32[16,1,512]{2,1,0:T(1,128)}), f32[16,1,512]{2,1,0:T(1,128)S(1)}, u32[]{:S(2)}, u32[]{:S(2)}) async-start(f32[16,1,512]{2,1,0:T(1,128)} %broadcast_in_dim.11), calls=%async_computation.1 | async-start | bytes 65536 | tf_op jit(solution)/shard_map/all_to_all | solution.py:185
  71.2 17.7 %collective-permute-start = (bf16[512,512]{1,0:T(8,128)(2,1)S(1)}, bf16[512,512]{1,0:T(8,128)(2,1)S(1)}, u32[]{:S(2)}, u32[]{:S(2)}) collective-permute-start(bf16[512,512]{1,0:T(8,128)(2,1)S(1)} %all_gather.9.own), channel_id=1, source_target_pairs={{0,1},{1,2},{2,3},{3,4},{4,5},{5,6},{6,7},{7,8},{8,9},{9,10},{10,1... | collective-permute-start | bytes 1572872 | tf_op jit(solution)/shard_map/ppermute | solution.py:189
  75.1 15.3 %collective-permute-start.2 = (bf16[512,512]{1,0:T(8,128)(2,1)S(1)}, bf16[512,512]{1,0:T(8,128)(2,1)S(1)}, u32[]{:S(2)}, u32[]{:S(2)}) collective-permute-start(bf16[512,512]{1,0:T(8,128)(2,1)S(1)} %all_gather.9.own), channel_id=1, source_target_pairs={{0,15},{1,0},{2,1},{3,2},{4,3},{5,4},{6,5},{7,6},{8,7},{9,8},{10,9... | collective-permute-start | bytes 1572872 | tf_op jit(solution)/shard_map/ppermute | solution.py:189
  91.9 19.2 %collective-permute-start.5 = (bf16[4,3,64,512]{3,2,1,0:T(8,128)(2,1)S(1)}, bf16[4,3,64,512]{3,2,1,0:T(8,128)(2,1)S(1)}, u32[]{:S(2)}, u32[]{:S(2)}) collective-permute-start(bf16[4,3,64,512]{3,2,1,0:T(8,128)(2,1)S(1)} %get-tuple-element.24), channel_id=1, source_target_pairs={{0,16},{16,0},{1,17},{17,1},{2,18},{18,2},{3,19},{19,3},{4,20},{20... | collective-permute-start | bytes 2359304 | tf_op jit(solution)/shard_map/ppermute | solution.py:193
  93.8 11.8 %collective-permute-start.1 = (bf16[256,512]{1,0:T(8,128)(2,1)S(1)}, bf16[256,512]{1,0:T(8,128)(2,1)S(1)}, u32[]{:S(2)}, u32[]{:S(2)}) collective-permute-start(bf16[256,512]{1,0:T(8,128)(2,1)S(1)} %slice.8), channel_id=1, source_target_pairs={{0,1},{1,2},{2,3},{3,4},{4,5},{5,6},{6,7},{7,8},{8,9},{9,10},{10,1... | collective-permute-start | bytes 786440 | tf_op jit(solution)/shard_map/ppermute | solution.py:189
  97.3 10.9 %collective-permute-start.3 = (bf16[256,512]{1,0:T(8,128)(2,1)S(1)}, bf16[256,512]{1,0:T(8,128)(2,1)S(1)}, u32[]{:S(2)}, u32[]{:S(2)}) collective-permute-start(bf16[256,512]{1,0:T(8,128)(2,1)S(1)} %slice.9), channel_id=1, source_target_pairs={{0,15},{1,0},{2,1},{3,2},{4,3},{5,4},{6,5},{7,6},{8,7},{9,8},{10,9... | collective-permute-start | bytes 786440 | tf_op jit(solution)/shard_map/ppermute | solution.py:189
  108.2 4.5 %copy-start.1 = (bf16[256,512]{1,0:T(8,128)(2,1)}, bf16[256,512]{1,0:T(8,128)(2,1)S(1)}, u32[]{:S(2)}) copy-start(bf16[256,512]{1,0:T(8,128)(2,1)S(1)} %collective-permute-done.3.far_b) | copy-start | bytes 786436
  109.1 3.5 %collective-permute-start.4 = (bf16[4,64,512]{2,1,0:T(8,128)(2,1)S(1)}, bf16[4,64,512]{2,1,0:T(8,128)(2,1)S(1)}, u32[]{:S(2)}, u32[]{:S(2)}) collective-permute-start(bf16[4,64,512]{2,1,0:T(8,128)(2,1)S(1)} %get-tuple-element.22), channel_id=1, source_target_pairs={{0,16},{16,0},{1,17},{17,1},{2,18},{18,2},{3,19},{19,3},{4,20},{20... | collective-permute-start | bytes 786440 | tf_op jit(solution)/shard_map/ppermute | solution.py:193
  114.0 45.5 %all-to-all-start.2 = ((bf16[32,32,512]{2,1,0:T(8,128)(2,1)}), bf16[32,32,512]{2,1,0:T(8,128)(2,1)}, u32[]{:S(2)}, u32[]{:S(2)}) async-start(bf16[32,32,512]{2,1,0:T(8,128)(2,1)} %bitcast.6), calls=%async_computation.2 | async-start | bytes 2097152 | tf_op jit(solution)/shard_map/all_to_all | solution.py:234
  119.8 1.0 copy-start.2

commit v7 on v6

--- a/solution.py
+++ b/solution.py
@@ -69,14 +69,22 @@
     return [pltpu.VMEM((count, COLS, FEAT), jnp.bfloat16), pltpu.SemaphoreType.DMA((count,))]
 
 
-def grad_kernel(where, own, behind, ahead, far_a, far_b, w, x, gain, out, products, rows, sems):
-    pieces = [
-        (ref, COLS * far, shift, far)
-        for ref, shift in ((own, 0), (behind, NEAR - 1), (ahead, 1))
-        for far in range(FAR)
-    ]
+def grad_own_kernel(where, own, w, out, rows, sems):
+    pieces = [(own, COLS * far, 0, far) for far in range(FAR)]
+    out[...] = gradient(where, w, pieces, rows, sems, None)
+
+
+def grad_own(where, own, w_kv):
+    shape = jax.ShapeDtypeStruct((ROWS, FEAT), jnp.float32)
+    flops = 2 * FAR * ROWS * FEAT * COLS
+    hbm = pl.BlockSpec(memory_space=pltpu.HBM)
+    return call(grad_own_kernel, [None, hbm], shape, flops, 8 * ROWS * FEAT, scratch=w_scratch(FAR))(where, own, w_kv)
+
+
+def grad_rest_kernel(where, behind, ahead, far_a, far_b, w, before, x, gain, out, products, rows, sems):
+    pieces = [(ref, COLS * far, shift, far) for ref, shift in ((behind, NEAR - 1), (ahead, 1)) for far in range(FAR)]
     pieces += [(ref, COLS * (far % 2), 2, far) for far, ref in enumerate((far_a, far_a, far_b, far_b))]
-    total = gradient(where, w, pieces, rows, sems, None)
+    total = gradient(where, w, pieces, rows, sems, before[...])
     out[...] = total
     part = x[...].astype(jnp.float32) * gain[...].astype(jnp.float32) * total
     lanes = part[:, :COLS]
@@ -85,13 +93,19 @@
     products[...] = jnp.sum(lanes.T, axis=0, keepdims=True)
 
 
-def grad_step(where, own, behind, ahead, far_a, far_b, w_kv, x, gain):
+def grad_rest(where, behind, ahead, far_a, far_b, w_kv, before, x, gain):
     shapes = [jax.ShapeDtypeStruct((ROWS, FEAT), jnp.float32), jax.ShapeDtypeStruct((1, ROWS), jnp.float32)]
-    flops = 2 * TP * ROWS * FEAT * COLS
+    flops = 6 * FAR * ROWS * FEAT * COLS
     hbm = pl.BlockSpec(memory_space=pltpu.HBM)
     return call(
-        grad_kernel, [None] * 5 + [hbm, None, None], shapes, flops, 24 * ROWS * FEAT, scratch=w_scratch(TP)
-    )(where, own, behind, ahead, far_a, far_b, w_kv, x, gain)
+        grad_rest_kernel,
+        [None] * 4 + [hbm, None, None, None],
+        shapes,
+        flops,
+        24 * ROWS * FEAT,
+        scratch=w_scratch(3 * FAR),
+        aliases={6: 0},
+    )(where, behind, ahead, far_a, far_b, w_kv, before, x, gain)
 
 
 def split_rows(where, term):
@@ -194,8 +208,7 @@
 
 
 def gather_sum(vector):
-    near = jnp.sum(lax.all_gather(vector, "zl", axis=0, tiled=True), axis=0, keepdims=True)
-    return jnp.sum(lax.all_gather(near, "zh", axis=0, tiled=True), axis=0)
+    return jnp.sum(lax.all_gather(vector, Z, axis=0, tiled=True), axis=0)
 
 
 def step(layer_input, gain, w_kv, d_kv, destination):
@@ -226,6 +239,7 @@
 
     keep_near, send_near = weight_near(where, own, behind, ahead, normed)
     taken_near = swap(send_near)
+    grad = grad_own(where, own, w_kv)
     placed = combine_near(where, keep_near, taken_near)
     keep_far, send_far = weight_far(where, far_a, far_b, normed)
     taken_far = swap(send_far)
@@ -234,7 +248,7 @@
     parts = lax.all_to_all(pair.reshape(CHIPS, 32, FEAT), "chip", split_axis=0, concat_axis=0, tiled=True)
     grad_weight = jnp.sum(parts.astype(jnp.float32), axis=0)
 
-    dnormed, products = grad_step(where, own, behind, ahead, far_a, far_b, w_kv, x, gain[None, :])
+    dnormed, products = grad_rest(where, behind, ahead, far_a, far_b, w_kv, grad, x, gain[None, :])
     mean_dot = gather_sum(products) / D
     along = x.astype(jnp.float32) * (inverse**3 * mean_dot)[:, None]
     grad_x = (inverse[:, None] * gain_wide * dnormed - along).astype(jnp.bfloat16)

time: 162 us -> 160 us (0.988)
  blocking collectives: 62.6 us -> 59.4 us
    all_gather x2 -> x1, blocking collectives: 32.6 us -> 29.4 us  [gather_sum(): return jnp.sum(lax.all_gather(vector, Z, axis=0, tiled=True), axis=0)]
    pallas_call x1 -> x2, Pallas kernels: 5.03 us -> 6.61 us  [the longest x1 4.19 us: grad_rest(): call(grad_rest_kernel, [None] * 4 + [hbm, None, None, None], shapes, flop...]
  transfers between devices with their start and end apart: 9 -> 9, of which waited for: 6 -> 6; matrix products, arithmetic and copies ran while one was open for 3% -> 3% of each run, Pallas kernels for 5% -> 6%
where the time goes in v7:
time: 160 us; the launch traced here: 159 us
  blocking collectives  59.4 us (37%)
  starting transfers between devices  52.9 us (33%)
  waiting for transfers between devices  25.9 us (16%)
  Pallas kernels  12.8 us (8%)
  other arithmetic  6.41 us (4%)
    all_gather x1, blocking collectives, step(): own = lax.all_gather(block, 'zh', axis=0, tiled=True)  30 us
    all_gather x1, blocking collectives, gather_sum(): return jnp.sum(lax.all_gather(vector, Z, axis=0, tiled=True), axis=0)  29.4 us
    all_to_all x1, starting transfers between devices, step(): lax.all_to_all(d_kv, ('chip', 'core'), split_axis=0, concat_axis=0, tiled...  17.4 us
    ppermute x4, starting transfers between devices, hop(): return lax.ppermute(array, Z, [(i, (i + step) % TP) for i in range(TP)])  14.1 us
    ppermute x4, waiting for transfers between devices, hop(): return lax.ppermute(array, Z, [(i, (i + step) % TP) for i in range(TP)])  13.2 us
    all_to_all x1, starting transfers between devices, tensor_sum(): lax.all_to_all(spread, Z, split_axis=0, concat_axis=0, tiled=True)  11.8 us
    all_to_all x1, waiting for transfers between devices, step(): lax.all_to_all(d_kv, ('chip', 'core'), split_axis=0, concat_axis=0, tiled...  6.9 us
    all_to_all x1, starting transfers between devices, step(): lax.all_to_all(pair.reshape(CHIPS, 32, FEAT), 'chip', split_axis=0, conca...  5.83 us
  transfers between devices with their start and end apart: 9, of which 6 were waited for; matrix products, arithmetic and copies ran while one was open for 3% of the time, Pallas kernels for 6%

profile of v7, /device:TPU:2, one launch (start us, length us, event | category | flops | bytes accessed | tf_op | source)
XLA Modules:
  0.0 159.0 jit_solution(12568654419680161324)
XLA Ops:
  0.6 0.0 copy-start
  0.6 0.0 copy-start.3
  0.7 17.4 %all-to-all-start = ((bf16[64,8,128]{2,1,0:T(8,128)(2,1)}), bf16[64,8,128]{2,1,0:T(8,128)(2,1)S(1)}, u32[]{:S(2)}, u32[]{:S(2)}) async-start(bf16[64,8,128]{2,1,0:T(8,128)(2,1)} %bitcast.8), calls=%async_computation | async-start | bytes 262144 | tf_op jit(solution)/shard_map/all_to_all | solution.py:217
  18.0 0.9 convert_reduce_fusion.1
  18.9 0.7 add_select_fusion
  19.6 1.2 fusion
  20.9 0.1 pad_add_fusion.where
  20.9 0.1 fusion.3.onehot
  21.1 6.9 %all-to-all-done = bf16[64,8,128]{2,1,0:T(8,128)(2,1)S(1)} async-done(((bf16[64,8,128]{2,1,0:T(8,128)(2,1)}), bf16[64,8,128]{2,1,0:T(8,128)(2,1)S(1)}, u32[]{:S(2)}, u32[]{:S(2)}) %all-to-all-start) | async-done | bytes 131104 | tf_op jit(solution)/shard_map/all_to_all | solution.py:217
  28.0 0.8 shard_map.68
  28.8 30.0 %all_gather.6.own = bf16[512,512]{1,0:T(8,128)(2,1)S(1)} all-gather(bf16[128,512]{1,0:T(8,128)(2,1)S(1)} %shard_map.68), channel_id=1, replica_groups=mesh['chip'=32,'core'=2,'zh'=4,'zl'=4] {'zh'}, dimensions={0}, use_global_device_ids=true | all-gather | bytes 655360 | tf_op jit(solution)/shard_map/all_gather | solution.py:231
  58.8 0.6 broadcast_in_dim.9
  59.4 11.8 %all-to-all-start.1 = ((f32[16,1,512]{2,1,0:T(1,128)}), f32[16,1,512]{2,1,0:T(1,128)S(1)}, u32[]{:S(2)}, u32[]{:S(2)}) async-start(f32[16,1,512]{2,1,0:T(1,128)} %broadcast_in_dim.9), calls=%async_computation.1 | async-start | bytes 65536 | tf_op jit(solution)/shard_map/all_to_all | solution.py:199
  71.2 3.8 %collective-permute-start = (bf16[512,512]{1,0:T(8,128)(2,1)S(1)}, bf16[512,512]{1,0:T(8,128)(2,1)S(1)}, u32[]{:S(2)}, u32[]{:S(2)}) collective-permute-start(bf16[512,512]{1,0:T(8,128)(2,1)S(1)} %all_gather.6.own), channel_id=1, source_target_pairs={{0,1},{1,2},{2,3},{3,4},{4,5},{5,6},{6,7},{7,8},{8,9},{9,10},{10,1... | collective-permute-start | bytes 1572872 | tf_op jit(solution)/shard_map/ppermute | solution.py:203
  75.1 3.2 %collective-permute-start.2 = (bf16[512,512]{1,0:T(8,128)(2,1)S(1)}, bf16[512,512]{1,0:T(8,128)(2,1)S(1)}, u32[]{:S(2)}, u32[]{:S(2)}) collective-permute-start(bf16[512,512]{1,0:T(8,128)(2,1)S(1)} %all_gather.6.own), channel_id=1, source_target_pairs={{0,15},{1,0},{2,1},{3,2},{4,3},{5,4},{6,5},{7,6},{8,7},{9,8},{10,9... | collective-permute-start | bytes 1572872 | tf_op jit(solution)/shard_map/ppermute | solution.py:203
  78.3 0.0 copy-done.3
  78.3 5.8 %all-to-all-done.1 = f32[16,1,512]{2,1,0:T(1,128)S(1)} async-done(((f32[16,1,512]{2,1,0:T(1,128)}), f32[16,1,512]{2,1,0:T(1,128)S(1)}, u32[]{:S(2)}, u32[]{:S(2)}) %all-to-all-start.1) | async-done | bytes 32800 | tf_op jit(solution)/shard_map/all_to_all | solution.py:199
  84.2 0.0 copy-done
  84.2 0.2 fusion.2.normed
  84.4 4.5 %collective-permute-done.behind = bf16[512,512]{1,0:T(8,128)(2,1)S(1)} collective-permute-done((bf16[512,512]{1,0:T(8,128)(2,1)S(1)}, bf16[512,512]{1,0:T(8,128)(2,1)S(1)}, u32[]{:S(2)}, u32[]{:S(2)}) %collective-permute-start) | collective-permute-done | bytes 524320 | tf_op jit(solution)/shard_map/ppermute | solution.py:203
  88.9 1.5 collective-permute-done.2.ahead
  90.3 1.5 shard_map.70
  91.9 1.9 %collective-permute-start.5 = (bf16[4,3,64,512]{3,2,1,0:T(8,128)(2,1)S(1)}, bf16[4,3,64,512]{3,2,1,0:T(8,128)(2,1)S(1)}, u32[]{:S(2)}, u32[]{:S(2)}) collective-permute-start(bf16[4,3,64,512]{3,2,1,0:T(8,128)(2,1)S(1)} %get-tuple-element.24), channel_id=1, source_target_pairs={{0,16},{16,0},{1,17},{17,1},{2,18},{18,2},{3,19},{19,3},{4,20},{20... | collective-permute-start | bytes 2359304 | tf_op jit(solution)/shard_map/ppermute | solution.py:207
  93.8 3.4 %collective-permute-start.1 = (bf16[256,512]{1,0:T(8,128)(2,1)S(1)}, bf16[256,512]{1,0:T(8,128)(2,1)S(1)}, u32[]{:S(2)}, u32[]{:S(2)}) collective-permute-start(bf16[256,512]{1,0:T(8,128)(2,1)S(1)} %slice.8), channel_id=1, source_target_pairs={{0,1},{1,2},{2,3},{3,4},{4,5},{5,6},{6,7},{7,8},{8,9},{9,10},{10,1... | collective-permute-start | bytes 786440 | tf_op jit(solution)/shard_map/ppermute | solution.py:203
  97.3 3.6 %collective-permute-start.3 = (bf16[256,512]{1,0:T(8,128)(2,1)S(1)}, bf16[256,512]{1,0:T(8,128)(2,1)S(1)}, u32[]{:S(2)}, u32[]{:S(2)}) collective-permute-start(bf16[256,512]{1,0:T(8,128)(2,1)S(1)} %slice.9), channel_id=1, source_target_pairs={{0,15},{1,0},{2,1},{3,2},{4,3},{5,4},{6,5},{7,6},{8,7},{9,8},{10,9... | collective-permute-start | bytes 786440 | tf_op jit(solution)/shard_map/ppermute | solution.py:203
  100.9 4.7 %collective-permute-done.1.far_a = bf16[256,512]{1,0:T(8,128)(2,1)S(1)} collective-permute-done((bf16[256,512]{1,0:T(8,128)(2,1)S(1)}, bf16[256,512]{1,0:T(8,128)(2,1)S(1)}, u32[]{:S(2)}, u32[]{:S(2)}) %collective-permute-start.1) | collective-permute-done | bytes 262176 | tf_op jit(solution)/shard_map/ppermute | solution.py:203
  105.7 2.5 %collective-permute-done.3.far_b = bf16[256,512]{1,0:T(8,128)(2,1)S(1)} collective-permute-done((bf16[256,512]{1,0:T(8,128)(2,1)S(1)}, bf16[256,512]{1,0:T(8,128)(2,1)S(1)}, u32[]{:S(2)}, u32[]{:S(2)}) %collective-permute-start.3) | collective-permute-done | bytes 262176 | tf_op jit(solution)/shard_map/ppermute | solution.py:203
  108.2 0.0 copy-start.1
  108.2 1.0 shard_map.69
  109.1 1.9 %collective-permute-start.4 = (bf16[4,64,512]{2,1,0:T(8,128)(2,1)S(1)}, bf16[4,64,512]{2,1,0:T(8,128)(2,1)S(1)}, u32[]{:S(2)}, u32[]{:S(2)}) collective-permute-start(bf16[4,64,512]{2,1,0:T(8,128)(2,1)S(1)} %get-tuple-element.22), channel_id=1, source_target_pairs={{0,16},{16,0},{1,17},{17,1},{2,18},{18,2},{3,19},{19,3},{4,20},{20... | collective-permute-start | bytes 786440 | tf_op jit(solution)/shard_map/ppermute | solution.py:207
  111.1 0.0 collective-permute-done.5.taken
  111.1 1.6 shard_map.71.placed
  112.7 0.0 copy-done.1
  112.7 0.0 collective-permute-done.4.taken
  112.7 1.3 shard_map.72
  114.0 5.8 %all-to-all-start.2 = ((bf16[32,32,512]{2,1,0:T(8,128)(2,1)}), bf16[32,32,512]{2,1,0:T(8,128)(2,1)}, u32[]{:S(2)}, u32[]{:S(2)}) async-start(bf16[32,32,512]{2,1,0:T(8,128)(2,1)} %bitcast.5), calls=%async_computation.2 | async-start | bytes 2097152 | tf_op jit(solution)/shard_map/all_to_all | solution.py:248
  119.8 0.0 copy-start.2
  119.8 2.4 %shard_map.73.before = f32[512,512]{1,0:T(8,128)S(1)} custom-call(s32[2]{0:T(128)S(1)} %pad_add_fusion.where, bf16[512,512]{1,0:T(8,128)(2,1)S(1)} %all_gather.6.own, bf16[2048,512]{1,0:T(8,128)(2,1)} %w.3), custom_call_target="tpu_custom_call" | custom-call | flops 268435456 | bytes 2097152 | tf_op jit(solution)/shard_map/pallas_call | solution.py:81
  122.3 0.0 copy-done.2
  122.3 4.2 %shard_map.74 = (f32[512,512]{1,0:T(8,128)S(1)}, f32[1,512]{1,0:T(1,128)S(1)}) custom-call(s32[2]{0:T(128)S(1)} %pad_add_fusion.where, bf16[512,512]{1,0:T(8,128)(2,1)S(1)} %collective-permute-done.behind, bf16[512,512]{1,0:T(8,128)(2,1)S(1)} %collective-permute-done.2.ahead, ...), custom_call_target="tpu_custom_call", output_to_operand_aliasing={{0}: (6, {})} | custom-call | flops 805306368 | bytes 6291456 | tf_op jit(solution)/shard_map/pallas_call | solution.py:100
  126.5 29.4 %all-gather = f32[16,1,512]{2,1,0:T(1,128)S(1)} all-gather(f32[1,1,512]{2,1,0:T(1,128)S(1)} %bitcast.7), channel_id=1, replica_groups=mesh['chip'=32,'core'=2,'zh'=4,'zl'=4] {'zh','zl'}, dimensions={0}, use_global_device_ids=true | all-gather | bytes 34816 | tf_op jit(solution)/shard_map/all_gather | solution.py:211
  155.9 1.1 subtract_convert_fusion
  156.9 0.0 all-to-all-done.2
  156.9 2.0 %convert_reduce_fusion = f32[32,512]{1,0:T(8,128)} fusion(bf16[32,32,512]{2,1,0:T(8,128)(2,1)} %all-to-all-done.2), kind=kLoop, calls=%fused_computation | loop fusion | flops 1032192 | bytes 1114112 | tf_op jit(solution)/shard_map/reduce_sum | solution.py:249
  (8 shorter events, 0.1 us)
Async XLA Ops:
  0.6 83.5 %copy-start = (bf16[512,512]{1,0:T(8,128)(2,1)S(1)}, bf16[512,512]{1,0:T(8,128)(2,1)}, u32[]{:S(2)}) copy-start(bf16[512,512]{1,0:T(8,128)(2,1)} %x) | copy-start | bytes 1572868
  0.6 77.7 %copy-start.3 = (bf16[512]{0:T(512)(128)(2,1)S(1)}, bf16[512]{0:T(512)(128)(2,1)}, u32[]{:S(2)}) copy-start(bf16[512]{0:T(512)(128)(2,1)} %param.6) | copy-start | bytes 3076
  0.7 27.3 %all-to-all-start = ((bf16[64,8,128]{2,1,0:T(8,128)(2,1)}), bf16[64,8,128]{2,1,0:T(8,128)(2,1)S(1)}, u32[]{:S(2)}, u32[]{:S(2)}) async-start(bf16[64,8,128]{2,1,0:T(8,128)(2,1)} %bitcast.8), calls=%async_computation | async-start | bytes 262144 | tf_op jit(solution)/shard_map/all_to_all | solution.py:217
  59.4 24.7 %all-to-all-start.1 = ((f32[16,1,512]{2,1,0:T(1,128)}), f32[16,1,512]{2,1,0:T(1,128)S(1)}, u32[]{:S(2)}, u32[]{:S(2)}) async-start(f32[16,1,512]{2,1,0:T(1,128)} %broadcast_in_dim.9), calls=%async_computation.1 | async-start | bytes 65536 | tf_op jit(solution)/shard_map/all_to_all | solution.py:199
  71.2 17.7 %collective-permute-start = (bf16[512,512]{1,0:T(8,128)(2,1)S(1)}, bf16[512,512]{1,0:T(8,128)(2,1)S(1)}, u32[]{:S(2)}, u32[]{:S(2)}) collective-permute-start(bf16[512,512]{1,0:T(8,128)(2,1)S(1)} %all_gather.6.own), channel_id=1, source_target_pairs={{0,1},{1,2},{2,3},{3,4},{4,5},{5,6},{6,7},{7,8},{8,9},{9,10},{10,1... | collective-permute-start | bytes 1572872 | tf_op jit(solution)/shard_map/ppermute | solution.py:203
  75.1 15.3 %collective-permute-start.2 = (bf16[512,512]{1,0:T(8,128)(2,1)S(1)}, bf16[512,512]{1,0:T(8,128)(2,1)S(1)}, u32[]{:S(2)}, u32[]{:S(2)}) collective-permute-start(bf16[512,512]{1,0:T(8,128)(2,1)S(1)} %all_gather.6.own), channel_id=1, source_target_pairs={{0,15},{1,0},{2,1},{3,2},{4,3},{5,4},{6,5},{7,6},{8,7},{9,8},{10,9... | collective-permute-start | bytes 1572872 | tf_op jit(solution)/shard_map/ppermute | solution.py:203
  91.9 19.2 %collective-permute-start.5 = (bf16[4,3,64,512]{3,2,1,0:T(8,128)(2,1)S(1)}, bf16[4,3,64,512]{3,2,1,0:T(8,128)(2,1)S(1)}, u32[]{:S(2)}, u32[]{:S(2)}) collective-permute-start(bf16[4,3,64,512]{3,2,1,0:T(8,128)(2,1)S(1)} %get-tuple-element.24), channel_id=1, source_target_pairs={{0,16},{16,0},{1,17},{17,1},{2,18},{18,2},{3,19},{19,3},{4,20},{20... | collective-permute-start | bytes 2359304 | tf_op jit(solution)/shard_map/ppermute | solution.py:207
  93.8 11.8 %collective-permute-start.1 = (bf16[256,512]{1,0:T(8,128)(2,1)S(1)}, bf16[256,512]{1,0:T(8,128)(2,1)S(1)}, u32[]{:S(2)}, u32[]{:S(2)}) collective-permute-start(bf16[256,512]{1,0:T(8,128)(2,1)S(1)} %slice.8), channel_id=1, source_target_pairs={{0,1},{1,2},{2,3},{3,4},{4,5},{5,6},{6,7},{7,8},{8,9},{9,10},{10,1... | collective-permute-start | bytes 786440 | tf_op jit(solution)/shard_map/ppermute | solution.py:203
  97.3 10.9 %collective-permute-start.3 = (bf16[256,512]{1,0:T(8,128)(2,1)S(1)}, bf16[256,512]{1,0:T(8,128)(2,1)S(1)}, u32[]{:S(2)}, u32[]{:S(2)}) collective-permute-start(bf16[256,512]{1,0:T(8,128)(2,1)S(1)} %slice.9), channel_id=1, source_target_pairs={{0,15},{1,0},{2,1},{3,2},{4,3},{5,4},{6,5},{7,6},{8,7},{9,8},{10,9... | collective-permute-start | bytes 786440 | tf_op jit(solution)/shard_map/ppermute | solution.py:203
  108.2 4.5 %copy-start.1 = (bf16[256,512]{1,0:T(8,128)(2,1)}, bf16[256,512]{1,0:T(8,128)(2,1)S(1)}, u32[]{:S(2)}) copy-start(bf16[256,512]{1,0:T(8,128)(2,1)S(1)} %collective-permute-done.3.far_b) | copy-start | bytes 786436
  109.1 3.5 %collective-permute-start.4 = (bf16[4,64,512]{2,1,0:T(8,128)(2,1)S(1)}, bf16[4,64,512]{2,1,0:T(8,128)(2,1)S(1)}, u32[]{:S(2)}, u32[]{:S(2)}) collective-permute-start(bf16[4,64,512]{2,1,0:T(8,128)(2,1)S(1)} %get-tuple-element.22), channel_id=1, source_target_pairs={{0,16},{16,0},{1,17},{17,1},{2,18},{18,2},{3,19},{19,3},{4,20},{20... | collective-permute-start | bytes 786440 | tf_op jit(solution)/shard_map/ppermute | solution.py:207
  114.0 43.0 %all-to-all-start.2 = ((bf16[32,32,512]{2,1,0:T(8,128)(2,1)}), bf16[32,32,512]{2,1,0:T(8,128)(2,1)}, u32[]{:S(2)}, u32[]{:S(2)}) async-start(bf16[32,32,512]{2,1,0:T(8,128)(2,1)} %bitcast.5), calls=%async_computation.2 | async-start | bytes 2097152 | tf_op jit(solution)/shard_map/all_to_all | solution.py:248
  119.8 2.4 %copy-start.2 = (bf16[256,512]{1,0:T(8,128)(2,1)S(1)}, bf16[256,512]{1,0:T(8,128)(2,1)}, u32[]{:S(2)}) copy-start(bf16[256,512]{1,0:T(8,128)(2,1)} %copy-done.1) | copy-start | bytes 786436

commit v8 on v5

--- a/solution.py
+++ b/solution.py
@@ -15,7 +15,6 @@
 NEAR = 4
 TP = FAR * NEAR
 CHIPS = 32
-HALF = FAR * COLS // 2
 GRANT = 24 * 1024 * 1024
 Z = ("zh", "zl")
 TRANSPOSED = (((0,), (0,)), ((), ()))
@@ -46,36 +45,31 @@
     return call(place_kernel, [None] * 2, shape, 2 * ROWS * ROWS * COLS, ROWS * ROWS * 3)(where, received, onehot)
 
 
-def fetch(where, w, pieces, rows, sems):
+def gradient(where, w, groups, rows, sems, total):
     copies = []
-    for i, (_, _, shift, far) in enumerate(pieces):
-        owner = far * NEAR + lax.rem(where[0] + shift, NEAR)
-        source = w.at[pl.ds(pl.multiple_of(owner * COLS, COLS), COLS), :]
-        copies.append(pltpu.make_async_copy(source, rows.at[i], sems.at[i]))
-        copies[-1].start()
-    return copies
-
-
-def gradient(where, w, pieces, rows, sems, total):
-    copies = fetch(where, w, pieces, rows, sems)
-    for i, (ref, at, _, _) in enumerate(pieces):
-        copies[i].wait()
-        term = lax.dot_general(ref[at : at + COLS, :], rows[i], TRANSPOSED, preferred_element_type=jnp.float32)
+    for group, (_, shift) in enumerate(groups):
+        for far in range(FAR):
+            i = FAR * group + far
+            owner = far * NEAR + lax.rem(where[0] + shift, NEAR)
+            source = w.at[pl.ds(pl.multiple_of(owner * COLS, COLS), COLS), :]
+            copies.append(pltpu.make_async_copy(source, rows.at[COLS * i : COLS * (i + 1), :], sems.at[i]))
+            copies[-1].start()
+    for group, (ref, _) in enumerate(groups):
+        for far in range(FAR):
+            copies[FAR * group + far].wait()
+        piece = rows[FAR * COLS * group : FAR * COLS * (group + 1), :]
+        term = lax.dot_general(ref[...], piece, TRANSPOSED, preferred_element_type=jnp.float32)
         total = term if total is None else total + term
     return total
 
 
+def w_scratch(groups):
+    count = FAR * groups
+    return [pltpu.VMEM((count * COLS, FEAT), jnp.bfloat16), pltpu.SemaphoreType.DMA((count,))]
+
+
 def grad_near_kernel(where, own, behind, ahead, w, out, rows, sems):
-    pieces = [
-        (ref, COLS * far, shift, far)
-        for ref, shift in ((own, 0), (behind, NEAR - 1), (ahead, 1))
-        for far in range(FAR)
-    ]
-    out[...] = gradient(where, w, pieces, rows, sems, None)
-
-
-def w_scratch(count):
-    return [pltpu.VMEM((count, COLS, FEAT), jnp.bfloat16), pltpu.SemaphoreType.DMA((count,))]
+    out[...] = gradient(where, w, [(own, 0), (behind, NEAR - 1), (ahead, 1)], rows, sems, None)
 
 
 def grad_near(where, own, behind, ahead, w_kv):
@@ -83,13 +77,12 @@
     flops = 6 * FAR * ROWS * FEAT * COLS
     hbm = pl.BlockSpec(memory_space=pltpu.HBM)
     return call(
-        grad_near_kernel, [None] * 3 + [hbm], shape, flops, 14 * ROWS * FEAT, scratch=w_scratch(3 * FAR)
+        grad_near_kernel, [None] * 3 + [hbm], shape, flops, 14 * ROWS * FEAT, scratch=w_scratch(3)
     )(where, own, behind, ahead, w_kv)
 
 
-def grad_far_kernel(where, far_a, far_b, w, before, x, gain, out, products, rows, sems):
-    pieces = [(ref, COLS * (far % 2), 2, far) for far, ref in enumerate((far_a, far_a, far_b, far_b))]
-    total = gradient(where, w, pieces, rows, sems, before[...])
+def grad_far_kernel(where, far, w, before, x, gain, out, products, rows, sems):
+    total = gradient(where, w, [(far, 2)], rows, sems, before[...])
     out[...] = total
     part = x[...].astype(jnp.float32) * gain[...].astype(jnp.float32) * total
     lanes = part[:, :COLS]
@@ -98,13 +91,19 @@
     products[...] = jnp.sum(lanes.T, axis=0, keepdims=True)
 
 
-def grad_far(where, far_a, far_b, w_kv, before, x, gain):
+def grad_far(where, far, w_kv, before, x, gain):
     shapes = [jax.ShapeDtypeStruct((ROWS, FEAT), jnp.float32), jax.ShapeDtypeStruct((1, ROWS), jnp.float32)]
     flops = 2 * FAR * ROWS * FEAT * COLS
     hbm = pl.BlockSpec(memory_space=pltpu.HBM)
     return call(
-        grad_far_kernel, [None, None, hbm, None, None, None], shapes, flops, 14 * ROWS * FEAT, scratch=w_scratch(FAR)
-    )(where, far_a, far_b, w_kv, before, x, gain)
+        grad_far_kernel,
+        [None, hbm, None, None, None],
+        shapes,
+        flops,
+        14 * ROWS * FEAT,
+        scratch=w_scratch(1),
+        aliases={3: 0},
+    )(where, far, w_kv, before, x, gain)
 
 
 def split_rows(where, term):
@@ -129,19 +128,18 @@
     return call(weight_near_kernel, [None] * 4, shapes, flops, 18 * ROWS * FEAT)(where, own, behind, ahead, normed)
 
 
-def weight_far_kernel(where, far_a, far_b, normed, keep, send):
+def weight_far_kernel(where, blocks, normed, keep, send):
     for far in range(FAR):
-        ref, at = (far_a, far_b)[far // 2], COLS * (far % 2)
-        term = jnp.dot(ref[at : at + COLS, :], normed[...], preferred_element_type=jnp.float32)
+        term = jnp.dot(blocks[COLS * far : COLS * (far + 1), :], normed[...], preferred_element_type=jnp.float32)
         kept, sent = split_rows(where, term)
         keep[far] = kept
         send[far] = sent
 
 
-def weight_far(where, far_a, far_b, normed):
+def weight_far(where, blocks, normed):
     shapes = [jax.ShapeDtypeStruct((FAR, COLS // 2, FEAT), kind) for kind in (jnp.float32, jnp.bfloat16)]
     flops = 2 * FAR * ROWS * FEAT * COLS
-    return call(weight_far_kernel, [None] * 3, shapes, flops, 8 * ROWS * FEAT)(where, far_a, far_b, normed)
+    return call(weight_far_kernel, [None] * 2, shapes, flops, 8 * ROWS * FEAT)(where, blocks, normed)
 
 
 def combine_near_kernel(where, keep, taken, out, total, sems):
@@ -233,21 +231,20 @@
     ahead = hop(own, -1)
     inverse = lax.rsqrt(tensor_sum(squares) / D + EPS)
     normed = (values * inverse[:, None] * gain_wide).astype(jnp.bfloat16)
-    far_a = hop(behind[:HALF], 1)
-    far_b = hop(ahead[HALF:], -1)
-
-    grad = grad_near(where, own, behind, ahead, w_kv)
+    far = hop(behind, 1)
+
     keep_near, send_near = weight_near(where, own, behind, ahead, normed)
     taken_near = swap(send_near)
+    grad = grad_near(where, own, behind, ahead, w_kv)
     placed = combine_near(where, keep_near, taken_near)
-    keep_far, send_far = weight_far(where, far_a, far_b, normed)
+    keep_far, send_far = weight_far(where, far, normed)
     taken_far = swap(send_far)
     pair = combine_far(where, keep_far, taken_far, placed)
     pair, x, inverse = lax.optimization_barrier((pair, layer_input, inverse))
     parts = lax.all_to_all(pair.reshape(CHIPS, 32, FEAT), "chip", split_axis=0, concat_axis=0, tiled=True)
     grad_weight = jnp.sum(parts.astype(jnp.float32), axis=0)
 
-    dnormed, products = grad_far(where, far_a, far_b, w_kv, grad, x, gain[None, :])
+    dnormed, products = grad_far(where, far, w_kv, grad, x, gain[None, :])
     mean_dot = gather_sum(products) / D
     along = x.astype(jnp.float32) * (inverse**3 * mean_dot)[:, None]
     grad_x = (inverse[:, None] * gain_wide * dnormed - along).astype(jnp.bfloat16)

time: 160 us -> 154 us (0.963)
  starting transfers between devices: 52.9 us -> 48.1 us
  blocking collectives: 59.4 us -> 57 us
  waiting for transfers between devices: 25.9 us -> 27.6 us
    ppermute x4 -> x3, starting transfers between devices: 14.1 us -> 9.35 us  [hop(): return lax.ppermute(array, Z, [(i, (i + step) % TP) for i in range(TP)])]
    all_gather x1, blocking collectives: 29.4 us -> 27 us  [gather_sum(): return jnp.sum(lax.all_gather(vector, Z, axis=0, tiled=True), axis=0)]
    ppermute x4 -> x3, waiting for transfers between devices: 13.2 us -> 14.9 us  [hop(): return lax.ppermute(array, Z, [(i, (i + step) % TP) for i in range(TP)])]
  transfers between devices with their start and end apart: 9 -> 8, of which waited for: 6 -> 4; matrix products, arithmetic and copies ran while one was open for 3% -> 3% of each run, Pallas kernels for 6% -> 6%
where the time goes in v8:
time: 154 us; the launch traced here: 153 us
  blocking collectives  57 us (37%)
  starting transfers between devices  48.1 us (31%)
  waiting for transfers between devices  27.6 us (18%)
  Pallas kernels  11.4 us (7%)
  other arithmetic  6.41 us (4%)
  local copies, waits for them, and re-layouts  1.69 us (1%)
    all_gather x1, blocking collectives, step(): own = lax.all_gather(block, 'zh', axis=0, tiled=True)  30 us
    all_gather x1, blocking collectives, gather_sum(): return jnp.sum(lax.all_gather(vector, Z, axis=0, tiled=True), axis=0)  27 us
    all_to_all x1, starting transfers between devices, step(): lax.all_to_all(d_kv, ('chip', 'core'), split_axis=0, concat_axis=0, tiled...  17.4 us
    ppermute x3, waiting for transfers between devices, hop(): return lax.ppermute(array, Z, [(i, (i + step) % TP) for i in range(TP)])  14.9 us
    all_to_all x1, starting transfers between devices, tensor_sum(): lax.all_to_all(spread, Z, split_axis=0, concat_axis=0, tiled=True)  11.8 us
    ppermute x3, starting transfers between devices, hop(): return lax.ppermute(array, Z, [(i, (i + step) % TP) for i in range(TP)])  9.35 us
    all_to_all x1, waiting for transfers between devices, step(): lax.all_to_all(d_kv, ('chip', 'core'), split_axis=0, concat_axis=0, tiled...  6.9 us
    all_to_all x1, starting transfers between devices, step(): lax.all_to_all(pair.reshape(CHIPS, 32, FEAT), 'chip', split_axis=0, conca...  5.81 us
  transfers between devices with their start and end apart: 8, of which 4 were waited for; matrix products, arithmetic and copies ran while one was open for 3% of the time, Pallas kernels for 6%

profile of v8, /device:TPU:2, one launch (start us, length us, event | category | flops | bytes accessed | tf_op | source)
XLA Modules:
  0.0 153.2 jit_solution(16486622891414436355)
XLA Ops:
  0.6 0.0 copy-start
  0.6 0.0 copy-start.3
  0.7 17.4 %all-to-all-start = ((bf16[64,8,128]{2,1,0:T(8,128)(2,1)}), bf16[64,8,128]{2,1,0:T(8,128)(2,1)S(1)}, u32[]{:S(2)}, u32[]{:S(2)}) async-start(bf16[64,8,128]{2,1,0:T(8,128)(2,1)} %bitcast.8), calls=%async_computation | async-start | bytes 262144 | tf_op jit(solution)/shard_map/all_to_all | solution.py:214
  18.0 0.9 convert_reduce_fusion.1
  18.9 0.7 add_select_fusion
  19.6 1.2 fusion
  20.9 0.1 pad_add_fusion.where
  20.9 0.1 fusion.3.onehot
  21.1 6.9 %all-to-all-done = bf16[64,8,128]{2,1,0:T(8,128)(2,1)S(1)} async-done(((bf16[64,8,128]{2,1,0:T(8,128)(2,1)}), bf16[64,8,128]{2,1,0:T(8,128)(2,1)S(1)}, u32[]{:S(2)}, u32[]{:S(2)}) %all-to-all-start) | async-done | bytes 131104 | tf_op jit(solution)/shard_map/all_to_all | solution.py:214
  28.0 0.8 shard_map.68
  28.8 30.0 %all_gather.6.own = bf16[512,512]{1,0:T(8,128)(2,1)S(1)} all-gather(bf16[128,512]{1,0:T(8,128)(2,1)S(1)} %shard_map.68), channel_id=1, replica_groups=mesh['chip'=32,'core'=2,'zh'=4,'zl'=4] {'zh'}, dimensions={0}, use_global_device_ids=true | all-gather | bytes 655360 | tf_op jit(solution)/shard_map/all_gather | solution.py:228
  58.8 0.6 broadcast_in_dim.9
  59.4 11.8 %all-to-all-start.1 = ((f32[16,1,512]{2,1,0:T(1,128)}), f32[16,1,512]{2,1,0:T(1,128)S(1)}, u32[]{:S(2)}, u32[]{:S(2)}) async-start(f32[16,1,512]{2,1,0:T(1,128)} %broadcast_in_dim.9), calls=%async_computation.1 | async-start | bytes 65536 | tf_op jit(solution)/shard_map/all_to_all | solution.py:196
  71.2 3.8 %collective-permute-start = (bf16[512,512]{1,0:T(8,128)(2,1)S(1)}, bf16[512,512]{1,0:T(8,128)(2,1)S(1)}, u32[]{:S(2)}, u32[]{:S(2)}) collective-permute-start(bf16[512,512]{1,0:T(8,128)(2,1)S(1)} %all_gather.6.own), channel_id=1, source_target_pairs={{0,1},{1,2},{2,3},{3,4},{4,5},{5,6},{6,7},{7,8},{8,9},{9,10},{10,1... | collective-permute-start | bytes 1572872 | tf_op jit(solution)/shard_map/ppermute | solution.py:200
  75.1 3.2 %collective-permute-start.3 = (bf16[512,512]{1,0:T(8,128)(2,1)S(1)}, bf16[512,512]{1,0:T(8,128)(2,1)S(1)}, u32[]{:S(2)}, u32[]{:S(2)}) collective-permute-start(bf16[512,512]{1,0:T(8,128)(2,1)S(1)} %all_gather.6.own), channel_id=1, source_target_pairs={{0,15},{1,0},{2,1},{3,2},{4,3},{5,4},{6,5},{7,6},{8,7},{9,8},{10,9... | collective-permute-start | bytes 1572872 | tf_op jit(solution)/shard_map/ppermute | solution.py:200
  78.3 0.0 copy-done.3
  78.3 5.8 %all-to-all-done.1 = f32[16,1,512]{2,1,0:T(1,128)S(1)} async-done(((f32[16,1,512]{2,1,0:T(1,128)}), f32[16,1,512]{2,1,0:T(1,128)S(1)}, u32[]{:S(2)}, u32[]{:S(2)}) %all-to-all-start.1) | async-done | bytes 32800 | tf_op jit(solution)/shard_map/all_to_all | solution.py:196
  84.2 0.0 copy-done
  84.2 0.2 fusion.2.normed
  84.4 4.5 %collective-permute-done.behind = bf16[512,512]{1,0:T(8,128)(2,1)S(1)} collective-permute-done((bf16[512,512]{1,0:T(8,128)(2,1)S(1)}, bf16[512,512]{1,0:T(8,128)(2,1)S(1)}, u32[]{:S(2)}, u32[]{:S(2)}) %collective-permute-start) | collective-permute-done | bytes 524320 | tf_op jit(solution)/shard_map/ppermute | solution.py:200
  88.9 2.3 %collective-permute-start.1 = (bf16[512,512]{1,0:T(8,128)(2,1)S(1)}, bf16[512,512]{1,0:T(8,128)(2,1)S(1)}, u32[]{:S(2)}, u32[]{:S(2)}) collective-permute-start(bf16[512,512]{1,0:T(8,128)(2,1)S(1)} %collective-permute-done.behind), channel_id=1, source_target_pairs={{0,1},{1,2},{2,3},{3,4},{4,5},{5,6},{6,7},{7,8},{8,9},{9,10},{10,1... | collective-permute-start | bytes 1572872 | tf_op jit(solution)/shard_map/ppermute | solution.py:200
  91.2 0.0 collective-permute-done.3.ahead
  91.2 0.0 copy-start.1
  91.2 1.5 %shard_map.70 = (f32[4,3,64,512]{3,2,1,0:T(8,128)S(1)}, bf16[4,3,64,512]{3,2,1,0:T(8,128)(2,1)S(1)}) custom-call(s32[2]{0:T(128)S(1)} %pad_add_fusion.where, bf16[512,512]{1,0:T(8,128)(2,1)S(1)} %all_gather.6.own, bf16[512,512]{1,0:T(8,128)(2,1)S(1)} %collective-permute-done.behind, bf16[512,512]{1,0:T(8,128)(2,1)S(1)} %collective-permute-done.3.ahead, ...), custom_call_target="tpu_custom_call" | custom-call | flops 805306368 | bytes 4718592 | tf_op jit(solution)/shard_map/pallas_call | solution.py:128
  92.8 1.9 %collective-permute-start.4 = (bf16[4,3,64,512]{3,2,1,0:T(8,128)(2,1)S(1)}, bf16[4,3,64,512]{3,2,1,0:T(8,128)(2,1)S(1)}, u32[]{:S(2)}, u32[]{:S(2)}) collective-permute-start(bf16[4,3,64,512]{3,2,1,0:T(8,128)(2,1)S(1)} %get-tuple-element.24), channel_id=1, source_target_pairs={{0,16},{16,0},{1,17},{17,1},{2,18},{18,2},{3,19},{19,3},{4,20},{20... | collective-permute-start | bytes 2359304 | tf_op jit(solution)/shard_map/ppermute | solution.py:204
  94.7 10.4 %collective-permute-done.1.blocks.far = bf16[512,512]{1,0:T(8,128)(2,1)S(1)} collective-permute-done((bf16[512,512]{1,0:T(8,128)(2,1)S(1)}, bf16[512,512]{1,0:T(8,128)(2,1)S(1)}, u32[]{:S(2)}, u32[]{:S(2)}) %collective-permute-start.1) | collective-permute-done | bytes 524320 | tf_op jit(solution)/shard_map/ppermute | solution.py:200
  105.1 1.0 shard_map.69
  106.1 1.9 %collective-permute-start.2 = (bf16[4,64,512]{2,1,0:T(8,128)(2,1)S(1)}, bf16[4,64,512]{2,1,0:T(8,128)(2,1)S(1)}, u32[]{:S(2)}, u32[]{:S(2)}) collective-permute-start(bf16[4,64,512]{2,1,0:T(8,128)(2,1)S(1)} %get-tuple-element.22), channel_id=1, source_target_pairs={{0,16},{16,0},{1,17},{17,1},{2,18},{18,2},{3,19},{19,3},{4,20},{20... | collective-permute-start | bytes 786440 | tf_op jit(solution)/shard_map/ppermute | solution.py:204
  108.0 0.0 collective-permute-done.4.taken
  108.0 1.5 %shard_map.71.placed = bf16[4,4,64,512]{3,2,1,0:T(8,128)(2,1)} custom-call(s32[2]{0:T(128)S(1)} %pad_add_fusion.where, f32[4,3,64,512]{3,2,1,0:T(8,128)S(1)} %get-tuple-element.23.keep, bf16[4,3,64,512]{3,2,1,0:T(8,128)(2,1)S(1)} %collective-permute-done.4.taken), custom_call_target="tpu_custom_call" | custom-call | flops 786432 | bytes 3145728 | tf_op jit(solution)/shard_map/pallas_call | solution.py:158
  109.6 0.0 copy-done.1
  109.6 0.0 collective-permute-done.2.taken
  109.6 1.3 shard_map.72
  110.9 5.8 %all-to-all-start.2 = ((bf16[32,32,512]{2,1,0:T(8,128)(2,1)}), bf16[32,32,512]{2,1,0:T(8,128)(2,1)}, u32[]{:S(2)}, u32[]{:S(2)}) async-start(bf16[32,32,512]{2,1,0:T(8,128)(2,1)} %bitcast.5), calls=%async_computation.2 | async-start | bytes 2097152 | tf_op jit(solution)/shard_map/all_to_all | solution.py:244
  116.7 0.0 copy-start.2
  116.8 1.0 copy-done.2
  117.8 3.0 %shard_map.73.before = f32[512,512]{1,0:T(8,128)S(1)} custom-call(s32[2]{0:T(128)S(1)} %pad_add_fusion.where, bf16[512,512]{1,0:T(8,128)(2,1)S(1)} %all_gather.6.own, bf16[512,512]{1,0:T(8,128)(2,1)S(1)} %collective-permute-done.behind, bf16[512,512]{1,0:T(8,128)(2,1)S(1)} %copy-done.2, bf16[2048,512]{1,0:T(8,128)(2,1)} %w.3), custom_call_target="tpu_custom_call" | custom-call | flops 805306368 | bytes 3670016 | tf_op jit(solution)/shard_map/pallas_call | solution.py:79
  120.8 2.2 %shard_map.74 = (f32[512,512]{1,0:T(8,128)S(1)}, f32[1,512]{1,0:T(1,128)S(1)}) custom-call(s32[2]{0:T(128)S(1)} %pad_add_fusion.where, bf16[512,512]{1,0:T(8,128)(2,1)S(1)} %collective-permute-done.1.blocks.far, bf16[2048,512]{1,0:T(8,128)(2,1)} %w.3, f32[512,512]{1,0:T(8,128)S(1)} %shard_map.73.before, ...), custom_call_target="tpu_custom_call", output_to_operand_aliasing={{0}: (3, {})} | custom-call | flops 268435456 | bytes 3670016 | tf_op jit(solution)/shard_map/pallas_call | solution.py:98
  123.1 27.0 %all-gather = f32[16,1,512]{2,1,0:T(1,128)S(1)} all-gather(f32[1,1,512]{2,1,0:T(1,128)S(1)} %bitcast.7), channel_id=1, replica_groups=mesh['chip'=32,'core'=2,'zh'=4,'zl'=4] {'zh','zl'}, dimensions={0}, use_global_device_ids=true | all-gather | bytes 34816 | tf_op jit(solution)/shard_map/all_gather | solution.py:208
  150.1 1.1 subtract_convert_fusion
  151.2 0.0 all-to-all-done.2
  151.2 2.0 %convert_reduce_fusion = f32[32,512]{1,0:T(8,128)} fusion(bf16[32,32,512]{2,1,0:T(8,128)(2,1)} %all-to-all-done.2), kind=kLoop, calls=%fused_computation | loop fusion | flops 1032192 | bytes 1114112 | tf_op jit(solution)/shard_map/reduce_sum | solution.py:245
  (6 shorter events, 0.1 us)
Async XLA Ops:
  0.6 83.5 %copy-start = (bf16[512,512]{1,0:T(8,128)(2,1)S(1)}, bf16[512,512]{1,0:T(8,128)(2,1)}, u32[]{:S(2)}) copy-start(bf16[512,512]{1,0:T(8,128)(2,1)} %x) | copy-start | bytes 1572868
  0.6 77.7 %copy-start.3 = (bf16[512]{0:T(512)(128)(2,1)S(1)}, bf16[512]{0:T(512)(128)(2,1)}, u32[]{:S(2)}) copy-start(bf16[512]{0:T(512)(128)(2,1)} %param.6) | copy-start | bytes 3076
  0.7 27.3 %all-to-all-start = ((bf16[64,8,128]{2,1,0:T(8,128)(2,1)}), bf16[64,8,128]{2,1,0:T(8,128)(2,1)S(1)}, u32[]{:S(2)}, u32[]{:S(2)}) async-start(bf16[64,8,128]{2,1,0:T(8,128)(2,1)} %bitcast.8), calls=%async_computation | async-start | bytes 262144 | tf_op jit(solution)/shard_map/all_to_all | solution.py:214
  59.4 24.7 %all-to-all-start.1 = ((f32[16,1,512]{2,1,0:T(1,128)}), f32[16,1,512]{2,1,0:T(1,128)S(1)}, u32[]{:S(2)}, u32[]{:S(2)}) async-start(f32[16,1,512]{2,1,0:T(1,128)} %broadcast_in_dim.9), calls=%async_computation.1 | async-start | bytes 65536 | tf_op jit(solution)/shard_map/all_to_all | solution.py:196
  71.2 17.7 %collective-permute-start = (bf16[512,512]{1,0:T(8,128)(2,1)S(1)}, bf16[512,512]{1,0:T(8,128)(2,1)S(1)}, u32[]{:S(2)}, u32[]{:S(2)}) collective-permute-start(bf16[512,512]{1,0:T(8,128)(2,1)S(1)} %all_gather.6.own), channel_id=1, source_target_pairs={{0,1},{1,2},{2,3},{3,4},{4,5},{5,6},{6,7},{7,8},{8,9},{9,10},{10,1... | collective-permute-start | bytes 1572872 | tf_op jit(solution)/shard_map/ppermute | solution.py:200
  75.1 16.1 %collective-permute-start.3 = (bf16[512,512]{1,0:T(8,128)(2,1)S(1)}, bf16[512,512]{1,0:T(8,128)(2,1)S(1)}, u32[]{:S(2)}, u32[]{:S(2)}) collective-permute-start(bf16[512,512]{1,0:T(8,128)(2,1)S(1)} %all_gather.6.own), channel_id=1, source_target_pairs={{0,15},{1,0},{2,1},{3,2},{4,3},{5,4},{6,5},{7,6},{8,7},{9,8},{10,9... | collective-permute-start | bytes 1572872 | tf_op jit(solution)/shard_map/ppermute | solution.py:200
  88.9 16.2 %collective-permute-start.1 = (bf16[512,512]{1,0:T(8,128)(2,1)S(1)}, bf16[512,512]{1,0:T(8,128)(2,1)S(1)}, u32[]{:S(2)}, u32[]{:S(2)}) collective-permute-start(bf16[512,512]{1,0:T(8,128)(2,1)S(1)} %collective-permute-done.behind), channel_id=1, source_target_pairs={{0,1},{1,2},{2,3},{3,4},{4,5},{5,6},{6,7},{7,8},{8,9},{9,10},{10,1... | collective-permute-start | bytes 1572872 | tf_op jit(solution)/shard_map/ppermute | solution.py:200
  91.2 18.4 %copy-start.1 = (bf16[512,512]{1,0:T(8,128)(2,1)}, bf16[512,512]{1,0:T(8,128)(2,1)S(1)}, u32[]{:S(2)}) copy-start(bf16[512,512]{1,0:T(8,128)(2,1)S(1)} %collective-permute-done.3.ahead) | copy-start | bytes 1572868
  92.8 15.3 %collective-permute-start.4 = (bf16[4,3,64,512]{3,2,1,0:T(8,128)(2,1)S(1)}, bf16[4,3,64,512]{3,2,1,0:T(8,128)(2,1)S(1)}, u32[]{:S(2)}, u32[]{:S(2)}) collective-permute-start(bf16[4,3,64,512]{3,2,1,0:T(8,128)(2,1)S(1)} %get-tuple-element.24), channel_id=1, source_target_pairs={{0,16},{16,0},{1,17},{17,1},{2,18},{18,2},{3,19},{19,3},{4,20},{20... | collective-permute-start | bytes 2359304 | tf_op jit(solution)/shard_map/ppermute | solution.py:204
  106.1 3.5 %collective-permute-start.2 = (bf16[4,64,512]{2,1,0:T(8,128)(2,1)S(1)}, bf16[4,64,512]{2,1,0:T(8,128)(2,1)S(1)}, u32[]{:S(2)}, u32[]{:S(2)}) collective-permute-start(bf16[4,64,512]{2,1,0:T(8,128)(2,1)S(1)} %get-tuple-element.22), channel_id=1, source_target_pairs={{0,16},{16,0},{1,17},{17,1},{2,18},{18,2},{3,19},{19,3},{4,20},{20... | collective-permute-start | bytes 786440 | tf_op jit(solution)/shard_map/ppermute | solution.py:204
  110.9 40.3 %all-to-all-start.2 = ((bf16[32,32,512]{2,1,0:T(8,128)(2,1)}), bf16[32,32,512]{2,1,0:T(8,128)(2,1)}, u32[]{:S(2)}, u32[]{:S(2)}) async-start(bf16[32,32,512]{2,1,0:T(8,128)(2,1)} %bitcast.5), calls=%async_computation.2 | async-start | bytes 2097152 | tf_op jit(solution)/shard_map/all_to_all | solution.py:244
  116.7 1.0 copy-start.2

commit v9 on v8

--- a/solution.py
+++ b/solution.py
@@ -191,6 +191,32 @@
     )(where, keep, taken, placed)
 
 
+def total_kernel(where, parts, out, buffer, sems):
+    step = CHIPS // 4
+    copies = []
+    for i in range(4):
+        piece = slice(step * i, step * (i + 1))
+        copies.append(pltpu.make_async_copy(parts.at[piece], buffer.at[piece], sems.at[i]))
+        copies[-1].start()
+    total = jnp.zeros(out.shape, jnp.float32)
+    for i in range(4):
+        copies[i].wait()
+        for j in range(step * i, step * (i + 1)):
+            total = total + buffer[j].astype(jnp.float32)
+    out[...] = total
+
+
+def total(where, parts):
+    return call(
+        total_kernel,
+        [pl.BlockSpec(memory_space=pltpu.HBM)],
+        jax.ShapeDtypeStruct(parts.shape[1:], jnp.float32),
+        parts.size,
+        2 * parts.size,
+        scratch=[pltpu.VMEM(parts.shape, parts.dtype), pltpu.SemaphoreType.DMA((4,))],
+    )(where, parts)
+
+
 def tensor_sum(vector):
     spread = jnp.broadcast_to(vector.reshape(1, ROWS), (TP, ROWS))
     return jnp.sum(lax.all_to_all(spread, Z, split_axis=0, concat_axis=0, tiled=True), axis=0)
@@ -242,7 +268,7 @@
     pair = combine_far(where, keep_far, taken_far, placed)
     pair, x, inverse = lax.optimization_barrier((pair, layer_input, inverse))
     parts = lax.all_to_all(pair.reshape(CHIPS, 32, FEAT), "chip", split_axis=0, concat_axis=0, tiled=True)
-    grad_weight = jnp.sum(parts.astype(jnp.float32), axis=0)
+    grad_weight = total(where, parts)
 
     dnormed, products = grad_far(where, far, w_kv, grad, x, gain[None, :])
     mean_dot = gather_sum(products) / D

time: 154 us -> 154 us (level)
  other arithmetic: 6.41 us -> 4.4 us
    reduce_sum x1 -> x0, other arithmetic: 2.01 us -> none  [step(): grad_weight = jnp.sum(parts.astype(jnp.float32), axis=0)]
where the time goes in v9:
time: 154 us; the launch traced here: 153 us
  blocking collectives  57 us (37%)
  starting transfers between devices  47.5 us (31%)
  waiting for transfers between devices  27.6 us (18%)
  Pallas kernels  12.9 us (8%)
  other arithmetic  4.4 us (3%)
  local copies, waits for them, and re-layouts  2.74 us (2%)
    all_gather x1, blocking collectives, step(): own = lax.all_gather(block, 'zh', axis=0, tiled=True)  30 us
    all_gather x1, blocking collectives, gather_sum(): return jnp.sum(lax.all_gather(vector, Z, axis=0, tiled=True), axis=0)  26.9 us
    all_to_all x1, starting transfers between devices, step(): lax.all_to_all(d_kv, ('chip', 'core'), split_axis=0, concat_axis=0, tiled...  17.4 us
    ppermute x3, waiting for transfers between devices, hop(): return lax.ppermute(array, Z, [(i, (i + step) % TP) for i in range(TP)])  14.9 us
    all_to_all x1, starting transfers between devices, tensor_sum(): lax.all_to_all(spread, Z, split_axis=0, concat_axis=0, tiled=True)  11.8 us
    ppermute x3, starting transfers between devices, hop(): return lax.ppermute(array, Z, [(i, (i + step) % TP) for i in range(TP)])  9.35 us
    all_to_all x1, waiting for transfers between devices, step(): lax.all_to_all(d_kv, ('chip', 'core'), split_axis=0, concat_axis=0, tiled...  6.9 us
    all_to_all x1, waiting for transfers between devices, tensor_sum(): lax.all_to_all(spread, Z, split_axis=0, concat_axis=0, tiled=True)  5.78 us
  transfers between devices with their start and end apart: 8, of which 4 were waited for; matrix products, arithmetic and copies ran while one was open for 3% of the time, Pallas kernels for 6%

profile of v9, /device:TPU:2, one launch (start us, length us, event | category | flops | bytes accessed | tf_op | source)
XLA Modules:
  0.0 153.0 jit_solution(1747958686880933237)
XLA Ops:
  0.6 0.0 copy-start
  0.6 0.0 copy-start.7
  0.7 17.4 %all-to-all-start = ((bf16[64,8,128]{2,1,0:T(8,128)(2,1)}), bf16[64,8,128]{2,1,0:T(8,128)(2,1)S(1)}, u32[]{:S(2)}, u32[]{:S(2)}) async-start(bf16[64,8,128]{2,1,0:T(8,128)(2,1)} %bitcast.8), calls=%async_computation | async-start | bytes 262144 | tf_op jit(solution)/shard_map/all_to_all | solution.py:240
  18.0 0.9 convert_reduce_fusion
  18.9 0.7 add_select_fusion
  19.6 1.2 fusion
  20.9 0.1 pad_add_fusion.where
  20.9 0.1 fusion.3.onehot
  21.1 6.9 %all-to-all-done = bf16[64,8,128]{2,1,0:T(8,128)(2,1)S(1)} async-done(((bf16[64,8,128]{2,1,0:T(8,128)(2,1)}), bf16[64,8,128]{2,1,0:T(8,128)(2,1)S(1)}, u32[]{:S(2)}, u32[]{:S(2)}) %all-to-all-start) | async-done | bytes 131104 | tf_op jit(solution)/shard_map/all_to_all | solution.py:240
  28.0 0.8 shard_map.68
  28.8 30.0 %all_gather.6.own = bf16[512,512]{1,0:T(8,128)(2,1)S(1)} all-gather(bf16[128,512]{1,0:T(8,128)(2,1)S(1)} %shard_map.68), channel_id=1, replica_groups=mesh['chip'=32,'core'=2,'zh'=4,'zl'=4] {'zh'}, dimensions={0}, use_global_device_ids=true | all-gather | bytes 655360 | tf_op jit(solution)/shard_map/all_gather | solution.py:254
  58.8 0.6 broadcast_in_dim.9
  59.4 11.8 %all-to-all-start.1 = ((f32[16,1,512]{2,1,0:T(1,128)}), f32[16,1,512]{2,1,0:T(1,128)S(1)}, u32[]{:S(2)}, u32[]{:S(2)}) async-start(f32[16,1,512]{2,1,0:T(1,128)} %broadcast_in_dim.9), calls=%async_computation.1 | async-start | bytes 65536 | tf_op jit(solution)/shard_map/all_to_all | solution.py:222
  71.2 3.8 %collective-permute-start = (bf16[512,512]{1,0:T(8,128)(2,1)S(1)}, bf16[512,512]{1,0:T(8,128)(2,1)S(1)}, u32[]{:S(2)}, u32[]{:S(2)}) collective-permute-start(bf16[512,512]{1,0:T(8,128)(2,1)S(1)} %all_gather.6.own), channel_id=1, source_target_pairs={{0,1},{1,2},{2,3},{3,4},{4,5},{5,6},{6,7},{7,8},{8,9},{9,10},{10,1... | collective-permute-start | bytes 1572872 | tf_op jit(solution)/shard_map/ppermute | solution.py:226
  75.1 3.2 %collective-permute-start.3 = (bf16[512,512]{1,0:T(8,128)(2,1)S(1)}, bf16[512,512]{1,0:T(8,128)(2,1)S(1)}, u32[]{:S(2)}, u32[]{:S(2)}) collective-permute-start(bf16[512,512]{1,0:T(8,128)(2,1)S(1)} %all_gather.6.own), channel_id=1, source_target_pairs={{0,15},{1,0},{2,1},{3,2},{4,3},{5,4},{6,5},{7,6},{8,7},{9,8},{10,9... | collective-permute-start | bytes 1572872 | tf_op jit(solution)/shard_map/ppermute | solution.py:226
  78.3 0.0 copy-done.7
  78.3 5.8 %all-to-all-done.1 = f32[16,1,512]{2,1,0:T(1,128)S(1)} async-done(((f32[16,1,512]{2,1,0:T(1,128)}), f32[16,1,512]{2,1,0:T(1,128)S(1)}, u32[]{:S(2)}, u32[]{:S(2)}) %all-to-all-start.1) | async-done | bytes 32800 | tf_op jit(solution)/shard_map/all_to_all | solution.py:222
  84.2 0.0 copy-done
  84.2 0.2 fusion.2.normed
  84.4 4.5 %collective-permute-done.behind = bf16[512,512]{1,0:T(8,128)(2,1)S(1)} collective-permute-done((bf16[512,512]{1,0:T(8,128)(2,1)S(1)}, bf16[512,512]{1,0:T(8,128)(2,1)S(1)}, u32[]{:S(2)}, u32[]{:S(2)}) %collective-permute-start) | collective-permute-done | bytes 524320 | tf_op jit(solution)/shard_map/ppermute | solution.py:226
  88.9 0.0 copy-start.3
  88.9 2.3 %collective-permute-start.1 = (bf16[512,512]{1,0:T(8,128)(2,1)S(1)}, bf16[512,512]{1,0:T(8,128)(2,1)S(1)}, u32[]{:S(2)}, u32[]{:S(2)}) collective-permute-start(bf16[512,512]{1,0:T(8,128)(2,1)S(1)} %collective-permute-done.behind), channel_id=1, source_target_pairs={{0,1},{1,2},{2,3},{3,4},{4,5},{5,6},{6,7},{7,8},{8,9},{9,10},{10,1... | collective-permute-start | bytes 1572872 | tf_op jit(solution)/shard_map/ppermute | solution.py:226
  91.2 0.0 collective-permute-done.3.ahead
  91.2 0.0 copy-start.5
  91.2 1.5 %shard_map.70 = (f32[4,3,64,512]{3,2,1,0:T(8,128)S(1)}, bf16[4,3,64,512]{3,2,1,0:T(8,128)(2,1)S(1)}) custom-call(s32[2]{0:T(128)S(1)} %pad_add_fusion.where, bf16[512,512]{1,0:T(8,128)(2,1)S(1)} %all_gather.6.own, bf16[512,512]{1,0:T(8,128)(2,1)S(1)} %collective-permute-done.behind, bf16[512,512]{1,0:T(8,128)(2,1)S(1)} %collective-permute-done.3.ahead, ...), custom_call_target="tpu_custom_call" | custom-call | flops 805306368 | bytes 4718592 | tf_op jit(solution)/shard_map/pallas_call | solution.py:128
  92.8 1.9 %collective-permute-start.4 = (bf16[4,3,64,512]{3,2,1,0:T(8,128)(2,1)S(1)}, bf16[4,3,64,512]{3,2,1,0:T(8,128)(2,1)S(1)}, u32[]{:S(2)}, u32[]{:S(2)}) collective-permute-start(bf16[4,3,64,512]{3,2,1,0:T(8,128)(2,1)S(1)} %get-tuple-element.24), channel_id=1, source_target_pairs={{0,16},{16,0},{1,17},{17,1},{2,18},{18,2},{3,19},{19,3},{4,20},{20... | collective-permute-start | bytes 2359304 | tf_op jit(solution)/shard_map/ppermute | solution.py:230
  94.7 10.4 %collective-permute-done.1.blocks.far = bf16[512,512]{1,0:T(8,128)(2,1)S(1)} collective-permute-done((bf16[512,512]{1,0:T(8,128)(2,1)S(1)}, bf16[512,512]{1,0:T(8,128)(2,1)S(1)}, u32[]{:S(2)}, u32[]{:S(2)}) %collective-permute-start.1) | collective-permute-done | bytes 524320 | tf_op jit(solution)/shard_map/ppermute | solution.py:226
  105.1 0.0 copy-start.1
  105.1 1.0 shard_map.69
  106.1 1.9 %collective-permute-start.2 = (bf16[4,64,512]{2,1,0:T(8,128)(2,1)S(1)}, bf16[4,64,512]{2,1,0:T(8,128)(2,1)S(1)}, u32[]{:S(2)}, u32[]{:S(2)}) collective-permute-start(bf16[4,64,512]{2,1,0:T(8,128)(2,1)S(1)} %get-tuple-element.22), channel_id=1, source_target_pairs={{0,16},{16,0},{1,17},{17,1},{2,18},{18,2},{3,19},{19,3},{4,20},{20... | collective-permute-start | bytes 786440 | tf_op jit(solution)/shard_map/ppermute | solution.py:230
  108.0 0.0 collective-permute-done.4.taken
  108.0 1.6 %shard_map.71.placed = bf16[4,4,64,512]{3,2,1,0:T(8,128)(2,1)} custom-call(s32[2]{0:T(128)S(1)} %pad_add_fusion.where, f32[4,3,64,512]{3,2,1,0:T(8,128)S(1)} %get-tuple-element.23.keep, bf16[4,3,64,512]{3,2,1,0:T(8,128)(2,1)S(1)} %collective-permute-done.4.taken), custom_call_target="tpu_custom_call" | custom-call | flops 786432 | bytes 3145728 | tf_op jit(solution)/shard_map/pallas_call | solution.py:158
  109.6 0.0 copy-done.3
  109.6 0.0 copy-done.5
  109.6 0.0 copy-done.1
  109.6 0.0 collective-permute-done.2.taken
  109.6 1.3 shard_map.72
  111.0 5.2 %all-to-all-start.2 = ((bf16[32,32,512]{2,1,0:T(8,128)(2,1)}), bf16[32,32,512]{2,1,0:T(8,128)(2,1)S(1)}, u32[]{:S(2)}, u32[]{:S(2)}) async-start(bf16[32,32,512]{2,1,0:T(8,128)(2,1)} %bitcast.5), calls=%async_computation.2 | async-start | bytes 2097152 | tf_op jit(solution)/shard_map/all_to_all | solution.py:270
  116.1 0.0 copy-start.4
  116.2 1.0 copy-done.4
  117.2 0.0 copy-start.6
  117.2 1.0 copy-done.6
  118.2 0.0 copy-start.2
  118.2 3.0 %shard_map.73.before = f32[512,512]{1,0:T(8,128)S(1)} custom-call(s32[2]{0:T(128)S(1)} %pad_add_fusion.where, bf16[512,512]{1,0:T(8,128)(2,1)S(1)} %all_gather.6.own, bf16[512,512]{1,0:T(8,128)(2,1)S(1)} %copy-done.4, bf16[512,512]{1,0:T(8,128)(2,1)S(1)} %copy-done.6, bf16[2048,512]{1,0:T(8,128)(2,1)} %w.3), custom_call_target="tpu_custom_call" | custom-call | flops 805306368 | bytes 3670016 | tf_op jit(solution)/shard_map/pallas_call | solution.py:79
  121.3 0.0 copy-done.2
  121.3 2.2 %shard_map.74 = (f32[512,512]{1,0:T(8,128)S(1)}, f32[1,512]{1,0:T(1,128)S(1)}) custom-call(s32[2]{0:T(128)S(1)} %pad_add_fusion.where, bf16[512,512]{1,0:T(8,128)(2,1)S(1)} %copy-done.2, bf16[2048,512]{1,0:T(8,128)(2,1)} %w.3, f32[512,512]{1,0:T(8,128)S(1)} %shard_map.73.before, bf16[512,512]{1,0:T(8,128)(2,1)S(1)} %copy-done, ...), custom_call_target="tpu_custom_call", output_to_operand_aliasing={{0}: (3, {})} | custom-call | flops 268435456 | bytes 3670016 | tf_op jit(solution)/shard_map/pallas_call | solution.py:98
  123.5 26.9 %all-gather = f32[16,1,512]{2,1,0:T(1,128)S(1)} all-gather(f32[1,1,512]{2,1,0:T(1,128)S(1)} %bitcast.7), channel_id=1, replica_groups=mesh['chip'=32,'core'=2,'zh'=4,'zl'=4] {'zh','zl'}, dimensions={0}, use_global_device_ids=true | all-gather | bytes 34816 | tf_op jit(solution)/shard_map/all_gather | solution.py:234
  150.5 1.1 subtract_convert_fusion
  151.6 0.0 all-to-all-done.2.parts
  151.6 1.4 shard_map.75
  (6 shorter events, 0.1 us)
Async XLA Ops:
  0.6 83.5 %copy-start = (bf16[512,512]{1,0:T(8,128)(2,1)S(1)}, bf16[512,512]{1,0:T(8,128)(2,1)}, u32[]{:S(2)}) copy-start(bf16[512,512]{1,0:T(8,128)(2,1)} %x) | copy-start | bytes 1572868
  0.6 77.7 %copy-start.7 = (bf16[512]{0:T(512)(128)(2,1)S(1)}, bf16[512]{0:T(512)(128)(2,1)}, u32[]{:S(2)}) copy-start(bf16[512]{0:T(512)(128)(2,1)} %param.6) | copy-start | bytes 3076
  0.7 27.3 %all-to-all-start = ((bf16[64,8,128]{2,1,0:T(8,128)(2,1)}), bf16[64,8,128]{2,1,0:T(8,128)(2,1)S(1)}, u32[]{:S(2)}, u32[]{:S(2)}) async-start(bf16[64,8,128]{2,1,0:T(8,128)(2,1)} %bitcast.8), calls=%async_computation | async-start | bytes 262144 | tf_op jit(solution)/shard_map/all_to_all | solution.py:240
  59.4 24.7 %all-to-all-start.1 = ((f32[16,1,512]{2,1,0:T(1,128)}), f32[16,1,512]{2,1,0:T(1,128)S(1)}, u32[]{:S(2)}, u32[]{:S(2)}) async-start(f32[16,1,512]{2,1,0:T(1,128)} %broadcast_in_dim.9), calls=%async_computation.1 | async-start | bytes 65536 | tf_op jit(solution)/shard_map/all_to_all | solution.py:222
  71.2 17.7 %collective-permute-start = (bf16[512,512]{1,0:T(8,128)(2,1)S(1)}, bf16[512,512]{1,0:T(8,128)(2,1)S(1)}, u32[]{:S(2)}, u32[]{:S(2)}) collective-permute-start(bf16[512,512]{1,0:T(8,128)(2,1)S(1)} %all_gather.6.own), channel_id=1, source_target_pairs={{0,1},{1,2},{2,3},{3,4},{4,5},{5,6},{6,7},{7,8},{8,9},{9,10},{10,1... | collective-permute-start | bytes 1572872 | tf_op jit(solution)/shard_map/ppermute | solution.py:226
  75.1 16.1 %collective-permute-start.3 = (bf16[512,512]{1,0:T(8,128)(2,1)S(1)}, bf16[512,512]{1,0:T(8,128)(2,1)S(1)}, u32[]{:S(2)}, u32[]{:S(2)}) collective-permute-start(bf16[512,512]{1,0:T(8,128)(2,1)S(1)} %all_gather.6.own), channel_id=1, source_target_pairs={{0,15},{1,0},{2,1},{3,2},{4,3},{5,4},{6,5},{7,6},{8,7},{9,8},{10,9... | collective-permute-start | bytes 1572872 | tf_op jit(solution)/shard_map/ppermute | solution.py:226
  88.9 20.7 %copy-start.3 = (bf16[512,512]{1,0:T(8,128)(2,1)}, bf16[512,512]{1,0:T(8,128)(2,1)S(1)}, u32[]{:S(2)}) copy-start(bf16[512,512]{1,0:T(8,128)(2,1)S(1)} %collective-permute-done.behind) | copy-start | bytes 1572868
  88.9 16.2 %collective-permute-start.1 = (bf16[512,512]{1,0:T(8,128)(2,1)S(1)}, bf16[512,512]{1,0:T(8,128)(2,1)S(1)}, u32[]{:S(2)}, u32[]{:S(2)}) collective-permute-start(bf16[512,512]{1,0:T(8,128)(2,1)S(1)} %collective-permute-done.behind), channel_id=1, source_target_pairs={{0,1},{1,2},{2,3},{3,4},{4,5},{5,6},{6,7},{7,8},{8,9},{9,10},{10,1... | collective-permute-start | bytes 1572872 | tf_op jit(solution)/shard_map/ppermute | solution.py:226
  91.2 18.4 %copy-start.5 = (bf16[512,512]{1,0:T(8,128)(2,1)}, bf16[512,512]{1,0:T(8,128)(2,1)S(1)}, u32[]{:S(2)}) copy-start(bf16[512,512]{1,0:T(8,128)(2,1)S(1)} %collective-permute-done.3.ahead) | copy-start | bytes 1572868
  92.8 15.3 %collective-permute-start.4 = (bf16[4,3,64,512]{3,2,1,0:T(8,128)(2,1)S(1)}, bf16[4,3,64,512]{3,2,1,0:T(8,128)(2,1)S(1)}, u32[]{:S(2)}, u32[]{:S(2)}) collective-permute-start(bf16[4,3,64,512]{3,2,1,0:T(8,128)(2,1)S(1)} %get-tuple-element.24), channel_id=1, source_target_pairs={{0,16},{16,0},{1,17},{17,1},{2,18},{18,2},{3,19},{19,3},{4,20},{20... | collective-permute-start | bytes 2359304 | tf_op jit(solution)/shard_map/ppermute | solution.py:230
  105.1 4.5 %copy-start.1 = (bf16[512,512]{1,0:T(8,128)(2,1)}, bf16[512,512]{1,0:T(8,128)(2,1)S(1)}, u32[]{:S(2)}) copy-start(bf16[512,512]{1,0:T(8,128)(2,1)S(1)} %collective-permute-done.1.blocks.far) | copy-start | bytes 1572868
  106.1 3.5 %collective-permute-start.2 = (bf16[4,64,512]{2,1,0:T(8,128)(2,1)S(1)}, bf16[4,64,512]{2,1,0:T(8,128)(2,1)S(1)}, u32[]{:S(2)}, u32[]{:S(2)}) collective-permute-start(bf16[4,64,512]{2,1,0:T(8,128)(2,1)S(1)} %get-tuple-element.22), channel_id=1, source_target_pairs={{0,16},{16,0},{1,17},{17,1},{2,18},{18,2},{3,19},{19,3},{4,20},{20... | collective-permute-start | bytes 786440 | tf_op jit(solution)/shard_map/ppermute | solution.py:230
  111.0 40.6 %all-to-all-start.2 = ((bf16[32,32,512]{2,1,0:T(8,128)(2,1)}), bf16[32,32,512]{2,1,0:T(8,128)(2,1)S(1)}, u32[]{:S(2)}, u32[]{:S(2)}) async-start(bf16[32,32,512]{2,1,0:T(8,128)(2,1)} %bitcast.5), calls=%async_computation.2 | async-start | bytes 2097152 | tf_op jit(solution)/shard_map/all_to_all | solution.py:270
  116.1 1.0 copy-start.4
  117.2 1.0 copy-start.6
  118.2 3.0 %copy-start.2 = (bf16[512,512]{1,0:T(8,128)(2,1)S(1)}, bf16[512,512]{1,0:T(8,128)(2,1)}, u32[]{:S(2)}) copy-start(bf16[512,512]{1,0:T(8,128)(2,1)} %copy-done.1) | copy-start | bytes 1572868
